TPU v7x, 128 devices: a whole 4x4x4 slice. The times are simulated.
128 devices in a mesh: row: 32 (over z, y, core), col: 4 (over x).
Axes of the slice: x: 4, y: 4, z: 4, core: 2. Of those that a mesh axis runs over, the one named last changes fastest.
Arguments:
- matrix: float32 [24576, 16384], P('row', 'col'), may hold values from -6 to 6
Outputs:
- updated: float32 [24576, 16384], P('row', 'col')
All inputs are finite; a program needn't handle non-finite values.
Results may differ from a plain program's by a relative error of at most 0.0003.
Values sent between devices are 32-bit elements; how exact they have to be, the bound alone decides.
No kernel may reach another device: no remote copies, remote signals or barrier semaphores. Data moves between devices by JAX's collectives and lax.ppermute only.
A program may use at most 128 MiB of HBM per device.

v0:
```python
import jax
import jax.numpy as jnp
from jax import lax
from jax.sharding import PartitionSpec as P

PANEL = 128


def broadcast(x, axis, root):
    mine = lax.axis_index(axis) == root
    return lax.psum(jnp.where(mine, x, jnp.zeros_like(x)), axis)


def column_steps(working):
    count = working.shape[0]
    current = working
    for column in range(count - 1):
        pivot_value = current[column, column]
        multiplier = current[column + 1 :, column] / pivot_value
        trailing_block = (
            current[column + 1 :, column + 1 :]
            - multiplier[:, None] * current[column, column + 1 :][None, :]
        )
        current = current.at[column + 1 :, column + 1 :].set(trailing_block)
        current = current.at[column + 1 :, column].set(multiplier)
    lower_unit = jnp.tril(current, -1) + jnp.eye(count, dtype=current.dtype)
    upper_tri = jnp.triu(current)
    return (lower_unit, upper_tri)


def eliminate(working):
    count = working.shape[0]
    if count <= 8:
        return column_steps(working)
    half = count // 2
    lower_top, upper_top = eliminate(working[:half, :half])
    upper_right = jax.scipy.linalg.solve_triangular(
        lower_top, working[:half, half:], lower=True, unit_diagonal=True
    )
    lower_left = jax.scipy.linalg.solve_triangular(
        upper_top.T, working[half:, :half].T, lower=True
    ).T
    schur = working[half:, half:] - jnp.dot(
        lower_left, upper_right, precision=lax.Precision.HIGHEST
    )
    lower_bottom, upper_bottom = eliminate(schur)
    rest = count - half
    zeros_right = jnp.zeros((half, rest), dtype=working.dtype)
    zeros_left = jnp.zeros((rest, half), dtype=working.dtype)
    lower_unit = jnp.concatenate(
        [
            jnp.concatenate([lower_top, zeros_right], axis=1),
            jnp.concatenate([lower_left, lower_bottom], axis=1),
        ],
        axis=0,
    )
    upper_tri = jnp.concatenate(
        [
            jnp.concatenate([upper_top, upper_right], axis=1),
            jnp.concatenate([zeros_left, upper_bottom], axis=1),
        ],
        axis=0,
    )
    return (lower_unit, upper_tri)


def combine_coefficients(lower_unit, upper_tri, projected):
    scaled = jnp.dot(upper_tri.T, projected, precision=lax.Precision.HIGHEST)
    return jax.scipy.linalg.solve_triangular(lower_unit, scaled, lower=True, unit_diagonal=True)


def on_device(matrix):
    high = lax.Precision.HIGHEST
    row_count = matrix.shape[0]
    column_block = broadcast(matrix[:, :PANEL], "col", 0)
    gram_part = jnp.dot(column_block.T, column_block, precision=high)
    gram_total = lax.psum(gram_part, "row")
    cholesky_low = jnp.linalg.cholesky(gram_total)
    basis_local = jax.scipy.linalg.solve_triangular(cholesky_low, column_block.T, lower=True)
    top_basis = broadcast(basis_local[:, :PANEL], "row", 0)
    lower_unit, upper_tri = eliminate(top_basis.T + jnp.eye(PANEL, dtype=jnp.float32))
    reflectors = jax.scipy.linalg.solve_triangular(upper_tri.T, basis_local, lower=True)
    global_rows = lax.axis_index("row") * row_count + jnp.arange(row_count)
    padded_lower = jnp.zeros_like(reflectors).at[:, :PANEL].set(lower_unit.T)
    reflectors = jnp.where(global_rows[None, :] < PANEL, padded_lower, reflectors)
    projected_part = jnp.dot(reflectors, matrix, precision=high)
    projected = lax.psum(projected_part, "row")
    coefficients = combine_coefficients(lower_unit, upper_tri, projected)
    return matrix - jnp.dot(reflectors.T, coefficients, precision=high)


def solution(mesh):
    in_specs = (P("row", "col"),)
    out_specs = P("row", "col")
    return jax.shard_map(
        on_device, mesh=mesh, in_specs=in_specs, out_specs=out_specs, check_vma=False
    )
```

profile of v0, /device:TPU:1, one launch (start us, length us, event | category | flops | bytes accessed | tf_op | source)
XLA Modules:
  0.0 833.7 jit_solution(9178054683234195617)
XLA Ops:
  6.5 1.8 slice_select_fusion
  8.4 44.5 %all-reduce.36.cloned.1.call-done = f32[768,128]{1,0:T(8,128)} async-done(((f32[768,128]{1,0:T(8,128)}), f32[768,128]{1,0:T(8,128)}) %all-reduce.36.cloned.1.call-update) | async-done | bytes 393232 | tf_op jit(solution)/shard_map/psum | solution.py:11
  52.9 2.5 fusion.190
  55.6 99.4 %all-reduce.38.cloned.1.call-done = f32[128,128]{0,1:T(8,128)} async-done(((f32[128,128]{0,1:T(8,128)}), f32[128,128]{0,1:T(8,128)}) %all-reduce.38.cloned.1.call-update) | async-done | bytes 65552 | tf_op jit(solution)/shard_map/psum | solution.py:77
  156.8 11.7 %cholesky.21 = f32[128,128]{1,0:T(8,128)S(1)} custom-call(f32[128,128]{1,0:T(8,128)S(1)} %fusion.22), custom_call_target="Cholesky" | custom-call | tf_op jit(solution)/shard_map/jit(cholesky)/cholesky | solution.py:78
  170.0 9.8 %custom-call.62 = f32[1,128,128]{1,2,0:T(8,128)S(1)} custom-call(f32[1,128,128]{2,1,0:T(8,128)S(1)} %fusion.2), custom_call_target="InvertDiagBlocksLowerTriangular" | custom-call | tf_op jit(solution)/shard_map/jit(_solve_triangular)/triangular_solve | solution.py:79
  179.8 1.5 fusion
  182.7 93.5 %all-reduce.40.cloned.1.call-done = f32[128,128]{0,1:T(8,128)} async-done(((f32[128,128]{0,1:T(8,128)}), f32[128,128]{0,1:T(8,128)}) %all-reduce.40.cloned.1.call-update) | async-done | bytes 65552 | tf_op jit(solution)/shard_map/psum | solution.py:11
  324.4 1.2 custom-call.65
  371.6 2.4 custom-call.70
  374.5 2.4 custom-call.69
  423.0 1.2 custom-call.74
  424.6 1.2 custom-call.73
  472.2 4.9 custom-call.36
  477.7 4.9 custom-call.37
  577.4 2.4 custom-call.84
  580.3 2.4 custom-call.83
  678.3 9.8 %custom-call.91 = f32[1,128,128]{1,2,0:T(8,128)S(1)} custom-call(f32[1,128,128]{2,1,0:T(8,128)S(1)} %fusion.20), custom_call_target="InvertDiagBlocksLowerTriangular" | custom-call | tf_op jit(solution)/shard_map/jit(_solve_triangular)/triangular_solve | solution.py:82
  689.8 10.8 %fusion.191 = f32[128,4096]{1,0:T(8,128)} fusion(f32[128,768]{0,1:T(8,128)S(1)} %convolution_select_fusion, f32[768,4096]{1,0:T(8,128)} %param.465), kind=kOutput, calls=%fused_computation.612 | convolution fusion | flops 4831838208 | bytes 15073280 | tf_op jit(solution)/shard_map/dot_general | solution.py:86
  701.0 9.8 %custom-call.38 = f32[1,128,128]{1,2,0:T(8,128)S(1)} custom-call(f32[1,128,128]{2,1,0:T(8,128)S(1)} %fusion.16), custom_call_target="InvertDiagBlocksLowerTriangular" | custom-call | tf_op jit(solution)/shard_map/jit(_solve_triangular)/triangular_solve | solution.py:69
  710.8 96.1 %all-reduce.42.cloned.1.call-done = f32[128,4096]{1,0:T(8,128)} async-done(((f32[128,4096]{1,0:T(8,128)}), f32[128,4096]{1,0:T(8,128)}) %all-reduce.42.cloned.1.call-update) | async-done | bytes 2097168 | tf_op jit(solution)/shard_map/psum | solution.py:87
  806.9 3.5 fusion.162
  810.5 1.9 fusion.17
  812.4 14.6 %convolution_subtract_fusion = f32[768,4096]{1,0:T(8,128)} fusion(f32[768,4096]{1,0:T(8,128)} %param.465, f32[128,768]{0,1:T(8,128)S(1)} %convolution_select_fusion, f32[128,4096]{1,0:T(8,128)S(1)} %fusion.17), kind=kOutput, calls=%fused_computation | convolution fusion | flops 4834983936 | bytes 27656192 | tf_op jit(solution)/shard_map/dot_general | solution.py:89
  (928 shorter events, 343.4 us)
Async XLA Ops:
  6.5 46.4 %all-reduce.36.cloned.1.call-start = ((), (), s32[]{:S(2)}) async-start(), calls=%async_computation | async-start | bytes 786432 | tf_op jit(solution)/shard_map/psum | solution.py:11
  8.3 146.6 %all-reduce.38.cloned.1.call-start = ((), (), s32[]{:S(2)}) async-start(), calls=%async_computation.1 | async-start | bytes 131072 | tf_op jit(solution)/shard_map/psum | solution.py:77
  55.5 220.8 %all-reduce.40.cloned.1.call-start = ((), (), s32[]{:S(2)}) async-start(), calls=%async_computation.2 | async-start | bytes 131072 | tf_op jit(solution)/shard_map/psum | solution.py:11
  182.0 624.9 %all-reduce.42.cloned.1.call-start = ((), (), s32[]{:S(2)}) async-start(), calls=%async_computation.3 | async-start | bytes 4194304 | tf_op jit(solution)/shard_map/psum | solution.py:87
Sparse Core Ops, SparseCore 0:
  9.7 43.1 all-reduce.35
  56.5 98.4 all-reduce.37
  182.1 94.0 all-reduce.39
  700.8 106.0 all-reduce.41
where the time goes:
time: 845 us; the launch traced here: 834 us
  waiting for transfers between devices  334 us (40%)
  other arithmetic  235 us (28%)
  local copies, waits for them, and re-layouts  164 us (19%)
  between operations  55.7 us (7%)
  matrix products  45.8 us (5%)
    psum x2, waiting for transfers between devices, broadcast(): return lax.psum(jnp.where(mine, x, jnp.zeros_like(x)), axis)  138 us
    psum x1, waiting for transfers between devices, on_device(): gram_total = lax.psum(gram_part, 'row')  99.4 us
    psum x1, waiting for transfers between devices, on_device(): projected = lax.psum(projected_part, 'row')  96.1 us
    div x96, other arithmetic, column_steps(): multiplier = current[column + 1:, column] / pivot_value  68.8 us
    mul x96, other arithmetic, column_steps(): multiplier[:, None] * current[column, column + 1:][None, :]  68.5 us
    slice x96, local copies, waits for them, and re-layouts, column_steps(): pivot_value = current[column, column]  55.4 us
    scatter x112, local copies, waits for them, and re-layouts, column_steps(): current = current.at[column + 1:, column + 1:].set(trailing_block)  45.8 us
    scatter x112, local copies, waits for them, and re-layouts, column_steps(): current = current.at[column + 1:, column].set(multiplier)  31.1 us
  transfers between devices with their start and end apart: 4, of which 4 were waited for; matrix products, arithmetic and copies ran while one was open for 1% of the time, Pallas kernels for 0%

commit v1 on v0

v1 whole, which is shorter than its diff:
```python
import functools

import jax
import jax.numpy as jnp
from jax import lax
from jax.experimental import pallas as pl
from jax.experimental.pallas import tpu as pltpu
from jax.sharding import PartitionSpec as P

PANEL = 128
HIGH = lax.Precision.HIGHEST
F32 = jnp.float32
BF16 = jnp.bfloat16
VMEM_BYTES = 48 << 20


def row_of(z, y, c):
    return (z * 4 + y) * 2 + c


def axis_pairs(which, step, keep=lambda z, y, c: True):
    pairs = []
    for z in range(4):
        for y in range(4):
            for c in range(2):
                if not keep(z, y, c):
                    continue
                if (c == 0) == (which == 0):
                    to = row_of(z, (y + step) % 4, c)
                else:
                    to = row_of((z + step) % 4, y, c)
                pairs.append((row_of(z, y, c), to))
    return pairs


CORE_PAIRS = [(r, r ^ 1) for r in range(32)]


def first(x, step):
    return lax.ppermute(x, "row", axis_pairs(0, step))


def second(x, step):
    return lax.ppermute(x, "row", axis_pairs(1, step))


def swap(x):
    return lax.ppermute(x, "row", CORE_PAIRS)


def dot3(x, y):
    return jnp.dot(x, y, preferred_element_type=F32)


def split(x):
    high = x.astype(BF16)
    return high, (x - high.astype(F32)).astype(BF16)


def params():
    return pltpu.CompilerParams(vmem_limit_bytes=VMEM_BYTES)


def coords(r, half):
    y, z = (r // 2) % 4, r // 8
    return jnp.where(half == 0, y, z), jnp.where(half == 0, z, y)


def panel_kernel(r_ref, a_ref, pa_ref, pb_ref, keep_ref, send_ref):
    r = r_ref[0]
    panel = a_ref[...]
    rows = panel.shape[0] // 2
    pa_ref[...] = panel[:rows]
    pb_ref[...] = panel[rows:]
    gram = lax.dot_general(panel, panel, (((0,), (0,)), ((), ())), precision=HIGH, preferred_element_type=F32)
    top = jnp.where(r == 0, panel[:PANEL], 0.0)
    even = r % 2 == 0
    keep_ref[...] = jnp.where(even, gram, top)
    send_ref[...] = jnp.where(even, top, gram)


def panel_call(r, a):
    rows = a.shape[0]
    half = jax.ShapeDtypeStruct((rows // 2, PANEL), F32)
    square = jax.ShapeDtypeStruct((PANEL, PANEL), F32)
    whole = lambda shape: pl.BlockSpec(shape, lambda i, r: (0,) * len(shape))
    return pl.pallas_call(
        panel_kernel,
        grid_spec=pltpu.PrefetchScalarGridSpec(
            num_scalar_prefetch=1,
            grid=(1,),
            in_specs=[pl.BlockSpec((rows, PANEL), lambda i, r: (0, 0))],
            out_specs=[whole((rows // 2, PANEL))] * 2 + [whole((PANEL, PANEL))] * 2,
        ),
        out_shape=[half, half, square, square],
        compiler_params=params(),
        name="panel",
    )(r, a)


def top_kernel(a_ref, lower_ref, upper_ref):
    for k in range(16):
        lower_ref[k] = a_ref[:, k * PANEL : (k + 1) * PANEL]
        upper_ref[k] = a_ref[:, (k + 16) * PANEL : (k + 17) * PANEL]


def top_call(a):
    cols = a.shape[1]
    out = jax.ShapeDtypeStruct((16, PANEL, PANEL), F32)
    return pl.pallas_call(
        top_kernel,
        grid=(1,),
        in_specs=[pl.BlockSpec((PANEL, cols), lambda i: (0, 0))],
        out_specs=[pl.BlockSpec((16, PANEL, PANEL), lambda i: (0, 0, 0))] * 2,
        out_shape=[out, out],
        compiler_params=params(),
        name="top_rows",
    )(a)


def pick_panel(x, pa, pb, ra1, ra2, rb1, rb2):
    upper = jnp.where(x == 0, pa[...], jnp.where(x == 1, ra1[...], ra2[...]))
    lower = jnp.where(x == 0, pb[...], jnp.where(x == 3, rb1[...], rb2[...]))
    return jnp.concatenate([upper, lower], axis=0)


def product_steps(s_ref, a_ref, lhs, out_ref):
    half = s_ref[2]
    _, b0 = coords(s_ref[0], half)
    high, low = split(a_ref[...])
    both = dot3(lhs, high)
    result = both[:PANEL] + both[PANEL:] + dot3(lhs[:PANEL], low)
    for b in range(4):
        out_ref[(b - b0 + 4) % 4] = result[:, b * PANEL : (b + 1) * PANEL]


def product_first_kernel(s_ref, a_ref, pa, pb, ra1, ra2, rb1, rb2, out_ref, lhs_ref, panel_ref):
    @pl.when(pl.program_id(0) == 0)
    def _():
        panel = pick_panel(s_ref[1], pa, pb, ra1, ra2, rb1, rb2)
        panel_ref[...] = panel
        high, low = split(panel.T)
        lhs_ref[:PANEL] = high
        lhs_ref[PANEL:] = low

    product_steps(s_ref, a_ref, lhs_ref[...], out_ref)


def product_second_kernel(s_ref, a_ref, lhs_ref, out_ref):
    product_steps(s_ref, a_ref, lhs_ref[...], out_ref)


def piece_map(i, s_ref):
    half = s_ref[2]
    a0, _ = coords(s_ref[0], half)
    return (0, half * 4 + (a0 + i) % 4)


def product_call(scalars, a, panels=None, lhs=None):
    rows = a.shape[0]
    whole = lambda shape: pl.BlockSpec(shape, lambda i, s: (0,) * len(shape))
    a_spec = pl.BlockSpec((rows, 512), piece_map)
    w_spec = pl.BlockSpec((4, PANEL, PANEL), lambda i, s: (i, 0, 0))
    w_shape = jax.ShapeDtypeStruct((16, PANEL, PANEL), F32)
    if lhs is None:
        return pl.pallas_call(
            product_first_kernel,
            grid_spec=pltpu.PrefetchScalarGridSpec(
                num_scalar_prefetch=1,
                grid=(4,),
                in_specs=[a_spec] + [whole((rows // 2, PANEL))] * 6,
                out_specs=[w_spec, whole((2 * PANEL, rows)), whole((rows, PANEL))],
            ),
            out_shape=[
                w_shape,
                jax.ShapeDtypeStruct((2 * PANEL, rows), BF16),
                jax.ShapeDtypeStruct((rows, PANEL), F32),
            ],
            compiler_params=params(),
            name="product_first",
        )(scalars, a, *panels)
    return pl.pallas_call(
        product_second_kernel,
        grid_spec=pltpu.PrefetchScalarGridSpec(
            num_scalar_prefetch=1,
            grid=(4,),
            in_specs=[a_spec, whole((2 * PANEL, rows))],
            out_specs=w_spec,
        ),
        out_shape=w_shape,
        compiler_params=params(),
        name="product_second",
    )(scalars, a, lhs)


def eliminate_steps(blocks, full):
    lane = lax.broadcasted_iota(jnp.int32, (8, PANEL), 1)
    sub = lax.broadcasted_iota(jnp.int32, (8, PANEL), 0)
    for k in range(PANEL):
        at, off = k // 8, k % 8
        row = blocks[at][off : off + 1, :]
        inverse = 1.0 / row[:, k : k + 1]
        here = lane == k
        scaled = jnp.where(here[:1], inverse, row * inverse)
        spread = jnp.broadcast_to(scaled, (8, PANEL))
        for i in range(0 if full else at, 16):
            col = jnp.broadcast_to(blocks[i][:, k : k + 1], (8, PANEL))
            new = jnp.where(here, 0.0, blocks[i]) - col * spread
            if i == at:
                if full:
                    new = jnp.where(sub == off, spread, new)
                else:
                    new = jnp.where(sub > off, new, blocks[i])
            blocks[i] = new
    return blocks


def factor_kernel(r_ref, g_ref, other_ref, out_ref):
    even = r_ref[0] % 2 == 0
    gram = jnp.where(even, g_ref[...], other_ref[...])
    blocks = eliminate_steps([gram[8 * i : 8 * i + 8] for i in range(16)], False)
    lane = lax.broadcasted_iota(jnp.int32, (8, PANEL), 1)
    sub = lax.broadcasted_iota(jnp.int32, (8, PANEL), 0)
    for i in range(16):
        at = sub + 8 * i
        pivot = jnp.sum(jnp.where(lane == at, blocks[i], 0.0), axis=1, keepdims=True)
        scale = lax.rsqrt(pivot)
        unit = jnp.where(lane < at, blocks[i], jnp.where(lane == at, 1.0, 0.0))
        out_ref[8 * i : 8 * i + 8] = unit * scale


SMEM_SPEC = pl.BlockSpec(memory_space=pltpu.SMEM)


def small_call(kernel, out_shape, name, *args):
    vmem = pl.BlockSpec(memory_space=pltpu.VMEM)
    return pl.pallas_call(
        kernel,
        in_specs=[SMEM_SPEC] + [vmem] * (len(args) - 1),
        out_specs=vmem,
        out_shape=out_shape,
        compiler_params=params(),
        name=name,
    )(*args)


def basis_kernel(r_ref, linv_ref, g_ref, other_ref, panel_ref, out_ref):
    even = r_ref[0] % 2 == 0
    top = jnp.where(even, other_ref[...], g_ref[...])
    linv = linv_ref[...]
    nt = (((1,), (1,)), ((), ()))
    q_top = lax.dot_general(top, linv, nt, precision=HIGH, preferred_element_type=F32)
    lane = lax.broadcasted_iota(jnp.int32, (8, PANEL), 1)
    sub = lax.broadcasted_iota(jnp.int32, (8, PANEL), 0)
    blocks = [q_top[8 * i : 8 * i + 8] + jnp.where(lane == sub + 8 * i, 1.0, 0.0) for i in range(16)]
    kinv = jnp.concatenate(eliminate_steps(blocks, True), axis=0)
    tn = (((0,), (0,)), ((), ()))
    change = lax.dot_general(linv, kinv, tn, precision=HIGH, preferred_element_type=F32)
    basis = jnp.dot(panel_ref[...], change, precision=HIGH, preferred_element_type=F32)
    rest = basis[PANEL:]
    upper = basis[:PANEL] + jnp.where(r_ref[0] == 0, kinv, 0.0)
    for part, begin, end in ((upper, 0, PANEL), (rest, PANEL, basis.shape[0])):
        high, low = split(part)
        out_ref[begin:end, 0:PANEL] = high
        out_ref[begin:end, PANEL : 2 * PANEL] = low
        out_ref[begin:end, 2 * PANEL :] = high


def shard_kernel(r_ref, linv_ref, top_ref, w0, w1, w2, w3, out_ref):
    w = w0[...] + w1[...] + w2[...] + w3[...]
    out_ref[...] = jnp.dot(linv_ref[...], w, precision=HIGH, preferred_element_type=F32) + top_ref[...]


def update_kernel(s_ref, a_ref, v_ref, z0, z1, z2, z3, *rest):
    out_ref = rest[-1]
    half = s_ref[2]
    _, b0 = coords(s_ref[0], half)
    for i, z_ref in enumerate((z0, z1, z2, z3)):

        @pl.when(pl.program_id(0) == i)
        def _(z_ref=z_ref):
            for b in range(4):
                high, low = split(z_ref[(b0 - b + 4) % 4])
                stacked = jnp.concatenate([high, high, low], axis=0)
                cols = slice(b * PANEL, (b + 1) * PANEL)
                out_ref[:, cols] = a_ref[:, cols] - dot3(v_ref[...], stacked)


def gather_map(i, s_ref):
    half = s_ref[2]
    a0, _ = coords(s_ref[0], half)
    return (0, half * 4 + (a0 - i + 4) % 4)


def update_call(scalars, a, v, pieces, out=None):
    rows, cols = a.shape
    whole = lambda shape: pl.BlockSpec(shape, lambda i, s: (0,) * len(shape))
    extra, extra_specs, alias = (), [], {}
    if out is not None:
        extra, extra_specs, alias = (out,), [pl.BlockSpec(memory_space=pl.ANY)], {7: 0}
    return pl.pallas_call(
        update_kernel,
        grid_spec=pltpu.PrefetchScalarGridSpec(
            num_scalar_prefetch=1,
            grid=(4,),
            in_specs=[pl.BlockSpec((rows, 512), gather_map), whole((rows, 3 * PANEL))]
            + [whole((4, PANEL, PANEL))] * 4
            + extra_specs,
            out_specs=pl.BlockSpec((rows, 512), gather_map),
        ),
        out_shape=jax.ShapeDtypeStruct((rows, cols), F32),
        input_output_aliases=alias,
        compiler_params=params(),
        name="update",
    )(scalars, a, v, *pieces, *extra)


def on_device(a):
    r = lax.axis_index("row").astype(jnp.int32)
    x = lax.axis_index("col").astype(jnp.int32)
    r1 = r.reshape(1)
    core = r % 2
    own = jnp.stack([r, x, core])
    other = jnp.stack([r, x, 1 - core])

    pa, pb, keep, send = panel_call(r1, a)
    ra1 = lax.ppermute(pa, "col", [(0, 1)])
    rb1 = lax.ppermute(pb, "col", [(0, 3)])
    rb2 = lax.ppermute(jnp.where(x == 0, pb, rb1), "col", [(0, 1), (3, 2)])
    ra2 = lax.ppermute(jnp.where(x == 0, pa, ra1), "col", [(0, 3), (1, 2)])

    g = keep + swap(send)
    g = g + first(g, 1) + first(g, 2) + first(g, 3)
    g = g + second(g, 1) + second(g, 2) + second(g, 3)
    away = [lax.ppermute(g, "col", [(0, s)]) for s in (1, 2, 3)]
    g = jnp.where(x == 0, g, away[0] + away[1] + away[2])
    g_other = swap(g)

    lower, upper = top_call(a)
    upper = lax.ppermute(upper, "row", [(0, 1)])
    mine = jnp.where(core == 0, lower, upper)
    top = mine[0:4]
    corner = lambda z, y, c: z == 0 and y == 0
    for s in (1, 2, 3):
        got = lax.ppermute(mine[4 * s : 4 * s + 4], "row", axis_pairs(0, s, corner))
        top = jnp.where((jnp.where(core == 0, (r // 2) % 4, r // 8)) == s, got, top)
    edge = lambda z, y, c: (z if c == 0 else y) == 0
    shard_top = top[0]
    for t in (1, 2, 3):
        got = lax.ppermute(top[t], "row", axis_pairs(1, t, edge))
        shard_top = jnp.where((jnp.where(core == 0, r // 8, (r // 2) % 4)) == t, got, shard_top)

    w_other, lhs, panel = product_call(other, a, panels=(pa, pb, ra1, ra2, rb1, rb2))
    w_got = swap(w_other)
    w_own = product_call(own, a, lhs=lhs)
    w = [w_own[4 * s : 4 * s + 4] + w_got[4 * s : 4 * s + 4] for s in range(4)]
    w = w[0] + first(w[1], 1) + first(w[2], 2) + first(w[3], 3)
    w = [w[0]] + [second(w[t], t) for t in (1, 2, 3)]

    square = jax.ShapeDtypeStruct((PANEL, PANEL), F32)
    linv = small_call(factor_kernel, square, "factor", r1, g, g_other)
    z = small_call(shard_kernel, square, "shard", r1, linv, shard_top, *w)

    z = jnp.stack([z] + [second(z, t) for t in (1, 2, 3)])
    pieces = [z] + [first(z, s) for s in (1, 2, 3)]
    got = [swap(piece) for piece in pieces]

    stacked = jax.ShapeDtypeStruct((a.shape[0], 3 * PANEL), BF16)
    v = small_call(basis_kernel, stacked, "basis", r1, linv, g, g_other, panel)
    out = update_call(own, a, v, pieces)
    return update_call(other, a, v, got, out)


def solution(mesh):
    return jax.shard_map(
        on_device, mesh=mesh, in_specs=(P("row", "col"),), out_specs=P("row", "col"), check_vma=False
    )
```

time: 845 us -> 139 us (0.16); the launches traced: 834 us -> 138 us
  waiting for transfers between devices: 334 us -> 15 us
  other arithmetic: 235 us -> 4.91 us
  local copies, waits for them, and re-layouts: 164 us -> 0.92 us
  starting transfers between devices: 0.13 us -> 61.9 us
  between operations: 55.7 us -> 0.37 us
  Pallas kernels: 0 us -> 54.7 us
  matrix products: 45.8 us -> 0 us
    psum x4 -> x0, waiting for transfers between devices: 334 us -> none  [the longest x2 138 us: broadcast(): return lax.psum(jnp.where(mine, x, jnp.zeros_like(x)), axis)]
    another operation x68 -> x3, other arithmetic: 84.7 us -> 0.17 us  [the longest x1 0.08 us: on_device(): own = jnp.stack([r, x, core])]
    slice x216 -> x1, local copies, waits for them, and re-layouts: 82.6 us -> 0.88 us  [on_device(): got = lax.ppermute(mine[4 * s:4 * s + 4], 'row', axis_pairs(0, s, corner))]
    scatter x224 -> x0, local copies, waits for them, and re-layouts: 76.9 us -> none  [the longest x112 45.8 us: column_steps(): current = current.at[column + 1:, column + 1:].set(trailing_block)]
    div x97 -> x0, other arithmetic: 69.7 us -> none  [the longest x96 68.8 us: column_steps(): multiplier = current[column + 1:, column] / pivot_value]
    mul x96 -> x0, other arithmetic: 68.5 us -> none  [column_steps(): multiplier[:, None] * current[column, column + 1:][None, :]]
    ppermute x0 -> x39, starting transfers between devices: none -> 61.9 us  [the longest x7 18.2 us: swap(): return lax.ppermute(x, 'row', CORE_PAIRS)]
    pallas_call x0 -> x9, Pallas kernels: none -> 54.7 us  [the longest x3 23.3 us: small_call(): pl.pallas_call(kernel, in_specs=[SMEM_SPEC] + [vmem] * (len(args) - 1), o...]
  transfers between devices with their start and end apart: 4 -> 39, of which waited for: 4 -> 14; matrix products, arithmetic and copies ran while one was open for 1% -> 4% of each run, Pallas kernels for 0% -> 33%
where the time goes in v1:
time: 139 us; the launch traced here: 138 us
  starting transfers between devices  61.9 us (45%)
  Pallas kernels  54.7 us (39%)
  waiting for transfers between devices  15 us (11%)
  other arithmetic  4.91 us (4%)
    pallas_call x3, Pallas kernels, small_call(): pl.pallas_call(kernel, in_specs=[SMEM_SPEC] + [vmem] * (len(args) - 1), o...  23.3 us
    ppermute x7, starting transfers between devices, swap(): return lax.ppermute(x, 'row', CORE_PAIRS)  18.2 us
    pallas_call x2, Pallas kernels, update_call(): pl.pallas_call(update_kernel, grid_spec=pltpu.PrefetchScalarGridSpec(num_...  16.1 us
    ppermute x9, starting transfers between devices, first(): return lax.ppermute(x, 'row', axis_pairs(0, step))  10.5 us
    ppermute x9, waiting for transfers between devices, second(): return lax.ppermute(x, 'row', axis_pairs(1, step))  8.8 us
    ppermute x9, starting transfers between devices, second(): return lax.ppermute(x, 'row', axis_pairs(1, step))  7.61 us
    ppermute x3, starting transfers between devices, on_device(): got = lax.ppermute(mine[4 * s:4 * s + 4], 'row', axis_pairs(0, s, corner))  6.32 us
    pallas_call x1, Pallas kernels, product_call(): pl.pallas_call(product_first_kernel, grid_spec=pltpu.PrefetchScalarGridSp...  6.09 us
  transfers between devices with their start and end apart: 39, of which 14 were waited for; matrix products, arithmetic and copies ran while one was open for 4% of the time, Pallas kernels for 33%

profile of v1, /device:TPU:1, one launch (start us, length us, event | category | flops | bytes accessed | tf_op | source)
XLA Modules:
  0.0 137.8 jit_solution(16866081496733499113)
XLA Ops:
  1.5 4.0 %collective-permute-start.11 = (f32[384,128]{1,0:T(8,128)S(1)}, f32[384,128]{1,0:T(8,128)S(1)}, u32[]{:S(2)}, u32[]{:S(2)}) collective-permute-start(f32[384,128]{1,0:T(8,128)S(1)} %get-tuple-element.16.pa), channel_id=1, source_target_pairs={{0,1},{4,5},{8,9},{12,13},{16,17},{20,21},{24,25},{28,29},{32,33},... | collective-permute-start | bytes 589832 | tf_op jit(solution)/shard_map/ppermute | solution.py:327
  6.5 1.6 %collective-permute-start.13 = (f32[384,128]{1,0:T(8,128)S(1)}, f32[384,128]{1,0:T(8,128)S(1)}, u32[]{:S(2)}, u32[]{:S(2)}) collective-permute-start(f32[384,128]{1,0:T(8,128)S(1)} %get-tuple-element.17.pb), channel_id=1, source_target_pairs={{0,3},{4,7},{8,11},{12,15},{16,19},{20,23},{24,27},{28,31},{32,35}... | collective-permute-start | bytes 589832 | tf_op jit(solution)/shard_map/ppermute | solution.py:328
  8.2 2.6 %top_rows.1 = (f32[16,128,128]{2,1,0:T(8,128)S(1)}, f32[16,128,128]{2,1,0:T(8,128)}) custom-call(f32[768,4096]{1,0:T(8,128)} %a_ref.11), custom_call_target="tpu_custom_call" | custom-call | tf_op jit(solution)/shard_map/top_rows/pallas_call | solution.py:110
  12.2 4.1 %collective-permute-start.3 = (f32[128,128]{1,0:T(8,128)S(1)}, f32[128,128]{1,0:T(8,128)S(1)}, u32[]{:S(2)}, u32[]{:S(2)}) collective-permute-start(f32[128,128]{1,0:T(8,128)S(1)} %add.63), channel_id=1, source_target_pairs={{0,24},{4,100},{8,0},{12,108},{16,8},{20,116},{24,16},{28,124},{32... | collective-permute-start | bytes 196616 | tf_op jit(solution)/shard_map/ppermute | solution.py:40
  21.6 2.5 %collective-permute-start.6 = (f32[128,128]{1,0:T(8,128)S(1)}, f32[128,128]{1,0:T(8,128)S(1)}, u32[]{:S(2)}, u32[]{:S(2)}) collective-permute-start(f32[128,128]{1,0:T(8,128)S(1)} %add_add_fusion.1), channel_id=1, source_target_pairs={{0,96},{4,28},{8,104},{12,4},{16,112},{20,12},{24,120},{28,20},{32... | collective-permute-start | bytes 196616 | tf_op jit(solution)/shard_map/ppermute | solution.py:44
  25.3 6.1 %product_first.1 = (f32[16,128,128]{2,1,0:T(8,128)}, bf16[256,768]{1,0:T(8,128)(2,1)S(1)}, f32[768,128]{1,0:T(8,128)S(1)}) custom-call(s32[3]{0:T(128)S(1)} %pad_add_fusion.s_ref, f32[768,4096]{1,0:T(8,128)} %a_ref.11, f32[384,128]{1,0:T(8,128)S(1)} %get-tuple-element.16.pa, f32[384,128]{1,0:T(8,128)S(1)} %get-tuple-element.17.pb, ...), custom_call_target="tpu_custom_call" | custom-call | tf_op jit(solution)/shard_map/product_first/pallas_call | solution.py:166
  31.4 2.5 %collective-permute-start.22 = (f32[16,128,128]{2,1,0:T(8,128)}, f32[16,128,128]{2,1,0:T(8,128)}, u32[]{:S(2)}, u32[]{:S(2)}) collective-permute-start(f32[16,128,128]{2,1,0:T(8,128)} %get-tuple-element.22), channel_id=1, source_target_pairs={{0,4},{4,0},{8,12},{12,8},{16,20},{20,16},{24,28},{28,24},{32,36},... | collective-permute-start | bytes 3145736 | tf_op jit(solution)/shard_map/ppermute | solution.py:48
  33.9 3.3 %collective-permute-start.9 = (f32[128,128]{1,0:T(8,128)S(1)}, f32[128,128]{1,0:T(8,128)S(1)}, u32[]{:S(2)}, u32[]{:S(2)}) collective-permute-start(f32[128,128]{1,0:T(8,128)S(1)} %add_add_fusion), channel_id=1, source_target_pairs={{0,3},{4,7},{8,11},{12,15},{16,19},{20,23},{24,27},{28,31},{32,35}... | collective-permute-start | bytes 196616 | tf_op jit(solution)/shard_map/ppermute | solution.py:335
  44.5 2.7 %collective-permute-start.18 = (f32[4,128,128]{2,1,0:T(8,128)}, f32[4,128,128]{2,1,0:T(8,128)S(1)}, u32[]{:S(2)}, u32[]{:S(2)}) collective-permute-start(f32[4,128,128]{2,1,0:T(8,128)} %get-tuple-element.26), channel_id=1, source_target_pairs={{0,8},{4,36},{1,9},{5,37},{2,10},{6,38},{3,11},{7,39}} | collective-permute-start | bytes 786440 | tf_op jit(solution)/shard_map/ppermute | solution.py:345
  47.2 2.3 %collective-permute-start.17 = (f32[4,128,128]{2,1,0:T(8,128)S(1)}, f32[4,128,128]{2,1,0:T(8,128)S(1)}, u32[]{:S(2)}, u32[]{:S(2)}) collective-permute-start(f32[4,128,128]{2,1,0:T(8,128)S(1)} %get-tuple-element.27), channel_id=1, source_target_pairs={{0,16},{4,68},{1,17},{5,69},{2,18},{6,70},{3,19},{7,71}} | collective-permute-start | bytes 786440 | tf_op jit(solution)/shard_map/ppermute | solution.py:345
  51.0 10.9 %factor.1.linv_ref = f32[128,128]{1,0:T(8,128)S(1)} custom-call(s32[1]{0:T(128)} %bitcast.r_ref, f32[128,128]{1,0:T(8,128)S(1)} %add_select_fusion.g_ref, f32[128,128]{1,0:T(8,128)S(1)} %collective-permute-done.10.other_ref), custom_call_target="tpu_custom_call" | custom-call | tf_op jit(solution)/shard_map/factor/pallas_call | solution.py:237
  61.9 5.1 %product_second.1 = f32[16,128,128]{2,1,0:T(8,128)S(1)} custom-call(s32[3]{0:T(128)S(1)} %pad_add_fusion.2.s_ref, f32[768,4096]{1,0:T(8,128)} %a_ref.11, bf16[256,768]{1,0:T(8,128)(2,1)S(1)} %get-tuple-element.21.lhs_ref), custom_call_target="tpu_custom_call" | custom-call | tf_op jit(solution)/shard_map/product_second/pallas_call | solution.py:182
  68.3 2.7 %collective-permute-start.25 = (f32[4,128,128]{2,1,0:T(8,128)S(1)}, f32[4,128,128]{2,1,0:T(8,128)S(1)}, u32[]{:S(2)}, u32[]{:S(2)}) collective-permute-start(f32[4,128,128]{2,1,0:T(8,128)S(1)} %get-tuple-element.24), channel_id=1, source_target_pairs={{0,24},{4,100},{8,0},{12,108},{16,8},{20,116},{24,16},{28,124},{32... | collective-permute-start | bytes 786440 | tf_op jit(solution)/shard_map/ppermute | solution.py:40
  80.6 1.6 %collective-permute-done.28.w3 = f32[128,128]{1,0:T(8,128)S(1)} collective-permute-done((f32[128,128]{1,0:T(8,128)S(1)}, f32[128,128]{1,0:T(8,128)S(1)}, u32[]{:S(2)}, u32[]{:S(2)}) %collective-permute-start.28) | collective-permute-done | bytes 65568 | tf_op jit(solution)/shard_map/ppermute | solution.py:44
  82.2 1.6 %collective-permute-done.27.w2 = f32[128,128]{1,0:T(8,128)S(1)} collective-permute-done((f32[128,128]{1,0:T(8,128)S(1)}, f32[128,128]{1,0:T(8,128)S(1)}, u32[]{:S(2)}, u32[]{:S(2)}) %collective-permute-start.27) | collective-permute-done | bytes 65568 | tf_op jit(solution)/shard_map/ppermute | solution.py:44
  85.1 1.7 %collective-permute-start.31 = (f32[128,128]{1,0:T(8,128)S(1)}, f32[128,128]{1,0:T(8,128)S(1)}, u32[]{:S(2)}, u32[]{:S(2)}) collective-permute-start(f32[128,128]{1,0:T(8,128)S(1)} %shard.1), channel_id=1, source_target_pairs={{0,96},{4,28},{8,104},{12,4},{16,112},{20,12},{24,120},{28,20},{32... | collective-permute-start | bytes 196616 | tf_op jit(solution)/shard_map/ppermute | solution.py:44
  88.5 3.0 %collective-permute-done.30 = f32[128,128]{1,0:T(8,128)S(1)} collective-permute-done((f32[128,128]{1,0:T(8,128)S(1)}, f32[128,128]{1,0:T(8,128)S(1)}, u32[]{:S(2)}, u32[]{:S(2)}) %collective-permute-start.30) | collective-permute-done | bytes 65568 | tf_op jit(solution)/shard_map/ppermute | solution.py:44
  92.2 2.3 %collective-permute-start.37 = (f32[4,128,128]{2,1,0:T(8,128)S(1)}, f32[4,128,128]{2,1,0:T(8,128)S(1)}, u32[]{:S(2)}, u32[]{:S(2)}) collective-permute-start(f32[4,128,128]{2,1,0:T(8,128)S(1)} %pad_maximum_fusion.z0), channel_id=1, source_target_pairs={{0,24},{4,100},{8,0},{12,108},{16,8},{20,116},{24,16},{28,124},{32... | collective-permute-start | bytes 786440 | tf_op jit(solution)/shard_map/ppermute | solution.py:40
  95.1 5.0 %collective-permute-start.32 = (f32[4,128,128]{2,1,0:T(8,128)S(1)}, f32[4,128,128]{2,1,0:T(8,128)S(1)}, u32[]{:S(2)}, u32[]{:S(2)}) collective-permute-start(f32[4,128,128]{2,1,0:T(8,128)S(1)} %pad_maximum_fusion.z0), channel_id=1, source_target_pairs={{0,4},{4,0},{8,12},{12,8},{16,20},{20,16},{24,28},{28,24},{32,36},... | collective-permute-start | bytes 786440 | tf_op jit(solution)/shard_map/ppermute | solution.py:48
  100.6 5.2 %collective-permute-start.38 = (f32[4,128,128]{2,1,0:T(8,128)S(1)}, f32[4,128,128]{2,1,0:T(8,128)S(1)}, u32[]{:S(2)}, u32[]{:S(2)}) collective-permute-start(f32[4,128,128]{2,1,0:T(8,128)S(1)} %collective-permute-done.37.z3), channel_id=1, source_target_pairs={{0,4},{4,0},{8,12},{12,8},{16,20},{20,16},{24,28},{28,24},{32,36},... | collective-permute-start | bytes 786440 | tf_op jit(solution)/shard_map/ppermute | solution.py:48
  107.1 2.4 %collective-permute-start.34 = (f32[4,128,128]{2,1,0:T(8,128)S(1)}, f32[4,128,128]{2,1,0:T(8,128)S(1)}, u32[]{:S(2)}, u32[]{:S(2)}) collective-permute-start(f32[4,128,128]{2,1,0:T(8,128)S(1)} %collective-permute-done.33.z1), channel_id=1, source_target_pairs={{0,4},{4,0},{8,12},{12,8},{16,20},{20,16},{24,28},{28,24},{32,36},... | collective-permute-start | bytes 786440 | tf_op jit(solution)/shard_map/ppermute | solution.py:48
  109.5 12.1 %basis.1.v_ref = bf16[768,384]{1,0:T(8,128)(2,1)S(1)} custom-call(s32[1]{0:T(128)} %bitcast.r_ref, f32[128,128]{1,0:T(8,128)S(1)} %factor.1.linv_ref, f32[128,128]{1,0:T(8,128)S(1)} %add_select_fusion.g_ref, f32[128,128]{1,0:T(8,128)S(1)} %collective-permute-done.10.other_ref, f32[768,128]{1,0:T(8,128)S(1)} %get-tuple-element.18.panel_ref), custom_call_target="tpu_custom_call" | custom-call | tf_op jit(solution)/shard_map/basis/pallas_call | solution.py:237
  121.7 8.1 %update.2.rest_0_ = f32[768,4096]{1,0:T(8,128)} custom-call(s32[3]{0:T(128)S(1)} %pad_add_fusion.2.s_ref, f32[768,4096]{1,0:T(8,128)} %a_ref.11, bf16[768,384]{1,0:T(8,128)(2,1)S(1)} %basis.1.v_ref, f32[4,128,128]{2,1,0:T(8,128)S(1)} %pad_maximum_fusion.z0, f32[4,128,128]{2,1,0:T(8,128)S(1)} %collective-permute-done.33.z1, ...), custom_call_target="tpu_custom_call" | custom-call | tf_op jit(solution)/shard_map/update/pallas_call | solution.py:301
  129.8 8.1 %update.3 = f32[768,4096]{1,0:T(8,128)} custom-call(s32[3]{0:T(128)S(1)} %pad_add_fusion.s_ref, f32[768,4096]{1,0:T(8,128)} %a_ref.11, bf16[768,384]{1,0:T(8,128)(2,1)S(1)} %basis.1.v_ref, f32[4,128,128]{2,1,0:T(8,128)S(1)} %collective-permute-done.32.z0, f32[4,128,128]{2,1,0:T(8,128)S(1)} %collective-permute-done.34.z1, ...), custom_call_target="tpu_custom_call", output_to_operand_aliasing={{}: (7, {})} | custom-call | tf_op jit(solution)/shard_map/update/pallas_call | solution.py:301
  (82 shorter events, 36.0 us)
Async XLA Ops:
  1.5 14.8 %collective-permute-start.11 = (f32[384,128]{1,0:T(8,128)S(1)}, f32[384,128]{1,0:T(8,128)S(1)}, u32[]{:S(2)}, u32[]{:S(2)}) collective-permute-start(f32[384,128]{1,0:T(8,128)S(1)} %get-tuple-element.16.pa), channel_id=1, source_target_pairs={{0,1},{4,5},{8,9},{12,13},{16,17},{20,21},{24,25},{28,29},{32,33},... | collective-permute-start | bytes 589832 | tf_op jit(solution)/shard_map/ppermute | solution.py:327
  6.5 10.5 %collective-permute-start.13 = (f32[384,128]{1,0:T(8,128)S(1)}, f32[384,128]{1,0:T(8,128)S(1)}, u32[]{:S(2)}, u32[]{:S(2)}) collective-permute-start(f32[384,128]{1,0:T(8,128)S(1)} %get-tuple-element.17.pb), channel_id=1, source_target_pairs={{0,3},{4,7},{8,11},{12,15},{16,19},{20,23},{24,27},{28,31},{32,35}... | collective-permute-start | bytes 589832 | tf_op jit(solution)/shard_map/ppermute | solution.py:328
  10.8 31.5 %collective-permute-start.15 = (f32[16,128,128]{2,1,0:T(8,128)}, f32[16,128,128]{2,1,0:T(8,128)}, u32[]{:S(2)}, u32[]{:S(2)}) collective-permute-start(f32[16,128,128]{2,1,0:T(8,128)} %get-tuple-element.20), channel_id=1, source_target_pairs={{0,4},{1,5},{2,6},{3,7}} | collective-permute-start | bytes 3145736 | tf_op jit(solution)/shard_map/ppermute | solution.py:340
  17.0 7.5 %collective-permute-start.12 = (f32[384,128]{1,0:T(8,128)S(1)}, f32[384,128]{1,0:T(8,128)S(1)}, u32[]{:S(2)}, u32[]{:S(2)}) collective-permute-start(f32[384,128]{1,0:T(8,128)S(1)} %broadcast_select_fusion.2), channel_id=1, source_target_pairs={{0,3},{1,2},{4,7},{5,6},{8,11},{9,10},{12,15},{13,14},{16,19},{17,... | collective-permute-start | bytes 589832 | tf_op jit(solution)/shard_map/ppermute | solution.py:330
  18.4 6.9 %collective-permute-start.14 = (f32[384,128]{1,0:T(8,128)S(1)}, f32[384,128]{1,0:T(8,128)S(1)}, u32[]{:S(2)}, u32[]{:S(2)}) collective-permute-start(f32[384,128]{1,0:T(8,128)S(1)} %broadcast_select_fusion.1), channel_id=1, source_target_pairs={{0,1},{3,2},{4,5},{7,6},{8,9},{11,10},{12,13},{15,14},{16,17},{19,... | collective-permute-start | bytes 589832 | tf_op jit(solution)/shard_map/ppermute | solution.py:329
  21.6 12.2 %collective-permute-start.6 = (f32[128,128]{1,0:T(8,128)S(1)}, f32[128,128]{1,0:T(8,128)S(1)}, u32[]{:S(2)}, u32[]{:S(2)}) collective-permute-start(f32[128,128]{1,0:T(8,128)S(1)} %add_add_fusion.1), channel_id=1, source_target_pairs={{0,96},{4,28},{8,104},{12,4},{16,112},{20,12},{24,120},{28,20},{32... | collective-permute-start | bytes 196616 | tf_op jit(solution)/shard_map/ppermute | solution.py:44
  24.2 9.7 %collective-permute-start.5 = (f32[128,128]{1,0:T(8,128)S(1)}, f32[128,128]{1,0:T(8,128)S(1)}, u32[]{:S(2)}, u32[]{:S(2)}) collective-permute-start(f32[128,128]{1,0:T(8,128)S(1)} %add_add_fusion.1), channel_id=1, source_target_pairs={{0,64},{4,20},{8,72},{12,28},{16,80},{20,4},{24,88},{28,12},{32,96... | collective-permute-start | bytes 196616 | tf_op jit(solution)/shard_map/ppermute | solution.py:44
  24.5 9.4 %collective-permute-start.4 = (f32[128,128]{1,0:T(8,128)S(1)}, f32[128,128]{1,0:T(8,128)S(1)}, u32[]{:S(2)}, u32[]{:S(2)}) collective-permute-start(f32[128,128]{1,0:T(8,128)S(1)} %add_add_fusion.1), channel_id=1, source_target_pairs={{0,32},{4,12},{8,40},{12,20},{16,48},{20,28},{24,56},{28,4},{32,64... | collective-permute-start | bytes 196616 | tf_op jit(solution)/shard_map/ppermute | solution.py:44
  31.4 35.6 %collective-permute-start.22 = (f32[16,128,128]{2,1,0:T(8,128)}, f32[16,128,128]{2,1,0:T(8,128)}, u32[]{:S(2)}, u32[]{:S(2)}) collective-permute-start(f32[16,128,128]{2,1,0:T(8,128)} %get-tuple-element.22), channel_id=1, source_target_pairs={{0,4},{4,0},{8,12},{12,8},{16,20},{20,16},{24,28},{28,24},{32,36},... | collective-permute-start | bytes 3145736 | tf_op jit(solution)/shard_map/ppermute | solution.py:48
  41.5 9.4 %collective-permute-start.10 = (f32[128,128]{1,0:T(8,128)S(1)}, f32[128,128]{1,0:T(8,128)S(1)}, u32[]{:S(2)}, u32[]{:S(2)}) collective-permute-start(f32[128,128]{1,0:T(8,128)S(1)} %add_select_fusion.g_ref), channel_id=1, source_target_pairs={{0,4},{4,0},{8,12},{12,8},{16,20},{20,16},{24,28},{28,24},{32,36},... | collective-permute-start | bytes 196616 | tf_op jit(solution)/shard_map/ppermute | solution.py:48
  44.5 26.4 %collective-permute-start.18 = (f32[4,128,128]{2,1,0:T(8,128)}, f32[4,128,128]{2,1,0:T(8,128)S(1)}, u32[]{:S(2)}, u32[]{:S(2)}) collective-permute-start(f32[4,128,128]{2,1,0:T(8,128)} %get-tuple-element.26), channel_id=1, source_target_pairs={{0,8},{4,36},{1,9},{5,37},{2,10},{6,38},{3,11},{7,39}} | collective-permute-start | bytes 786440 | tf_op jit(solution)/shard_map/ppermute | solution.py:345
  47.2 23.7 %collective-permute-start.17 = (f32[4,128,128]{2,1,0:T(8,128)S(1)}, f32[4,128,128]{2,1,0:T(8,128)S(1)}, u32[]{:S(2)}, u32[]{:S(2)}) collective-permute-start(f32[4,128,128]{2,1,0:T(8,128)S(1)} %get-tuple-element.27), channel_id=1, source_target_pairs={{0,16},{4,68},{1,17},{5,69},{2,18},{6,70},{3,19},{7,71}} | collective-permute-start | bytes 786440 | tf_op jit(solution)/shard_map/ppermute | solution.py:345
  49.6 21.4 %collective-permute-start.16 = (f32[4,128,128]{2,1,0:T(8,128)S(1)}, f32[4,128,128]{2,1,0:T(8,128)S(1)}, u32[]{:S(2)}, u32[]{:S(2)}) collective-permute-start(f32[4,128,128]{2,1,0:T(8,128)S(1)} %get-tuple-element.28), channel_id=1, source_target_pairs={{0,24},{4,100},{1,25},{5,101},{2,26},{6,102},{3,27},{7,103}} | collective-permute-start | bytes 786440 | tf_op jit(solution)/shard_map/ppermute | solution.py:345
  68.3 8.8 %collective-permute-start.25 = (f32[4,128,128]{2,1,0:T(8,128)S(1)}, f32[4,128,128]{2,1,0:T(8,128)S(1)}, u32[]{:S(2)}, u32[]{:S(2)}) collective-permute-start(f32[4,128,128]{2,1,0:T(8,128)S(1)} %get-tuple-element.24), channel_id=1, source_target_pairs={{0,24},{4,100},{8,0},{12,108},{16,8},{20,116},{24,16},{28,124},{32... | collective-permute-start | bytes 786440 | tf_op jit(solution)/shard_map/ppermute | solution.py:40
  70.9 7.0 %collective-permute-start.24 = (f32[4,128,128]{2,1,0:T(8,128)S(1)}, f32[4,128,128]{2,1,0:T(8,128)S(1)}, u32[]{:S(2)}, u32[]{:S(2)}) collective-permute-start(f32[4,128,128]{2,1,0:T(8,128)S(1)} %get-tuple-element.25), channel_id=1, source_target_pairs={{0,16},{4,68},{8,24},{12,76},{16,0},{20,84},{24,8},{28,92},{32,48}... | collective-permute-start | bytes 786440 | tf_op jit(solution)/shard_map/ppermute | solution.py:40
  72.0 7.2 %collective-permute-start.21 = (f32[128,128]{1,0:T(8,128)S(1)}, f32[128,128]{1,0:T(8,128)S(1)}, u32[]{:S(2)}, u32[]{:S(2)}) collective-permute-start(f32[128,128]{1,0:T(8,128)S(1)} %get-tuple-element.33), channel_id=1, source_target_pairs={{0,32},{4,12},{8,40},{16,48},{24,56},{36,44},{68,76},{100,108},{1,... | collective-permute-start | bytes 196616 | tf_op jit(solution)/shard_map/ppermute | solution.py:350
  73.3 7.3 %collective-permute-start.20 = (f32[128,128]{1,0:T(8,128)S(1)}, f32[128,128]{1,0:T(8,128)S(1)}, u32[]{:S(2)}, u32[]{:S(2)}) collective-permute-start(f32[128,128]{1,0:T(8,128)S(1)} %get-tuple-element.34), channel_id=1, source_target_pairs={{0,64},{4,20},{8,72},{16,80},{24,88},{36,52},{68,84},{100,116},{1,... | collective-permute-start | bytes 196616 | tf_op jit(solution)/shard_map/ppermute | solution.py:350
  92.2 8.4 %collective-permute-start.37 = (f32[4,128,128]{2,1,0:T(8,128)S(1)}, f32[4,128,128]{2,1,0:T(8,128)S(1)}, u32[]{:S(2)}, u32[]{:S(2)}) collective-permute-start(f32[4,128,128]{2,1,0:T(8,128)S(1)} %pad_maximum_fusion.z0), channel_id=1, source_target_pairs={{0,24},{4,100},{8,0},{12,108},{16,8},{20,116},{24,16},{28,124},{32... | collective-permute-start | bytes 786440 | tf_op jit(solution)/shard_map/ppermute | solution.py:40
  94.5 11.4 %collective-permute-start.35 = (f32[4,128,128]{2,1,0:T(8,128)S(1)}, f32[4,128,128]{2,1,0:T(8,128)S(1)}, u32[]{:S(2)}, u32[]{:S(2)}) collective-permute-start(f32[4,128,128]{2,1,0:T(8,128)S(1)} %pad_maximum_fusion.z0), channel_id=1, source_target_pairs={{0,16},{4,68},{8,24},{12,76},{16,0},{20,84},{24,8},{28,92},{32,48}... | collective-permute-start | bytes 786440 | tf_op jit(solution)/shard_map/ppermute | solution.py:40
  94.5 12.7 %collective-permute-start.33 = (f32[4,128,128]{2,1,0:T(8,128)S(1)}, f32[4,128,128]{2,1,0:T(8,128)S(1)}, u32[]{:S(2)}, u32[]{:S(2)}) collective-permute-start(f32[4,128,128]{2,1,0:T(8,128)S(1)} %pad_maximum_fusion.z0), channel_id=1, source_target_pairs={{0,8},{4,36},{8,16},{12,44},{16,24},{20,52},{24,0},{28,60},{32,40}... | collective-permute-start | bytes 786440 | tf_op jit(solution)/shard_map/ppermute | solution.py:40
  95.1 34.6 %collective-permute-start.32 = (f32[4,128,128]{2,1,0:T(8,128)S(1)}, f32[4,128,128]{2,1,0:T(8,128)S(1)}, u32[]{:S(2)}, u32[]{:S(2)}) collective-permute-start(f32[4,128,128]{2,1,0:T(8,128)S(1)} %pad_maximum_fusion.z0), channel_id=1, source_target_pairs={{0,4},{4,0},{8,12},{12,8},{16,20},{20,16},{24,28},{28,24},{32,36},... | collective-permute-start | bytes 786440 | tf_op jit(solution)/shard_map/ppermute | solution.py:48
  100.6 29.1 %collective-permute-start.38 = (f32[4,128,128]{2,1,0:T(8,128)S(1)}, f32[4,128,128]{2,1,0:T(8,128)S(1)}, u32[]{:S(2)}, u32[]{:S(2)}) collective-permute-start(f32[4,128,128]{2,1,0:T(8,128)S(1)} %collective-permute-done.37.z3), channel_id=1, source_target_pairs={{0,4},{4,0},{8,12},{12,8},{16,20},{20,16},{24,28},{28,24},{32,36},... | collective-permute-start | bytes 786440 | tf_op jit(solution)/shard_map/ppermute | solution.py:48
  105.8 23.9 %collective-permute-start.36 = (f32[4,128,128]{2,1,0:T(8,128)S(1)}, f32[4,128,128]{2,1,0:T(8,128)S(1)}, u32[]{:S(2)}, u32[]{:S(2)}) collective-permute-start(f32[4,128,128]{2,1,0:T(8,128)S(1)} %collective-permute-done.35.z2), channel_id=1, source_target_pairs={{0,4},{4,0},{8,12},{12,8},{16,20},{20,16},{24,28},{28,24},{32,36},... | collective-permute-start | bytes 786440 | tf_op jit(solution)/shard_map/ppermute | solution.py:48
  107.1 22.6 %collective-permute-start.34 = (f32[4,128,128]{2,1,0:T(8,128)S(1)}, f32[4,128,128]{2,1,0:T(8,128)S(1)}, u32[]{:S(2)}, u32[]{:S(2)}) collective-permute-start(f32[4,128,128]{2,1,0:T(8,128)S(1)} %collective-permute-done.33.z1), channel_id=1, source_target_pairs={{0,4},{4,0},{8,12},{12,8},{16,20},{20,16},{24,28},{28,24},{32,36},... | collective-permute-start | bytes 786440 | tf_op jit(solution)/shard_map/ppermute | solution.py:48
  (16 other events, 80.5 us)

commit v2 on v0

v2 whole, which is shorter than its diff:
```python
import functools

import jax
import jax.numpy as jnp
from jax import lax
from jax.experimental import pallas as pl
from jax.experimental.pallas import tpu as pltpu
from jax.sharding import PartitionSpec as P

PANEL = 128
WIDTH = 512
LARGE = 52
HIGH = lax.Precision.HIGHEST
F32 = jnp.float32
BF16 = jnp.bfloat16


def near(a):
    return a ^ 1


def far(a):
    return 3 - a


def row_of(z, y, c):
    return (z * 4 + y) * 2 + c


def axis_pairs(which, step, keep=lambda a, b: True):
    pairs = []
    for z in range(4):
        for y in range(4):
            for c in range(2):
                a, b = (z, y) if c else (y, z)
                if keep(a, b):
                    to = (step(a), b) if which == 0 else (a, step(b))
                    tz, ty = to if c else to[::-1]
                    pairs.append((row_of(z, y, c), row_of(tz, ty, c)))
    return pairs


def along(which, step, x, keep=lambda a, b: True):
    return lax.ppermute(x, "row", axis_pairs(which, step, keep))


def swap(x):
    return lax.ppermute(x, "row", [(r, r ^ 1) for r in range(32)])


def piece_at(a0, i):
    return jnp.where(i == 0, a0, jnp.where(i == 1, far(a0), jnp.where(i == 2, near(a0), a0 ^ 2)))


def dot3(x, y):
    return jnp.dot(x, y, preferred_element_type=F32)


def split(x):
    high = x.astype(BF16)
    return high, (x - high.astype(F32)).astype(BF16)


def params(mib):
    return pltpu.CompilerParams(vmem_limit_bytes=mib << 20)


def cost_of(microseconds):
    return pl.CostEstimate(flops=int(microseconds * 1.15e9), bytes_accessed=0, transcendentals=0)


def small_call(kernel, shapes, name, *args, scratch=(), mib=8, after=(), cost=None, hbm=0):
    vmem = pl.BlockSpec(memory_space=pltpu.VMEM)
    shapes = [shape if isinstance(shape[0], tuple) else (shape, F32) for shape in shapes]
    return pl.pallas_call(
        kernel,
        in_specs=[pl.BlockSpec(memory_space=pltpu.HBM)] * hbm
        + [vmem] * (len(args) - hbm)
        + [pl.BlockSpec(memory_space=pl.ANY)] * len(after),
        out_specs=[vmem] * len(shapes),
        out_shape=[jax.ShapeDtypeStruct(*shape) for shape in shapes],
        scratch_shapes=scratch,
        compiler_params=params(mib),
        cost_estimate=cost,
        name=name,
    )(*args, *after)


def place(flip=False):
    r = lax.axis_index("row")
    z, y, core = r >> 3, (r >> 1) & 3, r & 1
    if flip:
        core = 1 - core
    return core, jnp.where(core == 0, y, z), jnp.where(core == 0, z, y)


def panel_kernel(a_ref, pa_ref, pb_ref, sem):
    rows = pa_ref.shape[0]
    copies = [
        pltpu.make_async_copy(a_ref.at[i * rows : (i + 1) * rows, :PANEL], out_ref, sem.at[i])
        for i, out_ref in enumerate((pa_ref, pb_ref))
    ]
    for copy in copies:
        copy.start()
    for copy in copies:
        copy.wait()


def panel_call(a):
    half = jax.ShapeDtypeStruct((a.shape[0] // 2, PANEL), F32)
    return pl.pallas_call(
        panel_kernel,
        in_specs=[pl.BlockSpec(memory_space=pltpu.HBM)],
        out_specs=[pl.BlockSpec(memory_space=pltpu.VMEM)] * 2,
        out_shape=[half, half],
        scratch_shapes=[pltpu.SemaphoreType.DMA((2,))],
        compiler_params=params(LARGE),
        name="panel",
    )(a)


def top_kernel(a_ref, lower_ref, upper_ref, rows_ref, sem):
    copy = pltpu.make_async_copy(a_ref.at[:PANEL], rows_ref, sem)
    copy.start()
    copy.wait()
    for half, out_ref in enumerate((lower_ref, upper_ref)):
        for i, piece in enumerate((0, 3, 1, 2)):
            for j, shard in enumerate((0, 3, 1, 2)):
                begin = (4 * half + piece) * WIDTH + shard * PANEL
                out_ref[4 * i + j] = rows_ref[:, begin : begin + PANEL]


def top_call(a):
    scratch = [pltpu.VMEM((PANEL, a.shape[1]), F32), pltpu.SemaphoreType.DMA]
    keys = dict(scratch=scratch, mib=LARGE, hbm=1, cost=cost_of(1.5))
    return small_call(top_kernel, [(16, PANEL, PANEL)] * 2, "top_rows", a, **keys)


def load_kernel(a_ref, blocks_ref, sem):
    copies = []
    for i in range(8):
        source = a_ref.at[:, i * WIDTH : (i + 1) * WIDTH]
        copies.append(pltpu.make_async_copy(source, blocks_ref.at[i], sem.at[i]))
        copies[i].start()
    for copy in copies:
        copy.wait()


def load_call(a):
    scratch = [pltpu.SemaphoreType.DMA((8,))]
    keys = dict(scratch=scratch, mib=36, hbm=1, cost=cost_of(5))
    return small_call(load_kernel, [(8, a.shape[0], WIDTH)], "load", a, **keys)[0]


def share_kernel(index, below, mine_ref, got_ref, keep_ref, send_ref):
    count = keep_ref.shape[0]
    held = place()[index] < below

    @pl.when(held)
    def _():
        keep_ref[...] = mine_ref[:count]
        send_ref[...] = mine_ref[count:]

    @pl.when(jnp.logical_not(held))
    def _():
        keep_ref[...] = got_ref[:count]
        send_ref[...] = got_ref[count:]


def share(index, below, mine, got):
    shape = (mine.shape[0] // 2, PANEL, PANEL)
    return small_call(functools.partial(share_kernel, index, below), [shape] * 2, "share", mine, got)


def pick_panel(pa, pb, a01, a03, a12, b01, b03, b32):
    x = lax.axis_index("col")
    upper = jnp.where(x == 0, pa[...], jnp.where(x == 1, a01[...], jnp.where(x == 2, a12[...], a03[...])))
    lower = jnp.where(x == 0, pb[...], jnp.where(x == 1, b01[...], jnp.where(x == 2, b32[...], b03[...])))
    return jnp.concatenate([upper, lower], axis=0)


def product_steps(flip, a_ref, lhs_ref, out_ref):
    half, a0, _ = place(flip)
    for i in range(4):
        high, low = split(a_ref[half * 4 + piece_at(a0, i)])
        both = dot3(lhs_ref[...], high)
        out_ref[i] = both[:PANEL] + both[PANEL:] + dot3(lhs_ref[:PANEL], low)


def product_first_kernel(a_ref, *refs):
    out_ref, lhs_ref, panel_ref, keep_ref, send_ref = refs[-5:]
    r = lax.axis_index("row")
    panel = pick_panel(*refs[:8])
    panel_ref[...] = panel
    flipped = panel.T
    high, low = split(flipped)
    lhs_ref[:PANEL] = high
    lhs_ref[PANEL:] = low
    gram = jnp.dot(flipped, panel, precision=HIGH, preferred_element_type=F32)
    top = jnp.where(r == 0, panel[:PANEL], 0.0)
    even = r & 1 == 0
    keep_ref[...] = jnp.where(even, gram, top)
    send_ref[...] = jnp.where(even, top, gram)
    product_steps(True, a_ref, lhs_ref, out_ref)


def product_second_kernel(a_ref, lhs_ref, out_ref):
    product_steps(False, a_ref, lhs_ref, out_ref)


def product_call(blocks, panels=None, lhs=None):
    rows = blocks.shape[1]
    w = ((4, PANEL, WIDTH), F32)
    if lhs is not None:
        return small_call(product_second_kernel, [w], "product_second", blocks, lhs, mib=24, cost=cost_of(1.5))[0]
    square = ((PANEL, PANEL), F32)
    shapes = [w, ((2 * PANEL, rows), BF16), ((rows, PANEL), F32), square, square]
    return small_call(product_first_kernel, shapes, "product_first", blocks, *panels, mib=24, cost=cost_of(2))


def spread(x, j):
    return jnp.broadcast_to(x[:, j : j + 1], (8, PANEL))


def tree_sum(terms):
    while len(terms) > 1:
        odd = [terms[-1]] if len(terms) % 2 else []
        terms = [p + q for p, q in zip(terms[::2], terms[1::2])] + odd
    return terms[0]


def chol_blocks(blocks):
    lane = lax.broadcasted_iota(jnp.int32, (8, PANEL), 1)
    sub = lax.broadcasted_iota(jnp.int32, (8, PANEL), 0)
    done = []
    for p in range(16):
        at = 8 * p
        rows = [jnp.broadcast_to(blocks[p][j : j + 1], (8, PANEL)) for j in range(8)]
        d = [[spread(rows[i], at + j) for j in range(i + 1)] for i in range(8)]
        t = [[None] * 8 for _ in range(8)]
        for k in range(8):
            r = lax.rsqrt(d[k][k])
            low = {i: d[i][k] * r for i in range(k + 1, 8)}
            for j in range(k):
                t[k][j] = t[k][j] * r
            t[k][k] = r
            for i in range(k + 1, 8):
                for j in range(k + 1, i + 1):
                    d[i][j] = d[i][j] - low[i] * low[j]
                for j in range(k + 1):
                    step = low[i] * t[k][j]
                    t[i][j] = -step if t[i][j] is None else t[i][j] - step
        inside = (lane >= at) & (lane < at + 8)
        rows = [jnp.where(inside, jnp.where(lane == at + j, 1.0, 0.0), rows[j]) for j in range(8)]
        y = []
        for i in range(8):
            terms = [t[i][j] * rows[j] for j in range(i + 1)]
            y.append(tree_sum(terms))
        out = y[0]
        for i in range(1, 8):
            out = jnp.where(sub == i, y[i], out)
        done.append(jnp.where(lane < at + 8, out, 0.0))
        if p == 15:
            break
        xs = []
        for k in range(8):
            terms = [t[i][k] * y[i] for i in range(k, 8)]
            xs.append(tree_sum(terms))
        for i in range(p + 1, 16):
            terms = [spread(blocks[i], at + k) * xs[k] for k in range(8)]
            blocks[i] = jnp.where(inside, 0.0, blocks[i]) - tree_sum(terms)
    return done


def inverse_blocks(blocks):
    lane = lax.broadcasted_iota(jnp.int32, (8, PANEL), 1)
    sub = lax.broadcasted_iota(jnp.int32, (8, PANEL), 0)
    for p in range(16):
        at = 8 * p
        rows = [jnp.broadcast_to(blocks[p][j : j + 1], (8, PANEL)) for j in range(8)]
        d = [[spread(rows[i], at + j) for j in range(8)] for i in range(8)]
        for k in range(8):
            r = 1.0 / d[k][k]
            row = [r if j == k else d[k][j] * r for j in range(8)]
            for i in range(8):
                if i != k:
                    m = d[i][k]
                    d[i] = [-(m * row[j]) if j == k else d[i][j] - m * row[j] for j in range(8)]
            d[k] = row
        inside = (lane >= at) & (lane < at + 8)
        rows = [jnp.where(inside, jnp.where(lane == at + j, 1.0, 0.0), rows[j]) for j in range(8)]
        xs = []
        for k in range(8):
            terms = [d[k][j] * rows[j] for j in range(8)]
            xs.append(tree_sum(terms))
        new = []
        for i in range(16):
            if i == p:
                out = xs[0]
                for k in range(1, 8):
                    out = jnp.where(sub == k, xs[k], out)
                new.append(out)
                continue
            terms = [spread(blocks[i], at + k) * xs[k] for k in range(8)]
            new.append(jnp.where(inside, 0.0, blocks[i]) - tree_sum(terms))
        blocks = new
    return blocks


def factor_kernel(g_ref, other_ref, w_ref, top_ref, got_ref, out_ref, z_ref):
    core, _, b0 = place()
    gram = jnp.where(core == 0, g_ref[...], other_ref[...])
    blocks = chol_blocks([gram[8 * i : 8 * i + 8] for i in range(16)])
    for i in range(16):
        out_ref[8 * i : 8 * i + 8] = blocks[i]
    top = jnp.where(b0 < 2, top_ref[0], got_ref[0])
    z_ref[...] = jnp.dot(out_ref[...], w_ref[...], precision=HIGH, preferred_element_type=F32) + top


def basis_kernel(linv_ref, g_ref, other_ref, panel_ref, out_ref):
    core, _, _ = place()
    top = jnp.where(core == 0, other_ref[...], g_ref[...])
    linv = linv_ref[...]
    nt = (((1,), (1,)), ((), ()))
    q_top = lax.dot_general(top, linv, nt, precision=HIGH, preferred_element_type=F32)
    lane = lax.broadcasted_iota(jnp.int32, (8, PANEL), 1)
    sub = lax.broadcasted_iota(jnp.int32, (8, PANEL), 0)
    blocks = [q_top[8 * i : 8 * i + 8] + jnp.where(lane == sub + 8 * i, 1.0, 0.0) for i in range(16)]
    kinv = jnp.concatenate(inverse_blocks(blocks), axis=0)
    tn = (((0,), (0,)), ((), ()))
    change = lax.dot_general(linv, kinv, tn, precision=HIGH, preferred_element_type=F32)
    basis = jnp.dot(panel_ref[...], change, precision=HIGH, preferred_element_type=F32)
    rest = basis[PANEL:]
    upper = basis[:PANEL] + jnp.where(lax.axis_index("row") == 0, kinv, 0.0)
    for part, begin, end in ((upper, 0, PANEL), (rest, PANEL, basis.shape[0])):
        high, low = split(part)
        out_ref[begin:end, 0:PANEL] = high
        out_ref[begin:end, PANEL : 2 * PANEL] = low
        out_ref[begin:end, 2 * PANEL :] = high


def cores_kernel(own_ref, got_ref, keep_ref, kept_ref, *out_refs):
    gram = keep_ref[...] + kept_ref[...]
    for i, out_ref in enumerate(out_refs):
        out_ref[:, :WIDTH] = own_ref[i] + got_ref[i]
        out_ref[:, WIDTH:] = gram


def first_kernel(e0, e1, e2, e3, *refs):
    out_refs, shards = refs[:4], refs[4]
    total = e0[...] + e1[...] + e2[...] + e3[...]
    for t in range(4):
        shards[t] = total[:, t * PANEL : (t + 1) * PANEL]
    _, _, b0 = place()
    for i, out_ref in enumerate(out_refs):
        out_ref[:, :PANEL] = shards[piece_at(b0, i)]
        out_ref[:, PANEL:] = total[:, WIDTH:]


def second_kernel(e0, e1, e2, e3, w_ref, g_ref):
    total = e0[...] + e1[...] + e2[...] + e3[...]
    w_ref[...] = total[:, :PANEL]
    g_ref[...] = total[:, PANEL:]


def assemble_kernel(z0, z1, z2, z3, out_ref):
    _, _, b0 = place()
    for i, z_ref in enumerate((z0, z1, z2, z3)):
        out_ref[piece_at(b0, i)] = z_ref[...]


def update_kernel(count, begin, a_ref, v_ref, *refs):
    z_refs = refs[: 2 * count]
    out_ref, token_ref, buffer, sem = refs[-4:]
    token_ref[...] = jnp.zeros_like(token_ref)
    writes = []
    for i in range(2 * count):
        half, a0, _ = place(i >= count)
        piece = half * 4 + piece_at(a0, begin + i % count)
        cols = pl.ds(pl.multiple_of(piece * WIDTH, WIDTH), WIDTH)
        parts = [split(z_refs[i][t]) for t in range(4)]
        high = jnp.concatenate([part[0] for part in parts], axis=1)
        low = jnp.concatenate([part[1] for part in parts], axis=1)
        stacked = jnp.concatenate([high, high, low], axis=0)
        buffer[i] = a_ref[piece] - dot3(v_ref[...], stacked)
        writes.append(pltpu.make_async_copy(buffer.at[i], out_ref.at[:, cols], sem.at[i]))
        writes[i].start()
    for write in writes:
        write.wait()


def update_call(blocks, v, mine, theirs, begin, out=None):
    _, rows, width = blocks.shape
    count = len(mine)
    vmem = pl.BlockSpec(memory_space=pltpu.VMEM)
    extra = () if out is None else (out,)
    return pl.pallas_call(
        functools.partial(update_kernel, count, begin),
        in_specs=[vmem] * (2 + 2 * count) + [pl.BlockSpec(memory_space=pltpu.HBM)] * len(extra),
        out_specs=[pl.BlockSpec(memory_space=pltpu.HBM), vmem],
        out_shape=[jax.ShapeDtypeStruct((rows, 8 * width), F32), jax.ShapeDtypeStruct((8, PANEL), F32)],
        input_output_aliases={2 + 2 * count: 0} if extra else {},
        scratch_shapes=[pltpu.VMEM((2 * count, rows, WIDTH), F32), pltpu.SemaphoreType.DMA((2 * count,))],
        compiler_params=params(28),
        name="update",
    )(blocks, v, *mine, *theirs, *extra)


def hold_kernel(*refs):
    pass


def hold(arrays, after):
    anywhere = pl.BlockSpec(memory_space=pl.ANY)
    return pl.pallas_call(
        hold_kernel,
        in_specs=[anywhere] * (len(arrays) + 1),
        out_specs=[anywhere] * len(arrays),
        out_shape=[jax.ShapeDtypeStruct(array.shape, array.dtype) for array in arrays],
        input_output_aliases={i: i for i in range(len(arrays))},
        compiler_params=params(2),
        name="hold",
    )(*arrays, after)


def diagonal(a):
    return a ^ 2


STEPS = (far, near, diagonal)


def on_device(a):
    rows = a.shape[0]
    pa, pb = panel_call(a)
    a01 = lax.ppermute(pa, "col", [(0, 1)])
    b03 = lax.ppermute(pb, "col", [(0, 3)])
    b01 = lax.ppermute(pb, "col", [(0, 1)])
    a03 = lax.ppermute(pa, "col", [(0, 3)])
    a12 = lax.ppermute(a01, "col", [(1, 2)])
    b32 = lax.ppermute(b03, "col", [(3, 2)])

    lower, upper = top_call(a)
    upper = lax.ppermute(upper, "row", [(0, 1)])
    top, send = share(0, 1, lower, upper)
    got = along(0, near, send, lambda a, b: a == 0 and b == 0)
    top, send = share(1, 1, top, got)
    got = along(0, far, send, lambda a, b: a < 2 and b == 0)
    top, send = share(1, 2, top, got)
    got = along(1, near, send, lambda a, b: b == 0)
    top, send = share(2, 1, top, got)
    got = along(1, far, send, lambda a, b: b < 2)

    blocks = load_call(a)
    w_other, lhs, panel, keep, send = product_call(blocks, panels=(pa, pb, a01, a03, a12, b01, b03, b32))
    w_got, kept = swap(w_other), swap(send)
    w_own = product_call(blocks, lhs=lhs)
    e = small_call(cores_kernel, [(PANEL, WIDTH + PANEL)] * 4, "sum_cores", w_own, w_got, keep, kept)
    e = [e[0]] + [along(0, step, e[i + 1]) for i, step in enumerate(STEPS)]
    scratch = [pltpu.VMEM((4, PANEL, PANEL), F32)]
    e = small_call(first_kernel, [(PANEL, 2 * PANEL)] * 4, "sum_first", *e, scratch=scratch)
    e = [e[0]] + [along(1, step, e[i + 1]) for i, step in enumerate(STEPS)]
    w, g = small_call(second_kernel, [(PANEL, PANEL)] * 2, "sum_second", *e)
    g_other = swap(g)
    linv, z = small_call(factor_kernel, [(PANEL, PANEL)] * 2, "factor", g, g_other, w, top, got, cost=cost_of(5))

    z = [z] + [along(1, step, z) for step in STEPS]
    (z,) = small_call(assemble_kernel, [(4, PANEL, PANEL)], "assemble", *z)
    got = [along(0, step, z) for step in STEPS]
    theirs = swap(z)
    shapes = [((rows, 3 * PANEL), BF16)]
    (v,) = small_call(basis_kernel, shapes, "basis", linv, g, g_other, panel, mib=16, cost=cost_of(7))
    out, token = update_call(blocks, v, [z], [theirs], 0)
    got = hold(got, token)
    theirs = [swap(piece) for piece in got]
    out, _ = update_call(blocks, v, got[:2], theirs[:2], 1, out)
    out, _ = update_call(blocks, v, got[2:], theirs[2:], 3, out)
    return out


def solution(mesh):
    return jax.shard_map(
        on_device, mesh=mesh, in_specs=(P("row", "col"),), out_specs=P("row", "col"), check_vma=False
    )
```

time: 845 us -> 93.1 us (0.11); the launches traced: 834 us -> 92.8 us
  waiting for transfers between devices: 334 us -> 15.3 us
  other arithmetic: 235 us -> 0 us
  local copies, waits for them, and re-layouts: 164 us -> 0 us
  between operations: 55.7 us -> 0.53 us
  matrix products: 45.8 us -> 0 us
  starting transfers between devices: 0.13 us -> 43.2 us
  Pallas kernels: 0 us -> 33.7 us
    psum x4 -> x0, waiting for transfers between devices: 334 us -> none  [the longest x2 138 us: broadcast(): return lax.psum(jnp.where(mine, x, jnp.zeros_like(x)), axis)]
    another operation x68 -> x0, other arithmetic: 84.7 us -> none  [the longest x30 20.3 us: eliminate(): jax.scipy.linalg.solve_triangular(upper_top.T, working[half:, :half].T, l...]
    slice x216 -> x0, local copies, waits for them, and re-layouts: 82.6 us -> none  [the longest x96 55.4 us: column_steps(): pivot_value = current[column, column]]
    scatter x224 -> x0, local copies, waits for them, and re-layouts: 76.9 us -> none  [the longest x112 45.8 us: column_steps(): current = current.at[column + 1:, column + 1:].set(trailing_block)]
    div x97 -> x0, other arithmetic: 69.7 us -> none  [the longest x96 68.8 us: column_steps(): multiplier = current[column + 1:, column] / pivot_value]
    mul x96 -> x0, other arithmetic: 68.5 us -> none  [column_steps(): multiplier[:, None] * current[column, column + 1:][None, :]]
    ppermute x0 -> x30, starting transfers between devices: none -> 43.2 us  [the longest x16 23.5 us: along(): return lax.ppermute(x, 'row', axis_pairs(which, step, keep))]
    dot_general x19 -> x0, matrix products: 34.3 us -> none  [the longest x1 14.6 us: on_device(): return matrix - jnp.dot(reflectors.T, coefficients, precision=high)]
  transfers between devices with their start and end apart: 4 -> 30, of which waited for: 4 -> 10; matrix products, arithmetic and copies ran while one was open for 1% -> 0% of each run, Pallas kernels for 0% -> 27%
where the time goes in v2:
time: 93.1 us; the launch traced here: 92.8 us
  starting transfers between devices  43.2 us (46%)
  Pallas kernels  33.7 us (36%)
  waiting for transfers between devices  15.3 us (16%)
    pallas_call x14, Pallas kernels, small_call(): pl.pallas_call(kernel, in_specs=[pl.BlockSpec(memory_space=pltpu.HBM)] *...  23.6 us
    ppermute x16, starting transfers between devices, along(): return lax.ppermute(x, 'row', axis_pairs(which, step, keep))  23.5 us
    ppermute x16, waiting for transfers between devices, along(): return lax.ppermute(x, 'row', axis_pairs(which, step, keep))  14.2 us
    pallas_call x3, Pallas kernels, update_call(): pl.pallas_call(functools.partial(update_kernel, count, begin), in_specs=[...  9.09 us
    ppermute x7, starting transfers between devices, swap(): return lax.ppermute(x, 'row', [(r, r ^ 1) for r in range(32)])  8.54 us
    ppermute x1, starting transfers between devices, on_device(): a01 = lax.ppermute(pa, 'col', [(0, 1)])  3.96 us
    ppermute x1, starting transfers between devices, on_device(): b03 = lax.ppermute(pb, 'col', [(0, 3)])  1.94 us
  transfers between devices with their start and end apart: 30, of which 10 were waited for; matrix products, arithmetic and copies ran while one was open for 0% of the time, Pallas kernels for 27%

profile of v2, /device:TPU:1, one launch (start us, length us, event | category | flops | bytes accessed | tf_op | source)
XLA Modules:
  0.0 92.8 jit_solution(12807782045502124725)
XLA Ops:
  1.0 4.0 %collective-permute-start = (f32[384,128]{1,0:T(8,128)S(1)}, f32[384,128]{1,0:T(8,128)S(1)}, u32[]{:S(2)}, u32[]{:S(2)}) collective-permute-start(f32[384,128]{1,0:T(8,128)S(1)} %get-tuple-element.41.refs_0_), channel_id=1, source_target_pairs={{0,1},{4,5},{8,9},{12,13},{16,17},{20,21},{24,25},{28,29},{32,33},... | collective-permute-start | bytes 589832 | tf_op jit(solution)/shard_map/ppermute | solution.py:436
  5.0 1.9 %collective-permute-start.4 = (f32[384,128]{1,0:T(8,128)S(1)}, f32[384,128]{1,0:T(8,128)S(1)}, u32[]{:S(2)}, u32[]{:S(2)}) collective-permute-start(f32[384,128]{1,0:T(8,128)S(1)} %get-tuple-element.42.refs_1_), channel_id=1, source_target_pairs={{0,3},{4,7},{8,11},{12,15},{16,19},{20,23},{24,27},{28,31},{32,35}... | collective-permute-start | bytes 589832 | tf_op jit(solution)/shard_map/ppermute | solution.py:437
  9.6 2.6 %top_rows.1 = (f32[16,128,128]{2,1,0:T(8,128)S(1)}, f32[16,128,128]{2,1,0:T(8,128)}) custom-call(f32[768,4096]{1,0:T(8,128)} %a_ref.5), custom_call_target="tpu_custom_call" | custom-call | flops 1724999936 | tf_op jit(solution)/shard_map/top_rows/pallas_call | solution.py:75
  14.9 4.7 %load.1.a_ref = f32[8,768,512]{2,1,0:T(8,128)S(1)} custom-call(f32[768,4096]{1,0:T(8,128)} %a_ref.5), custom_call_target="tpu_custom_call" | custom-call | flops 5750000128 | tf_op jit(solution)/shard_map/load/pallas_call | solution.py:75
  19.7 2.1 %product_first.1 = (f32[4,128,512]{2,1,0:T(8,128)S(1)}, bf16[256,768]{1,0:T(8,128)(2,1)S(1)}, f32[768,128]{1,0:T(8,128)S(1)}, f32[128,128]{1,0:T(8,128)S(1)}, f32[128,128]{1,0:T(8,128)S(1)}) custom-call(f32[8,768,512]{2,1,0:T(8,128)S(1)} %load.1.a_ref, f32[384,128]{1,0:T(8,128)S(1)} %get-tuple-element.41.refs_0_, f32[384,128]{1,0:T(8,128)S(1)} %get-tuple-element.42.refs_1_, ...), custom_call_target="tpu_custom_call" | custom-call | flops 2300000000 | tf_op jit(solution)/shard_map/product_first/pallas_call | solution.py:75
  23.2 2.8 %collective-permute-start.16 = (f32[8,128,128]{2,1,0:T(8,128)S(1)}, f32[8,128,128]{2,1,0:T(8,128)S(1)}, u32[]{:S(2)}, u32[]{:S(2)}) collective-permute-start(f32[8,128,128]{2,1,0:T(8,128)S(1)} %get-tuple-element.60), channel_id=1, source_target_pairs={{0,8},{4,36},{1,9},{5,37},{2,10},{6,38},{3,11},{7,39}} | collective-permute-start | bytes 1572872 | tf_op jit(solution)/shard_map/ppermute | solution.py:44
  26.0 1.7 %product_second.1.own_ref = f32[4,128,512]{2,1,0:T(8,128)S(1)} custom-call(f32[8,768,512]{2,1,0:T(8,128)S(1)} %load.1.a_ref, bf16[256,768]{1,0:T(8,128)(2,1)S(1)} %get-tuple-element.43.lhs_ref), custom_call_target="tpu_custom_call" | custom-call | flops 1724999936 | tf_op jit(solution)/shard_map/product_second/pallas_call | solution.py:75
  30.6 1.4 %collective-permute-done.16.got_ref = f32[8,128,128]{2,1,0:T(8,128)S(1)} collective-permute-done((f32[8,128,128]{2,1,0:T(8,128)S(1)}, f32[8,128,128]{2,1,0:T(8,128)S(1)}, u32[]{:S(2)}, u32[]{:S(2)}) %collective-permute-start.16) | collective-permute-done | bytes 524320 | tf_op jit(solution)/shard_map/ppermute | solution.py:44
  33.4 2.3 %collective-permute-done.10.e3 = f32[128,640]{1,0:T(8,128)S(1)} collective-permute-done((f32[128,640]{1,0:T(8,128)S(1)}, f32[128,640]{1,0:T(8,128)S(1)}, u32[]{:S(2)}, u32[]{:S(2)}) %collective-permute-start.10) | collective-permute-done | bytes 327712 | tf_op jit(solution)/shard_map/ppermute | solution.py:44
  35.7 3.5 %collective-permute-done.8.e1 = f32[128,640]{1,0:T(8,128)S(1)} collective-permute-done((f32[128,640]{1,0:T(8,128)S(1)}, f32[128,640]{1,0:T(8,128)S(1)}, u32[]{:S(2)}, u32[]{:S(2)}) %collective-permute-start.8) | collective-permute-done | bytes 327712 | tf_op jit(solution)/shard_map/ppermute | solution.py:44
  40.6 2.6 %collective-permute-start.13 = (f32[128,256]{1,0:T(8,128)S(1)}, f32[128,256]{1,0:T(8,128)S(1)}, u32[]{:S(2)}, u32[]{:S(2)}) collective-permute-start(f32[128,256]{1,0:T(8,128)S(1)} %get-tuple-element.54), channel_id=1, source_target_pairs={{0,64},{4,20},{8,72},{12,28},{16,80},{20,4},{24,88},{28,12},{32,96... | collective-permute-start | bytes 393224 | tf_op jit(solution)/shard_map/ppermute | solution.py:44
  44.6 2.4 %collective-permute-done.13.e3 = f32[128,256]{1,0:T(8,128)S(1)} collective-permute-done((f32[128,256]{1,0:T(8,128)S(1)}, f32[128,256]{1,0:T(8,128)S(1)}, u32[]{:S(2)}, u32[]{:S(2)}) %collective-permute-start.13) | collective-permute-done | bytes 131104 | tf_op jit(solution)/shard_map/ppermute | solution.py:44
  47.0 2.8 %collective-permute-start.14 = (f32[128,128]{1,0:T(8,128)S(1)}, f32[128,128]{1,0:T(8,128)S(1)}, u32[]{:S(2)}, u32[]{:S(2)}) collective-permute-start(f32[128,128]{1,0:T(8,128)S(1)} %get-tuple-element.55.g_ref), channel_id=1, source_target_pairs={{0,4},{4,0},{8,12},{12,8},{16,20},{20,16},{24,28},{28,24},{32,36},... | collective-permute-start | bytes 196616 | tf_op jit(solution)/shard_map/ppermute | solution.py:48
  49.9 3.2 %collective-permute-start.19 = (f32[1,128,128]{2,1,0:T(8,128)S(1)}, f32[1,128,128]{2,1,0:T(8,128)S(1)}, u32[]{:S(2)}, u32[]{:S(2)}) collective-permute-start(f32[1,128,128]{2,1,0:T(8,128)S(1)} %get-tuple-element.66), channel_id=1, source_target_pairs={{0,96},{4,28},{8,104},{12,20},{16,112},{24,120},{32,64},{36,60},{4... | collective-permute-start | bytes 196616 | tf_op jit(solution)/shard_map/ppermute | solution.py:44
  54.4 5.0 %factor.1 = (f32[128,128]{1,0:T(8,128)S(1)}, f32[128,128]{1,0:T(8,128)S(1)}) custom-call(f32[128,128]{1,0:T(8,128)S(1)} %get-tuple-element.55.g_ref, f32[128,128]{1,0:T(8,128)S(1)} %collective-permute-done.14.other_ref, f32[128,128]{1,0:T(8,128)S(1)} %get-tuple-element.56.w_ref, f32[1,128,128]{2,1,0:T(8,128)S(1)} %get-tuple-element.65.top_ref, ...), custom_call_target="tpu_custom_call" | custom-call | flops 5750000128 | tf_op jit(solution)/shard_map/factor/pallas_call | solution.py:75
  59.4 3.1 %collective-permute-start.20 = (f32[128,128]{1,0:T(8,128)S(1)}, f32[128,128]{1,0:T(8,128)S(1)}, u32[]{:S(2)}, u32[]{:S(2)}) collective-permute-start(f32[128,128]{1,0:T(8,128)S(1)} %get-tuple-element.69.z0), channel_id=1, source_target_pairs={{0,96},{4,28},{8,104},{12,20},{16,112},{20,12},{24,120},{28,4},{32... | collective-permute-start | bytes 196616 | tf_op jit(solution)/shard_map/ppermute | solution.py:44
  64.2 1.6 %collective-permute-done.21.z2 = f32[128,128]{1,0:T(8,128)S(1)} collective-permute-done((f32[128,128]{1,0:T(8,128)S(1)}, f32[128,128]{1,0:T(8,128)S(1)}, u32[]{:S(2)}, u32[]{:S(2)}) %collective-permute-start.21) | collective-permute-done | bytes 65568 | tf_op jit(solution)/shard_map/ppermute | solution.py:44
  67.2 2.8 %collective-permute-start.26 = (f32[4,128,128]{2,1,0:T(8,128)S(1)}, f32[4,128,128]{2,1,0:T(8,128)S(1)}, u32[]{:S(2)}, u32[]{:S(2)}) collective-permute-start(f32[4,128,128]{2,1,0:T(8,128)S(1)} %assemble.1.refs_0_), channel_id=1, source_target_pairs={{0,4},{4,0},{8,12},{12,8},{16,20},{20,16},{24,28},{28,24},{32,36},... | collective-permute-start | bytes 786440 | tf_op jit(solution)/shard_map/ppermute | solution.py:48
  70.0 1.6 %collective-permute-start.23 = (f32[4,128,128]{2,1,0:T(8,128)S(1)}, f32[4,128,128]{2,1,0:T(8,128)S(1)}, u32[]{:S(2)}, u32[]{:S(2)}) collective-permute-start(f32[4,128,128]{2,1,0:T(8,128)S(1)} %assemble.1.refs_0_), channel_id=1, source_target_pairs={{0,24},{4,100},{8,16},{12,108},{16,8},{20,116},{24,0},{28,124},{32... | collective-permute-start | bytes 786440 | tf_op jit(solution)/shard_map/ppermute | solution.py:44
  71.7 2.1 %collective-permute-start.25 = (f32[4,128,128]{2,1,0:T(8,128)S(1)}, f32[4,128,128]{2,1,0:T(8,128)S(1)}, u32[]{:S(2)}, u32[]{:S(2)}) collective-permute-start(f32[4,128,128]{2,1,0:T(8,128)S(1)} %assemble.1.refs_0_), channel_id=1, source_target_pairs={{0,16},{4,68},{8,24},{12,76},{16,0},{20,84},{24,8},{28,92},{32,48}... | collective-permute-start | bytes 786440 | tf_op jit(solution)/shard_map/ppermute | solution.py:44
  73.8 7.0 %basis.1.v_ref = bf16[768,384]{1,0:T(8,128)(2,1)S(1)} custom-call(f32[128,128]{1,0:T(8,128)S(1)} %get-tuple-element.67.linv_ref, f32[128,128]{1,0:T(8,128)S(1)} %get-tuple-element.55.g_ref, f32[128,128]{1,0:T(8,128)S(1)} %collective-permute-done.14.other_ref, f32[768,128]{1,0:T(8,128)S(1)} %get-tuple-element.68.panel_ref), custom_call_target="tpu_custom_call" | custom-call | flops 8049999872 | tf_op jit(solution)/shard_map/basis/pallas_call | solution.py:75
  80.9 2.3 %update.3 = (f32[768,4096]{1,0:T(8,128)}, f32[8,128]{1,0:T(8,128)S(1)}) custom-call(f32[8,768,512]{2,1,0:T(8,128)S(1)} %load.1.a_ref, bf16[768,384]{1,0:T(8,128)(2,1)S(1)} %basis.1.v_ref, f32[4,128,128]{2,1,0:T(8,128)S(1)} %assemble.1.refs_0_, f32[4,128,128]{2,1,0:T(8,128)S(1)} %collective-permute-done.26.refs_1_), custom_call_target="tpu_custom_call" | custom-call | tf_op jit(solution)/shard_map/update/pallas_call | solution.py:397
  85.8 3.9 %update.4 = (f32[768,4096]{1,0:T(8,128)}, f32[8,128]{1,0:T(8,128)}) custom-call(f32[8,768,512]{2,1,0:T(8,128)S(1)} %load.1.a_ref, bf16[768,384]{1,0:T(8,128)(2,1)S(1)} %basis.1.v_ref, f32[4,128,128]{2,1,0:T(8,128)S(1)} %get-tuple-element.72.refs_0_, f32[4,128,128]{2,1,0:T(8,128)S(1)} %get-tuple-element.73.refs_1_, ...), custom_call_target="tpu_custom_call", output_to_operand_aliasing={{0}: (6, {})} | custom-call | tf_op jit(solution)/shard_map/update/pallas_call | solution.py:397
  89.7 2.9 %update.5 = (f32[768,4096]{1,0:T(8,128)}, f32[8,128]{1,0:T(8,128)}) custom-call(f32[8,768,512]{2,1,0:T(8,128)S(1)} %load.1.a_ref, bf16[768,384]{1,0:T(8,128)(2,1)S(1)} %basis.1.v_ref, f32[4,128,128]{2,1,0:T(8,128)S(1)} %get-tuple-element.71.refs_0_, f32[4,128,128]{2,1,0:T(8,128)S(1)} %collective-permute-done.27.refs_1_, ...), custom_call_target="tpu_custom_call", output_to_operand_aliasing={{0}: (4, {})} | custom-call | tf_op jit(solution)/shard_map/update/pallas_call | solution.py:397
  (55 shorter events, 21.9 us)
Async XLA Ops:
  1.0 12.5 %collective-permute-start = (f32[384,128]{1,0:T(8,128)S(1)}, f32[384,128]{1,0:T(8,128)S(1)}, u32[]{:S(2)}, u32[]{:S(2)}) collective-permute-start(f32[384,128]{1,0:T(8,128)S(1)} %get-tuple-element.41.refs_0_), channel_id=1, source_target_pairs={{0,1},{4,5},{8,9},{12,13},{16,17},{20,21},{24,25},{28,29},{32,33},... | collective-permute-start | bytes 589832 | tf_op jit(solution)/shard_map/ppermute | solution.py:436
  5.0 9.2 %collective-permute-start.4 = (f32[384,128]{1,0:T(8,128)S(1)}, f32[384,128]{1,0:T(8,128)S(1)}, u32[]{:S(2)}, u32[]{:S(2)}) collective-permute-start(f32[384,128]{1,0:T(8,128)S(1)} %get-tuple-element.42.refs_1_), channel_id=1, source_target_pairs={{0,3},{4,7},{8,11},{12,15},{16,19},{20,23},{24,27},{28,31},{32,35}... | collective-permute-start | bytes 589832 | tf_op jit(solution)/shard_map/ppermute | solution.py:437
  7.0 12.7 %collective-permute-start.1 = (f32[384,128]{1,0:T(8,128)S(1)}, f32[384,128]{1,0:T(8,128)S(1)}, u32[]{:S(2)}, u32[]{:S(2)}) collective-permute-start(f32[384,128]{1,0:T(8,128)S(1)} %get-tuple-element.41.refs_0_), channel_id=1, source_target_pairs={{0,3},{4,7},{8,11},{12,15},{16,19},{20,23},{24,27},{28,31},{32,35}... | collective-permute-start | bytes 589832 | tf_op jit(solution)/shard_map/ppermute | solution.py:439
  8.3 11.4 %collective-permute-start.3 = (f32[384,128]{1,0:T(8,128)S(1)}, f32[384,128]{1,0:T(8,128)S(1)}, u32[]{:S(2)}, u32[]{:S(2)}) collective-permute-start(f32[384,128]{1,0:T(8,128)S(1)} %get-tuple-element.42.refs_1_), channel_id=1, source_target_pairs={{0,1},{4,5},{8,9},{12,13},{16,17},{20,21},{24,25},{28,29},{32,33},... | collective-permute-start | bytes 589832 | tf_op jit(solution)/shard_map/ppermute | solution.py:438
  12.2 10.9 %collective-permute-start.15 = (f32[16,128,128]{2,1,0:T(8,128)}, f32[16,128,128]{2,1,0:T(8,128)S(1)}, u32[]{:S(2)}, u32[]{:S(2)}) collective-permute-start(f32[16,128,128]{2,1,0:T(8,128)} %get-tuple-element.58), channel_id=1, source_target_pairs={{0,4},{1,5},{2,6},{3,7}} | collective-permute-start | bytes 3145736 | tf_op jit(solution)/shard_map/ppermute | solution.py:444
  13.5 6.2 %collective-permute-start.2 = (f32[384,128]{1,0:T(8,128)S(1)}, f32[384,128]{1,0:T(8,128)S(1)}, u32[]{:S(2)}, u32[]{:S(2)}) collective-permute-start(f32[384,128]{1,0:T(8,128)S(1)} %collective-permute-done.refs_2_), channel_id=1, source_target_pairs={{1,2},{5,6},{9,10},{13,14},{17,18},{21,22},{25,26},{29,30},{33,34}... | collective-permute-start | bytes 589832 | tf_op jit(solution)/shard_map/ppermute | solution.py:440
  14.2 5.5 %collective-permute-start.5 = (f32[384,128]{1,0:T(8,128)S(1)}, f32[384,128]{1,0:T(8,128)S(1)}, u32[]{:S(2)}, u32[]{:S(2)}) collective-permute-start(f32[384,128]{1,0:T(8,128)S(1)} %collective-permute-done.4.refs_6_), channel_id=1, source_target_pairs={{3,2},{7,6},{11,10},{15,14},{19,18},{23,22},{27,26},{31,30},{35,34... | collective-permute-start | bytes 589832 | tf_op jit(solution)/shard_map/ppermute | solution.py:441
  21.8 5.9 %collective-permute-start.6 = (f32[4,128,512]{2,1,0:T(8,128)S(1)}, f32[4,128,512]{2,1,0:T(8,128)S(1)}, u32[]{:S(2)}, u32[]{:S(2)}) collective-permute-start(f32[4,128,512]{2,1,0:T(8,128)S(1)} %get-tuple-element.44), channel_id=1, source_target_pairs={{0,4},{4,0},{8,12},{12,8},{16,20},{20,16},{24,28},{28,24},{32,36},... | collective-permute-start | bytes 3145736 | tf_op jit(solution)/shard_map/ppermute | solution.py:48
  23.2 8.9 %collective-permute-start.16 = (f32[8,128,128]{2,1,0:T(8,128)S(1)}, f32[8,128,128]{2,1,0:T(8,128)S(1)}, u32[]{:S(2)}, u32[]{:S(2)}) collective-permute-start(f32[8,128,128]{2,1,0:T(8,128)S(1)} %get-tuple-element.60), channel_id=1, source_target_pairs={{0,8},{4,36},{1,9},{5,37},{2,10},{6,38},{3,11},{7,39}} | collective-permute-start | bytes 1572872 | tf_op jit(solution)/shard_map/ppermute | solution.py:44
  27.9 7.8 %collective-permute-start.10 = (f32[128,640]{1,0:T(8,128)S(1)}, f32[128,640]{1,0:T(8,128)S(1)}, u32[]{:S(2)}, u32[]{:S(2)}) collective-permute-start(f32[128,640]{1,0:T(8,128)S(1)} %get-tuple-element.50), channel_id=1, source_target_pairs={{0,16},{4,68},{8,24},{12,76},{16,0},{20,84},{24,8},{28,92},{32,48}... | collective-permute-start | bytes 983048 | tf_op jit(solution)/shard_map/ppermute | solution.py:44
  28.7 10.5 %collective-permute-start.8 = (f32[128,640]{1,0:T(8,128)S(1)}, f32[128,640]{1,0:T(8,128)S(1)}, u32[]{:S(2)}, u32[]{:S(2)}) collective-permute-start(f32[128,640]{1,0:T(8,128)S(1)} %get-tuple-element.48), channel_id=1, source_target_pairs={{0,24},{4,100},{8,16},{12,108},{16,8},{20,116},{24,0},{28,124},{32... | collective-permute-start | bytes 983048 | tf_op jit(solution)/shard_map/ppermute | solution.py:44
  29.7 9.5 %collective-permute-start.9 = (f32[128,640]{1,0:T(8,128)S(1)}, f32[128,640]{1,0:T(8,128)S(1)}, u32[]{:S(2)}, u32[]{:S(2)}) collective-permute-start(f32[128,640]{1,0:T(8,128)S(1)} %get-tuple-element.49), channel_id=1, source_target_pairs={{0,8},{4,36},{8,0},{12,44},{16,24},{20,52},{24,16},{28,60},{32,40}... | collective-permute-start | bytes 983048 | tf_op jit(solution)/shard_map/ppermute | solution.py:44
  32.1 11.2 %collective-permute-start.17 = (f32[4,128,128]{2,1,0:T(8,128)S(1)}, f32[4,128,128]{2,1,0:T(8,128)S(1)}, u32[]{:S(2)}, u32[]{:S(2)}) collective-permute-start(f32[4,128,128]{2,1,0:T(8,128)S(1)} %get-tuple-element.62), channel_id=1, source_target_pairs={{0,24},{4,100},{8,16},{36,68},{1,25},{5,101},{9,17},{37,69},{2,26}... | collective-permute-start | bytes 786440 | tf_op jit(solution)/shard_map/ppermute | solution.py:44
  39.3 5.3 %collective-permute-start.11 = (f32[128,256]{1,0:T(8,128)S(1)}, f32[128,256]{1,0:T(8,128)S(1)}, u32[]{:S(2)}, u32[]{:S(2)}) collective-permute-start(f32[128,256]{1,0:T(8,128)S(1)} %get-tuple-element.52), channel_id=1, source_target_pairs={{0,96},{4,28},{8,104},{12,20},{16,112},{20,12},{24,120},{28,4},{32... | collective-permute-start | bytes 393224 | tf_op jit(solution)/shard_map/ppermute | solution.py:44
  40.6 6.3 %collective-permute-start.13 = (f32[128,256]{1,0:T(8,128)S(1)}, f32[128,256]{1,0:T(8,128)S(1)}, u32[]{:S(2)}, u32[]{:S(2)}) collective-permute-start(f32[128,256]{1,0:T(8,128)S(1)} %get-tuple-element.54), channel_id=1, source_target_pairs={{0,64},{4,20},{8,72},{12,28},{16,80},{20,4},{24,88},{28,12},{32,96... | collective-permute-start | bytes 393224 | tf_op jit(solution)/shard_map/ppermute | solution.py:44
  43.3 6.6 %collective-permute-start.18 = (f32[2,128,128]{2,1,0:T(8,128)S(1)}, f32[2,128,128]{2,1,0:T(8,128)S(1)}, u32[]{:S(2)}, u32[]{:S(2)}) collective-permute-start(f32[2,128,128]{2,1,0:T(8,128)S(1)} %get-tuple-element.64), channel_id=1, source_target_pairs={{0,32},{4,12},{8,40},{16,48},{24,56},{36,44},{68,76},{100,108},{1,... | collective-permute-start | bytes 393224 | tf_op jit(solution)/shard_map/ppermute | solution.py:44
  47.0 6.1 %collective-permute-start.14 = (f32[128,128]{1,0:T(8,128)S(1)}, f32[128,128]{1,0:T(8,128)S(1)}, u32[]{:S(2)}, u32[]{:S(2)}) collective-permute-start(f32[128,128]{1,0:T(8,128)S(1)} %get-tuple-element.55.g_ref), channel_id=1, source_target_pairs={{0,4},{4,0},{8,12},{12,8},{16,20},{20,16},{24,28},{28,24},{32,36},... | collective-permute-start | bytes 196616 | tf_op jit(solution)/shard_map/ppermute | solution.py:48
  59.4 4.7 %collective-permute-start.20 = (f32[128,128]{1,0:T(8,128)S(1)}, f32[128,128]{1,0:T(8,128)S(1)}, u32[]{:S(2)}, u32[]{:S(2)}) collective-permute-start(f32[128,128]{1,0:T(8,128)S(1)} %get-tuple-element.69.z0), channel_id=1, source_target_pairs={{0,96},{4,28},{8,104},{12,20},{16,112},{20,12},{24,120},{28,4},{32... | collective-permute-start | bytes 196616 | tf_op jit(solution)/shard_map/ppermute | solution.py:44
  62.5 4.6 %collective-permute-start.22 = (f32[128,128]{1,0:T(8,128)S(1)}, f32[128,128]{1,0:T(8,128)S(1)}, u32[]{:S(2)}, u32[]{:S(2)}) collective-permute-start(f32[128,128]{1,0:T(8,128)S(1)} %get-tuple-element.69.z0), channel_id=1, source_target_pairs={{0,64},{4,20},{8,72},{12,28},{16,80},{20,4},{24,88},{28,12},{32,96... | collective-permute-start | bytes 196616 | tf_op jit(solution)/shard_map/ppermute | solution.py:44
  67.2 13.7 %collective-permute-start.26 = (f32[4,128,128]{2,1,0:T(8,128)S(1)}, f32[4,128,128]{2,1,0:T(8,128)S(1)}, u32[]{:S(2)}, u32[]{:S(2)}) collective-permute-start(f32[4,128,128]{2,1,0:T(8,128)S(1)} %assemble.1.refs_0_), channel_id=1, source_target_pairs={{0,4},{4,0},{8,12},{12,8},{16,20},{20,16},{24,28},{28,24},{32,36},... | collective-permute-start | bytes 786440 | tf_op jit(solution)/shard_map/ppermute | solution.py:48
  70.0 13.2 %collective-permute-start.23 = (f32[4,128,128]{2,1,0:T(8,128)S(1)}, f32[4,128,128]{2,1,0:T(8,128)S(1)}, u32[]{:S(2)}, u32[]{:S(2)}) collective-permute-start(f32[4,128,128]{2,1,0:T(8,128)S(1)} %assemble.1.refs_0_), channel_id=1, source_target_pairs={{0,24},{4,100},{8,16},{12,108},{16,8},{20,116},{24,0},{28,124},{32... | collective-permute-start | bytes 786440 | tf_op jit(solution)/shard_map/ppermute | solution.py:44
  71.6 11.6 %collective-permute-start.24 = (f32[4,128,128]{2,1,0:T(8,128)S(1)}, f32[4,128,128]{2,1,0:T(8,128)S(1)}, u32[]{:S(2)}, u32[]{:S(2)}) collective-permute-start(f32[4,128,128]{2,1,0:T(8,128)S(1)} %assemble.1.refs_0_), channel_id=1, source_target_pairs={{0,8},{4,36},{8,0},{12,44},{16,24},{20,52},{24,16},{28,60},{32,40}... | collective-permute-start | bytes 786440 | tf_op jit(solution)/shard_map/ppermute | solution.py:44
  71.7 11.5 %collective-permute-start.25 = (f32[4,128,128]{2,1,0:T(8,128)S(1)}, f32[4,128,128]{2,1,0:T(8,128)S(1)}, u32[]{:S(2)}, u32[]{:S(2)}) collective-permute-start(f32[4,128,128]{2,1,0:T(8,128)S(1)} %assemble.1.refs_0_), channel_id=1, source_target_pairs={{0,16},{4,68},{8,24},{12,76},{16,0},{20,84},{24,8},{28,92},{32,48}... | collective-permute-start | bytes 786440 | tf_op jit(solution)/shard_map/ppermute | solution.py:44
  84.3 5.4 %collective-permute-start.27 = (f32[4,128,128]{2,1,0:T(8,128)S(1)}, f32[4,128,128]{2,1,0:T(8,128)S(1)}, u32[]{:S(2)}, u32[]{:S(2)}) collective-permute-start(f32[4,128,128]{2,1,0:T(8,128)S(1)} %get-tuple-element.71.refs_0_), channel_id=1, source_target_pairs={{0,4},{4,0},{8,12},{12,8},{16,20},{20,16},{24,28},{28,24},{32,36},... | collective-permute-start | bytes 786440 | tf_op jit(solution)/shard_map/ppermute | solution.py:48
  (6 other events, 17.2 us)

commit v3 on v2

--- a/solution.py
+++ b/solution.py
@@ -21,6 +21,13 @@
 
 def far(a):
     return 3 - a
+
+
+def diagonal(a):
+    return a ^ 2
+
+
+STEPS = (far, near, diagonal)
 
 
 def row_of(z, y, c):
@@ -119,24 +126,7 @@
     )(a)
 
 
-def top_kernel(a_ref, lower_ref, upper_ref, rows_ref, sem):
-    copy = pltpu.make_async_copy(a_ref.at[:PANEL], rows_ref, sem)
-    copy.start()
-    copy.wait()
-    for half, out_ref in enumerate((lower_ref, upper_ref)):
-        for i, piece in enumerate((0, 3, 1, 2)):
-            for j, shard in enumerate((0, 3, 1, 2)):
-                begin = (4 * half + piece) * WIDTH + shard * PANEL
-                out_ref[4 * i + j] = rows_ref[:, begin : begin + PANEL]
-
-
-def top_call(a):
-    scratch = [pltpu.VMEM((PANEL, a.shape[1]), F32), pltpu.SemaphoreType.DMA]
-    keys = dict(scratch=scratch, mib=LARGE, hbm=1, cost=cost_of(1.5))
-    return small_call(top_kernel, [(16, PANEL, PANEL)] * 2, "top_rows", a, **keys)
-
-
-def load_kernel(a_ref, blocks_ref, sem):
+def load_kernel(a_ref, blocks_ref, lower_ref, upper_ref, sem):
     copies = []
     for i in range(8):
         source = a_ref.at[:, i * WIDTH : (i + 1) * WIDTH]
@@ -145,31 +135,40 @@
     for copy in copies:
         copy.wait()
 
+    @pl.when(lax.axis_index("row") == 0)
+    def _():
+        for i, piece in enumerate((0, 3, 1, 2)):
+            lower_ref[i] = blocks_ref[piece, :PANEL]
+            upper_ref[i] = blocks_ref[piece + 4, :PANEL]
+
 
 def load_call(a):
     scratch = [pltpu.SemaphoreType.DMA((8,))]
     keys = dict(scratch=scratch, mib=36, hbm=1, cost=cost_of(5))
-    return small_call(load_kernel, [(8, a.shape[0], WIDTH)], "load", a, **keys)[0]
-
-
-def share_kernel(index, below, mine_ref, got_ref, keep_ref, send_ref):
-    count = keep_ref.shape[0]
-    held = place()[index] < below
-
-    @pl.when(held)
-    def _():
-        keep_ref[...] = mine_ref[:count]
-        send_ref[...] = mine_ref[count:]
-
-    @pl.when(jnp.logical_not(held))
-    def _():
-        keep_ref[...] = got_ref[:count]
-        send_ref[...] = got_ref[count:]
-
-
-def share(index, below, mine, got):
-    shape = (mine.shape[0] // 2, PANEL, PANEL)
-    return small_call(functools.partial(share_kernel, index, below), [shape] * 2, "share", mine, got)
+    top = (4, PANEL, WIDTH)
+    return small_call(load_kernel, [(8, a.shape[0], WIDTH), top, top], "load", a, **keys)
+
+
+def split_kernel(lower_ref, upper_ref, *out_refs):
+    core, _, _ = place()
+    for i, out_ref in enumerate(out_refs):
+
+        @pl.when(core == 0)
+        def _(i=i, out_ref=out_ref):
+            out_ref[...] = lower_ref[i]
+
+        @pl.when(core != 0)
+        def _(i=i, out_ref=out_ref):
+            out_ref[...] = upper_ref[i]
+
+
+def pick_kernel(mine_ref, far_ref, near_ref, diagonal_ref, out_ref):
+    _, a0, _ = place()
+    for at, ref in ((0, mine_ref), (far(0), far_ref), (near(0), near_ref), (diagonal(0), diagonal_ref)):
+
+        @pl.when(a0 == at)
+        def _(ref=ref):
+            out_ref[...] = ref[...]
 
 
 def pick_panel(pa, pb, a01, a03, a12, b01, b03, b32):
@@ -208,14 +207,14 @@
     product_steps(False, a_ref, lhs_ref, out_ref)
 
 
-def product_call(blocks, panels=None, lhs=None):
+def product_call(blocks, panels=None, lhs=None, after=()):
     rows = blocks.shape[1]
     w = ((4, PANEL, WIDTH), F32)
     if lhs is not None:
         return small_call(product_second_kernel, [w], "product_second", blocks, lhs, mib=24, cost=cost_of(1.5))[0]
     square = ((PANEL, PANEL), F32)
     shapes = [w, ((2 * PANEL, rows), BF16), ((rows, PANEL), F32), square, square]
-    return small_call(product_first_kernel, shapes, "product_first", blocks, *panels, mib=24, cost=cost_of(2))
+    return small_call(product_first_kernel, shapes, "product_first", blocks, *panels, mib=24, cost=cost_of(2), after=after)
 
 
 def spread(x, j):
@@ -307,14 +306,12 @@
     return blocks
 
 
-def factor_kernel(g_ref, other_ref, w_ref, top_ref, got_ref, out_ref, z_ref):
-    core, _, b0 = place()
+def factor_kernel(g_ref, other_ref, out_ref):
+    core, _, _ = place()
     gram = jnp.where(core == 0, g_ref[...], other_ref[...])
     blocks = chol_blocks([gram[8 * i : 8 * i + 8] for i in range(16)])
     for i in range(16):
         out_ref[8 * i : 8 * i + 8] = blocks[i]
-    top = jnp.where(b0 < 2, top_ref[0], got_ref[0])
-    z_ref[...] = jnp.dot(out_ref[...], w_ref[...], precision=HIGH, preferred_element_type=F32) + top
 
 
 def basis_kernel(linv_ref, g_ref, other_ref, panel_ref, out_ref):
@@ -346,41 +343,37 @@
         out_ref[:, WIDTH:] = gram
 
 
-def first_kernel(e0, e1, e2, e3, *refs):
-    out_refs, shards = refs[:4], refs[4]
+def first_kernel(e0, e1, e2, e3, after_ref, w_ref, g_ref):
     total = e0[...] + e1[...] + e2[...] + e3[...]
-    for t in range(4):
-        shards[t] = total[:, t * PANEL : (t + 1) * PANEL]
+    w_ref[...] = total[:, :WIDTH]
+    g_ref[...] = total[:, WIDTH:]
+
+
+def gram_kernel(g0, g1, g2, g3, *refs):
+    out_ref = refs[-1]
+    out_ref[...] = g0[...] + g1[...] + g2[...] + g3[...]
+
+
+def piece_kernel(linv_ref, w0, w1, w2, w3, mine_ref, far_ref, near_ref, diagonal_ref, out_ref):
     _, _, b0 = place()
-    for i, out_ref in enumerate(out_refs):
-        out_ref[:, :PANEL] = shards[piece_at(b0, i)]
-        out_ref[:, PANEL:] = total[:, WIDTH:]
-
-
-def second_kernel(e0, e1, e2, e3, w_ref, g_ref):
-    total = e0[...] + e1[...] + e2[...] + e3[...]
-    w_ref[...] = total[:, :PANEL]
-    g_ref[...] = total[:, PANEL:]
-
-
-def assemble_kernel(z0, z1, z2, z3, out_ref):
-    _, _, b0 = place()
-    for i, z_ref in enumerate((z0, z1, z2, z3)):
-        out_ref[piece_at(b0, i)] = z_ref[...]
+    w = w0[...] + w1[...] + w2[...] + w3[...]
+    z = jnp.dot(linv_ref[...], w, precision=HIGH, preferred_element_type=F32)
+    for at, ref in ((0, mine_ref), (far(0), far_ref), (near(0), near_ref), (diagonal(0), diagonal_ref)):
+
+        @pl.when(b0 == at)
+        def _(ref=ref):
+            out_ref[...] = z + ref[...]
 
 
 def update_kernel(count, begin, a_ref, v_ref, *refs):
     z_refs = refs[: 2 * count]
-    out_ref, token_ref, buffer, sem = refs[-4:]
-    token_ref[...] = jnp.zeros_like(token_ref)
+    out_ref, buffer, sem = refs[-3:]
     writes = []
     for i in range(2 * count):
         half, a0, _ = place(i >= count)
         piece = half * 4 + piece_at(a0, begin + i % count)
         cols = pl.ds(pl.multiple_of(piece * WIDTH, WIDTH), WIDTH)
-        parts = [split(z_refs[i][t]) for t in range(4)]
-        high = jnp.concatenate([part[0] for part in parts], axis=1)
-        low = jnp.concatenate([part[1] for part in parts], axis=1)
+        high, low = split(z_refs[i][...])
         stacked = jnp.concatenate([high, high, low], axis=0)
         buffer[i] = a_ref[piece] - dot3(v_ref[...], stacked)
         writes.append(pltpu.make_async_copy(buffer.at[i], out_ref.at[:, cols], sem.at[i]))
@@ -397,11 +390,11 @@
     return pl.pallas_call(
         functools.partial(update_kernel, count, begin),
         in_specs=[vmem] * (2 + 2 * count) + [pl.BlockSpec(memory_space=pltpu.HBM)] * len(extra),
-        out_specs=[pl.BlockSpec(memory_space=pltpu.HBM), vmem],
-        out_shape=[jax.ShapeDtypeStruct((rows, 8 * width), F32), jax.ShapeDtypeStruct((8, PANEL), F32)],
+        out_specs=pl.BlockSpec(memory_space=pltpu.HBM),
+        out_shape=jax.ShapeDtypeStruct((rows, 8 * width), F32),
         input_output_aliases={2 + 2 * count: 0} if extra else {},
         scratch_shapes=[pltpu.VMEM((2 * count, rows, WIDTH), F32), pltpu.SemaphoreType.DMA((2 * count,))],
-        compiler_params=params(28),
+        compiler_params=params(32),
         name="update",
     )(blocks, v, *mine, *theirs, *extra)
 
@@ -423,13 +416,6 @@
     )(*arrays, after)
 
 
-def diagonal(a):
-    return a ^ 2
-
-
-STEPS = (far, near, diagonal)
-
-
 def on_device(a):
     rows = a.shape[0]
     pa, pb = panel_call(a)
@@ -440,42 +426,34 @@
     a12 = lax.ppermute(a01, "col", [(1, 2)])
     b32 = lax.ppermute(b03, "col", [(3, 2)])
 
-    lower, upper = top_call(a)
+    blocks, lower, upper = load_call(a)
     upper = lax.ppermute(upper, "row", [(0, 1)])
-    top, send = share(0, 1, lower, upper)
-    got = along(0, near, send, lambda a, b: a == 0 and b == 0)
-    top, send = share(1, 1, top, got)
-    got = along(0, far, send, lambda a, b: a < 2 and b == 0)
-    top, send = share(1, 2, top, got)
-    got = along(1, near, send, lambda a, b: b == 0)
-    top, send = share(2, 1, top, got)
-    got = along(1, far, send, lambda a, b: b < 2)
-
-    blocks = load_call(a)
-    w_other, lhs, panel, keep, send = product_call(blocks, panels=(pa, pb, a01, a03, a12, b01, b03, b32))
-    w_got, kept = swap(w_other), swap(send)
+    tops = small_call(split_kernel, [(PANEL, WIDTH)] * 4, "split", lower, upper)
+    got = [along(0, step, tops[i + 1], lambda a, b: a == 0 and b == 0) for i, step in enumerate(STEPS)]
+    (top,) = small_call(pick_kernel, [(PANEL, WIDTH)], "pick", tops[0], *got)
+    tops = [top] + [along(1, step, top, lambda a, b: b == 0) for step in STEPS]
+
+    w_other, lhs, panel, keep, send_g = product_call(blocks, panels=(pa, pb, a01, a03, a12, b01, b03, b32))
+    w_got, kept = swap(w_other), swap(send_g)
     w_own = product_call(blocks, lhs=lhs)
     e = small_call(cores_kernel, [(PANEL, WIDTH + PANEL)] * 4, "sum_cores", w_own, w_got, keep, kept)
     e = [e[0]] + [along(0, step, e[i + 1]) for i, step in enumerate(STEPS)]
-    scratch = [pltpu.VMEM((4, PANEL, PANEL), F32)]
-    e = small_call(first_kernel, [(PANEL, 2 * PANEL)] * 4, "sum_first", *e, scratch=scratch)
-    e = [e[0]] + [along(1, step, e[i + 1]) for i, step in enumerate(STEPS)]
-    w, g = small_call(second_kernel, [(PANEL, PANEL)] * 2, "sum_second", *e)
+    w, g = small_call(first_kernel, [(PANEL, WIDTH), (PANEL, PANEL)], "sum_first", *e, after=(top,))
+    g = [g] + [along(1, step, g) for step in STEPS]
+    w = [w] + [along(1, step, w) for step in STEPS]
+    (g,) = small_call(gram_kernel, [(PANEL, PANEL)], "sum_gram", *g, after=tops[1:], cost=cost_of(3))
     g_other = swap(g)
-    linv, z = small_call(factor_kernel, [(PANEL, PANEL)] * 2, "factor", g, g_other, w, top, got, cost=cost_of(5))
-
-    z = [z] + [along(1, step, z) for step in STEPS]
-    (z,) = small_call(assemble_kernel, [(4, PANEL, PANEL)], "assemble", *z)
+    (linv,) = small_call(factor_kernel, [(PANEL, PANEL)], "factor", g, g_other, cost=cost_of(0.5))
+    (z,) = small_call(piece_kernel, [(PANEL, WIDTH)], "piece", linv, *w, *tops)
+
     got = [along(0, step, z) for step in STEPS]
     theirs = swap(z)
     shapes = [((rows, 3 * PANEL), BF16)]
     (v,) = small_call(basis_kernel, shapes, "basis", linv, g, g_other, panel, mib=16, cost=cost_of(7))
-    out, token = update_call(blocks, v, [z], [theirs], 0)
-    got = hold(got, token)
-    theirs = [swap(piece) for piece in got]
-    out, _ = update_call(blocks, v, got[:2], theirs[:2], 1, out)
-    out, _ = update_call(blocks, v, got[2:], theirs[2:], 3, out)
-    return out
+    got = hold(got, v)
+    others = [swap(piece) for piece in got]
+    out = update_call(blocks, v, [z], [theirs], 0)
+    return update_call(blocks, v, got, others, 1, out)
 
 
 def solution(mesh):

time: 93.1 us -> 84.9 us (0.912); the launches traced: 92.8 us -> 83.6 us
  Pallas kernels: 33.7 us -> 27.9 us
  waiting for transfers between devices: 15.3 us -> 12.1 us
    ppermute x16 -> x18, waiting for transfers between devices: 14.2 us -> 10.5 us  [along(): return lax.ppermute(x, 'row', axis_pairs(which, step, keep))]
    pallas_call x14 -> x11, Pallas kernels: 23.6 us -> 20.3 us  [small_call(): pl.pallas_call(kernel, in_specs=[pl.BlockSpec(memory_space=pltpu.HBM)] *...]
    pallas_call x3 -> x2, Pallas kernels: 9.09 us -> 6.55 us  [update_call(): pl.pallas_call(functools.partial(update_kernel, count, begin), in_specs=[...]
    ppermute x7, starting transfers between devices: 8.54 us -> 7.06 us  [swap(): return lax.ppermute(x, 'row', [(r, r ^ 1) for r in range(32)])]
    ppermute x16 -> x18, starting transfers between devices: 23.5 us -> 24.8 us  [along(): return lax.ppermute(x, 'row', axis_pairs(which, step, keep))]
  transfers between devices with their start and end apart: 30 -> 32, of which waited for: 10 -> 8; matrix products, arithmetic and copies ran while one was open for 0% -> 0% of each run, Pallas kernels for 27% -> 27%
where the time goes in v3:
time: 84.9 us; the launch traced here: 83.6 us
  starting transfers between devices  43 us (51%)
  Pallas kernels  27.9 us (33%)
  waiting for transfers between devices  12.1 us (14%)
    ppermute x18, starting transfers between devices, along(): return lax.ppermute(x, 'row', axis_pairs(which, step, keep))  24.8 us
    pallas_call x11, Pallas kernels, small_call(): pl.pallas_call(kernel, in_specs=[pl.BlockSpec(memory_space=pltpu.HBM)] *...  20.3 us
    ppermute x18, waiting for transfers between devices, along(): return lax.ppermute(x, 'row', axis_pairs(which, step, keep))  10.5 us
    ppermute x7, starting transfers between devices, swap(): return lax.ppermute(x, 'row', [(r, r ^ 1) for r in range(32)])  7.06 us
    pallas_call x2, Pallas kernels, update_call(): pl.pallas_call(functools.partial(update_kernel, count, begin), in_specs=[...  6.55 us
    ppermute x1, starting transfers between devices, on_device(): a01 = lax.ppermute(pa, 'col', [(0, 1)])  3.96 us
    ppermute x1, starting transfers between devices, on_device(): b03 = lax.ppermute(pb, 'col', [(0, 3)])  1.94 us
  transfers between devices with their start and end apart: 32, of which 8 were waited for; matrix products, arithmetic and copies ran while one was open for 0% of the time, Pallas kernels for 27%

profile of v3, /device:TPU:1, one launch (start us, length us, event | category | flops | bytes accessed | tf_op | source)
XLA Modules:
  0.0 83.6 jit_solution(6037564953263357616)
XLA Ops:
  1.0 4.0 %collective-permute-start = (f32[384,128]{1,0:T(8,128)S(1)}, f32[384,128]{1,0:T(8,128)S(1)}, u32[]{:S(2)}, u32[]{:S(2)}) collective-permute-start(f32[384,128]{1,0:T(8,128)S(1)} %get-tuple-element.29.refs_0_), channel_id=1, source_target_pairs={{0,1},{4,5},{8,9},{12,13},{16,17},{20,21},{24,25},{28,29},{32,33},... | collective-permute-start | bytes 589832 | tf_op jit(solution)/shard_map/ppermute | solution.py:422
  5.0 1.9 %collective-permute-start.4 = (f32[384,128]{1,0:T(8,128)S(1)}, f32[384,128]{1,0:T(8,128)S(1)}, u32[]{:S(2)}, u32[]{:S(2)}) collective-permute-start(f32[384,128]{1,0:T(8,128)S(1)} %get-tuple-element.30.refs_1_), channel_id=1, source_target_pairs={{0,3},{4,7},{8,11},{12,15},{16,19},{20,23},{24,27},{28,31},{32,35}... | collective-permute-start | bytes 589832 | tf_op jit(solution)/shard_map/ppermute | solution.py:423
  7.0 1.3 %collective-permute-start.1 = (f32[384,128]{1,0:T(8,128)S(1)}, f32[384,128]{1,0:T(8,128)S(1)}, u32[]{:S(2)}, u32[]{:S(2)}) collective-permute-start(f32[384,128]{1,0:T(8,128)S(1)} %get-tuple-element.29.refs_0_), channel_id=1, source_target_pairs={{0,3},{4,7},{8,11},{12,15},{16,19},{20,23},{24,27},{28,31},{32,35}... | collective-permute-start | bytes 589832 | tf_op jit(solution)/shard_map/ppermute | solution.py:425
  11.2 4.7 %load.1 = (f32[8,768,512]{2,1,0:T(8,128)S(1)}, f32[4,128,512]{2,1,0:T(8,128)S(1)}, f32[4,128,512]{2,1,0:T(8,128)S(1)}) custom-call(f32[768,4096]{1,0:T(8,128)} %a_ref.3), custom_call_target="tpu_custom_call" | custom-call | flops 5750000128 | tf_op jit(solution)/shard_map/load/pallas_call | solution.py:82
  17.3 1.8 %product_first.1 = (f32[4,128,512]{2,1,0:T(8,128)S(1)}, bf16[256,768]{1,0:T(8,128)(2,1)S(1)}, f32[768,128]{1,0:T(8,128)S(1)}, f32[128,128]{1,0:T(8,128)S(1)}, f32[128,128]{1,0:T(8,128)S(1)}) custom-call(f32[8,768,512]{2,1,0:T(8,128)S(1)} %get-tuple-element.28.a_ref, f32[384,128]{1,0:T(8,128)S(1)} %get-tuple-element.29.refs_0_, ...), custom_call_target="tpu_custom_call" | custom-call | flops 2300000000 | tf_op jit(solution)/shard_map/product_first/pallas_call | solution.py:82
  19.1 3.0 %collective-permute-start.6 = (f32[4,128,512]{2,1,0:T(8,128)S(1)}, f32[4,128,512]{2,1,0:T(8,128)S(1)}, u32[]{:S(2)}, u32[]{:S(2)}) collective-permute-start(f32[4,128,512]{2,1,0:T(8,128)S(1)} %get-tuple-element.32), channel_id=1, source_target_pairs={{0,4},{4,0},{8,12},{12,8},{16,20},{20,16},{24,28},{28,24},{32,36},... | collective-permute-start | bytes 3145736 | tf_op jit(solution)/shard_map/ppermute | solution.py:55
  22.3 4.9 %collective-permute-start.12 = (f32[128,512]{1,0:T(8,128)S(1)}, f32[128,512]{1,0:T(8,128)S(1)}, u32[]{:S(2)}, u32[]{:S(2)}) collective-permute-start(f32[128,512]{1,0:T(8,128)S(1)} %get-tuple-element.42), channel_id=1, source_target_pairs={{0,24},{4,100},{1,25},{5,101},{2,26},{6,102},{3,27},{7,103}} | collective-permute-start | bytes 786440 | tf_op jit(solution)/shard_map/ppermute | solution.py:51
  27.2 1.4 %product_second.1.own_ref = f32[4,128,512]{2,1,0:T(8,128)S(1)} custom-call(f32[8,768,512]{2,1,0:T(8,128)S(1)} %get-tuple-element.28.a_ref, bf16[256,768]{1,0:T(8,128)(2,1)S(1)} %get-tuple-element.31.lhs_ref), custom_call_target="tpu_custom_call" | custom-call | flops 1724999936 | tf_op jit(solution)/shard_map/product_second/pallas_call | solution.py:82
  28.6 1.3 %collective-permute-start.13 = (f32[128,512]{1,0:T(8,128)S(1)}, f32[128,512]{1,0:T(8,128)S(1)}, u32[]{:S(2)}, u32[]{:S(2)}) collective-permute-start(f32[128,512]{1,0:T(8,128)S(1)} %get-tuple-element.43), channel_id=1, source_target_pairs={{0,8},{4,36},{1,9},{5,37},{2,10},{6,38},{3,11},{7,39}} | collective-permute-start | bytes 786440 | tf_op jit(solution)/shard_map/ppermute | solution.py:51
  30.2 1.3 %collective-permute-start.14 = (f32[128,512]{1,0:T(8,128)S(1)}, f32[128,512]{1,0:T(8,128)S(1)}, u32[]{:S(2)}, u32[]{:S(2)}) collective-permute-start(f32[128,512]{1,0:T(8,128)S(1)} %get-tuple-element.44), channel_id=1, source_target_pairs={{0,16},{4,68},{1,17},{5,69},{2,18},{6,70},{3,19},{7,71}} | collective-permute-start | bytes 786440 | tf_op jit(solution)/shard_map/ppermute | solution.py:51
  31.6 3.2 %collective-permute-start.10 = (f32[128,640]{1,0:T(8,128)S(1)}, f32[128,640]{1,0:T(8,128)S(1)}, u32[]{:S(2)}, u32[]{:S(2)}) collective-permute-start(f32[128,640]{1,0:T(8,128)S(1)} %get-tuple-element.38), channel_id=1, source_target_pairs={{0,16},{4,68},{8,24},{12,76},{16,0},{20,84},{24,8},{28,92},{32,48}... | collective-permute-start | bytes 983048 | tf_op jit(solution)/shard_map/ppermute | solution.py:51
  36.1 1.3 %collective-permute-start.20 = (f32[128,512]{1,0:T(8,128)S(1)}, f32[128,512]{1,0:T(8,128)S(1)}, u32[]{:S(2)}, u32[]{:S(2)}) collective-permute-start(f32[128,512]{1,0:T(8,128)S(1)} %pick.1.after_ref.mine_ref), channel_id=1, source_target_pairs={{0,64},{4,20},{8,72},{16,80},{24,88},{36,52},{68,84},{100,116},{1,... | collective-permute-start | bytes 786440 | tf_op jit(solution)/shard_map/ppermute | solution.py:51
  37.4 1.3 %collective-permute-start.19 = (f32[128,512]{1,0:T(8,128)S(1)}, f32[128,512]{1,0:T(8,128)S(1)}, u32[]{:S(2)}, u32[]{:S(2)}) collective-permute-start(f32[128,512]{1,0:T(8,128)S(1)} %pick.1.after_ref.mine_ref), channel_id=1, source_target_pairs={{0,32},{4,12},{8,40},{16,48},{24,56},{36,44},{68,76},{100,108},{1,... | collective-permute-start | bytes 786440 | tf_op jit(solution)/shard_map/ppermute | solution.py:51
  38.7 1.3 %collective-permute-start.18 = (f32[128,512]{1,0:T(8,128)S(1)}, f32[128,512]{1,0:T(8,128)S(1)}, u32[]{:S(2)}, u32[]{:S(2)}) collective-permute-start(f32[128,512]{1,0:T(8,128)S(1)} %pick.1.after_ref.mine_ref), channel_id=1, source_target_pairs={{0,96},{4,28},{8,104},{16,112},{24,120},{36,60},{68,92},{100,124},... | collective-permute-start | bytes 786440 | tf_op jit(solution)/shard_map/ppermute | solution.py:51
  40.7 7.0 %collective-permute-done.10.e3 = f32[128,640]{1,0:T(8,128)S(1)} collective-permute-done((f32[128,640]{1,0:T(8,128)S(1)}, f32[128,640]{1,0:T(8,128)S(1)}, u32[]{:S(2)}, u32[]{:S(2)}) %collective-permute-start.10) | collective-permute-done | bytes 327712 | tf_op jit(solution)/shard_map/ppermute | solution.py:51
  48.0 3.1 %collective-permute-start.15 = (f32[128,128]{1,0:T(8,128)S(1)}, f32[128,128]{1,0:T(8,128)S(1)}, u32[]{:S(2)}, u32[]{:S(2)}) collective-permute-start(f32[128,128]{1,0:T(8,128)S(1)} %get-tuple-element.45.g0), channel_id=1, source_target_pairs={{0,96},{4,28},{8,104},{12,20},{16,112},{20,12},{24,120},{28,4},{32... | collective-permute-start | bytes 196616 | tf_op jit(solution)/shard_map/ppermute | solution.py:51
  52.6 1.9 %collective-permute-start.22 = (f32[128,512]{1,0:T(8,128)S(1)}, f32[128,512]{1,0:T(8,128)S(1)}, u32[]{:S(2)}, u32[]{:S(2)}) collective-permute-start(f32[128,512]{1,0:T(8,128)S(1)} %get-tuple-element.47.w0), channel_id=1, source_target_pairs={{0,96},{4,28},{8,104},{12,20},{16,112},{20,12},{24,120},{28,4},{32... | collective-permute-start | bytes 786440 | tf_op jit(solution)/shard_map/ppermute | solution.py:51
  55.2 2.1 %collective-permute-start.21 = (f32[128,128]{1,0:T(8,128)S(1)}, f32[128,128]{1,0:T(8,128)S(1)}, u32[]{:S(2)}, u32[]{:S(2)}) collective-permute-start(f32[128,128]{1,0:T(8,128)S(1)} %sum_gram.1.g_ref), channel_id=1, source_target_pairs={{0,4},{4,0},{8,12},{12,8},{16,20},{20,16},{24,28},{28,24},{32,36},... | collective-permute-start | bytes 196616 | tf_op jit(solution)/shard_map/ppermute | solution.py:55
  58.2 4.5 %factor.1.linv_ref = f32[128,128]{1,0:T(8,128)S(1)} custom-call(f32[128,128]{1,0:T(8,128)S(1)} %sum_gram.1.g_ref, f32[128,128]{1,0:T(8,128)S(1)} %collective-permute-done.21.other_ref), custom_call_target="tpu_custom_call" | custom-call | flops 575000000 | tf_op jit(solution)/shard_map/factor/pallas_call | solution.py:82
  63.2 2.0 %collective-permute-start.27 = (f32[128,512]{1,0:T(8,128)S(1)}, f32[128,512]{1,0:T(8,128)S(1)}, u32[]{:S(2)}, u32[]{:S(2)}) collective-permute-start(f32[128,512]{1,0:T(8,128)S(1)} %piece.1.refs_0_), channel_id=1, source_target_pairs={{0,16},{4,68},{8,24},{12,76},{16,0},{20,84},{24,8},{28,92},{32,48}... | collective-permute-start | bytes 786440 | tf_op jit(solution)/shard_map/ppermute | solution.py:51
  65.2 2.2 %collective-permute-start.26 = (f32[128,512]{1,0:T(8,128)S(1)}, f32[128,512]{1,0:T(8,128)S(1)}, u32[]{:S(2)}, u32[]{:S(2)}) collective-permute-start(f32[128,512]{1,0:T(8,128)S(1)} %piece.1.refs_0_), channel_id=1, source_target_pairs={{0,8},{4,36},{8,0},{12,44},{16,24},{20,52},{24,16},{28,60},{32,40}... | collective-permute-start | bytes 786440 | tf_op jit(solution)/shard_map/ppermute | solution.py:51
  67.4 7.0 %basis.1.refs_3_.v_ref = bf16[768,384]{1,0:T(8,128)(2,1)S(1)} custom-call(f32[128,128]{1,0:T(8,128)S(1)} %factor.1.linv_ref, f32[128,128]{1,0:T(8,128)S(1)} %sum_gram.1.g_ref, f32[128,128]{1,0:T(8,128)S(1)} %collective-permute-done.21.other_ref, f32[768,128]{1,0:T(8,128)S(1)} %get-tuple-element.46.panel_ref), custom_call_target="tpu_custom_call" | custom-call | flops 8049999872 | tf_op jit(solution)/shard_map/basis/pallas_call | solution.py:82
  76.9 2.3 %update.2.refs_6_ = f32[768,4096]{1,0:T(8,128)} custom-call(f32[8,768,512]{2,1,0:T(8,128)S(1)} %get-tuple-element.28.a_ref, bf16[768,384]{1,0:T(8,128)(2,1)S(1)} %basis.1.refs_3_.v_ref, f32[128,512]{1,0:T(8,128)S(1)} %piece.1.refs_0_, f32[128,512]{1,0:T(8,128)S(1)} %collective-permute-done.31.refs_1_), custom_call_target="tpu_custom_call" | custom-call | tf_op jit(solution)/shard_map/update/pallas_call | solution.py:390
  79.2 4.3 %update.3 = f32[768,4096]{1,0:T(8,128)} custom-call(f32[8,768,512]{2,1,0:T(8,128)S(1)} %get-tuple-element.28.a_ref, bf16[768,384]{1,0:T(8,128)(2,1)S(1)} %basis.1.refs_3_.v_ref, f32[128,512]{1,0:T(8,128)S(1)} %get-tuple-element.48.refs_0_, f32[128,512]{1,0:T(8,128)S(1)} %get-tuple-element.49.refs_1_, ...), custom_call_target="tpu_custom_call", output_to_operand_aliasing={{}: (8, {})} | custom-call | tf_op jit(solution)/shard_map/update/pallas_call | solution.py:390
  (55 shorter events, 13.8 us)
Async XLA Ops:
  1.0 8.5 %collective-permute-start = (f32[384,128]{1,0:T(8,128)S(1)}, f32[384,128]{1,0:T(8,128)S(1)}, u32[]{:S(2)}, u32[]{:S(2)}) collective-permute-start(f32[384,128]{1,0:T(8,128)S(1)} %get-tuple-element.29.refs_0_), channel_id=1, source_target_pairs={{0,1},{4,5},{8,9},{12,13},{16,17},{20,21},{24,25},{28,29},{32,33},... | collective-permute-start | bytes 589832 | tf_op jit(solution)/shard_map/ppermute | solution.py:422
  7.0 10.3 %collective-permute-start.1 = (f32[384,128]{1,0:T(8,128)S(1)}, f32[384,128]{1,0:T(8,128)S(1)}, u32[]{:S(2)}, u32[]{:S(2)}) collective-permute-start(f32[384,128]{1,0:T(8,128)S(1)} %get-tuple-element.29.refs_0_), channel_id=1, source_target_pairs={{0,3},{4,7},{8,11},{12,15},{16,19},{20,23},{24,27},{28,31},{32,35}... | collective-permute-start | bytes 589832 | tf_op jit(solution)/shard_map/ppermute | solution.py:425
  8.3 9.0 %collective-permute-start.3 = (f32[384,128]{1,0:T(8,128)S(1)}, f32[384,128]{1,0:T(8,128)S(1)}, u32[]{:S(2)}, u32[]{:S(2)}) collective-permute-start(f32[384,128]{1,0:T(8,128)S(1)} %get-tuple-element.30.refs_1_), channel_id=1, source_target_pairs={{0,1},{4,5},{8,9},{12,13},{16,17},{20,21},{24,25},{28,29},{32,33},... | collective-permute-start | bytes 589832 | tf_op jit(solution)/shard_map/ppermute | solution.py:424
  9.6 7.7 %collective-permute-start.2 = (f32[384,128]{1,0:T(8,128)S(1)}, f32[384,128]{1,0:T(8,128)S(1)}, u32[]{:S(2)}, u32[]{:S(2)}) collective-permute-start(f32[384,128]{1,0:T(8,128)S(1)} %collective-permute-done.refs_2_), channel_id=1, source_target_pairs={{1,2},{5,6},{9,10},{13,14},{17,18},{21,22},{25,26},{29,30},{33,34}... | collective-permute-start | bytes 589832 | tf_op jit(solution)/shard_map/ppermute | solution.py:426
  10.5 6.8 %collective-permute-start.5 = (f32[384,128]{1,0:T(8,128)S(1)}, f32[384,128]{1,0:T(8,128)S(1)}, u32[]{:S(2)}, u32[]{:S(2)}) collective-permute-start(f32[384,128]{1,0:T(8,128)S(1)} %collective-permute-done.4.refs_6_), channel_id=1, source_target_pairs={{3,2},{7,6},{11,10},{15,14},{19,18},{23,22},{27,26},{31,30},{35,34... | collective-permute-start | bytes 589832 | tf_op jit(solution)/shard_map/ppermute | solution.py:427
  15.9 6.3 %collective-permute-start.11 = (f32[4,128,512]{2,1,0:T(8,128)S(1)}, f32[4,128,512]{2,1,0:T(8,128)S(1)}, u32[]{:S(2)}, u32[]{:S(2)}) collective-permute-start(f32[4,128,512]{2,1,0:T(8,128)S(1)} %get-tuple-element.40), channel_id=1, source_target_pairs={{0,4},{1,5},{2,6},{3,7}} | collective-permute-start | bytes 3145736 | tf_op jit(solution)/shard_map/ppermute | solution.py:430
  19.1 10.9 %collective-permute-start.6 = (f32[4,128,512]{2,1,0:T(8,128)S(1)}, f32[4,128,512]{2,1,0:T(8,128)S(1)}, u32[]{:S(2)}, u32[]{:S(2)}) collective-permute-start(f32[4,128,512]{2,1,0:T(8,128)S(1)} %get-tuple-element.32), channel_id=1, source_target_pairs={{0,4},{4,0},{8,12},{12,8},{16,20},{20,16},{24,28},{28,24},{32,36},... | collective-permute-start | bytes 3145736 | tf_op jit(solution)/shard_map/ppermute | solution.py:55
  22.1 7.9 %collective-permute-start.7 = (f32[128,128]{1,0:T(8,128)S(1)}, f32[128,128]{1,0:T(8,128)S(1)}, u32[]{:S(2)}, u32[]{:S(2)}) collective-permute-start(f32[128,128]{1,0:T(8,128)S(1)} %get-tuple-element.34), channel_id=1, source_target_pairs={{0,4},{4,0},{8,12},{12,8},{16,20},{20,16},{24,28},{28,24},{32,36},... | collective-permute-start | bytes 196616 | tf_op jit(solution)/shard_map/ppermute | solution.py:55
  22.3 9.3 %collective-permute-start.12 = (f32[128,512]{1,0:T(8,128)S(1)}, f32[128,512]{1,0:T(8,128)S(1)}, u32[]{:S(2)}, u32[]{:S(2)}) collective-permute-start(f32[128,512]{1,0:T(8,128)S(1)} %get-tuple-element.42), channel_id=1, source_target_pairs={{0,24},{4,100},{1,25},{5,101},{2,26},{6,102},{3,27},{7,103}} | collective-permute-start | bytes 786440 | tf_op jit(solution)/shard_map/ppermute | solution.py:51
  28.6 6.2 %collective-permute-start.13 = (f32[128,512]{1,0:T(8,128)S(1)}, f32[128,512]{1,0:T(8,128)S(1)}, u32[]{:S(2)}, u32[]{:S(2)}) collective-permute-start(f32[128,512]{1,0:T(8,128)S(1)} %get-tuple-element.43), channel_id=1, source_target_pairs={{0,8},{4,36},{1,9},{5,37},{2,10},{6,38},{3,11},{7,39}} | collective-permute-start | bytes 786440 | tf_op jit(solution)/shard_map/ppermute | solution.py:51
  30.1 8.6 %collective-permute-start.8 = (f32[128,640]{1,0:T(8,128)S(1)}, f32[128,640]{1,0:T(8,128)S(1)}, u32[]{:S(2)}, u32[]{:S(2)}) collective-permute-start(f32[128,640]{1,0:T(8,128)S(1)} %get-tuple-element.36), channel_id=1, source_target_pairs={{0,24},{4,100},{8,16},{12,108},{16,8},{20,116},{24,0},{28,124},{32... | collective-permute-start | bytes 983048 | tf_op jit(solution)/shard_map/ppermute | solution.py:51
  31.5 9.2 %collective-permute-start.9 = (f32[128,640]{1,0:T(8,128)S(1)}, f32[128,640]{1,0:T(8,128)S(1)}, u32[]{:S(2)}, u32[]{:S(2)}) collective-permute-start(f32[128,640]{1,0:T(8,128)S(1)} %get-tuple-element.37), channel_id=1, source_target_pairs={{0,8},{4,36},{8,0},{12,44},{16,24},{20,52},{24,16},{28,60},{32,40}... | collective-permute-start | bytes 983048 | tf_op jit(solution)/shard_map/ppermute | solution.py:51
  31.6 16.1 %collective-permute-start.10 = (f32[128,640]{1,0:T(8,128)S(1)}, f32[128,640]{1,0:T(8,128)S(1)}, u32[]{:S(2)}, u32[]{:S(2)}) collective-permute-start(f32[128,640]{1,0:T(8,128)S(1)} %get-tuple-element.38), channel_id=1, source_target_pairs={{0,16},{4,68},{8,24},{12,76},{16,0},{20,84},{24,8},{28,92},{32,48}... | collective-permute-start | bytes 983048 | tf_op jit(solution)/shard_map/ppermute | solution.py:51
  36.1 11.9 %collective-permute-start.20 = (f32[128,512]{1,0:T(8,128)S(1)}, f32[128,512]{1,0:T(8,128)S(1)}, u32[]{:S(2)}, u32[]{:S(2)}) collective-permute-start(f32[128,512]{1,0:T(8,128)S(1)} %pick.1.after_ref.mine_ref), channel_id=1, source_target_pairs={{0,64},{4,20},{8,72},{16,80},{24,88},{36,52},{68,84},{100,116},{1,... | collective-permute-start | bytes 786440 | tf_op jit(solution)/shard_map/ppermute | solution.py:51
  37.4 13.8 %collective-permute-start.19 = (f32[128,512]{1,0:T(8,128)S(1)}, f32[128,512]{1,0:T(8,128)S(1)}, u32[]{:S(2)}, u32[]{:S(2)}) collective-permute-start(f32[128,512]{1,0:T(8,128)S(1)} %pick.1.after_ref.mine_ref), channel_id=1, source_target_pairs={{0,32},{4,12},{8,40},{16,48},{24,56},{36,44},{68,76},{100,108},{1,... | collective-permute-start | bytes 786440 | tf_op jit(solution)/shard_map/ppermute | solution.py:51
  38.7 12.5 %collective-permute-start.18 = (f32[128,512]{1,0:T(8,128)S(1)}, f32[128,512]{1,0:T(8,128)S(1)}, u32[]{:S(2)}, u32[]{:S(2)}) collective-permute-start(f32[128,512]{1,0:T(8,128)S(1)} %pick.1.after_ref.mine_ref), channel_id=1, source_target_pairs={{0,96},{4,28},{8,104},{16,112},{24,120},{36,60},{68,92},{100,124},... | collective-permute-start | bytes 786440 | tf_op jit(solution)/shard_map/ppermute | solution.py:51
  47.9 6.5 %collective-permute-start.16 = (f32[128,128]{1,0:T(8,128)S(1)}, f32[128,128]{1,0:T(8,128)S(1)}, u32[]{:S(2)}, u32[]{:S(2)}) collective-permute-start(f32[128,128]{1,0:T(8,128)S(1)} %get-tuple-element.45.g0), channel_id=1, source_target_pairs={{0,32},{4,12},{8,40},{12,4},{16,48},{20,28},{24,56},{28,20},{32,0}... | collective-permute-start | bytes 196616 | tf_op jit(solution)/shard_map/ppermute | solution.py:51
  48.0 7.2 %collective-permute-start.15 = (f32[128,128]{1,0:T(8,128)S(1)}, f32[128,128]{1,0:T(8,128)S(1)}, u32[]{:S(2)}, u32[]{:S(2)}) collective-permute-start(f32[128,128]{1,0:T(8,128)S(1)} %get-tuple-element.45.g0), channel_id=1, source_target_pairs={{0,96},{4,28},{8,104},{12,20},{16,112},{20,12},{24,120},{28,4},{32... | collective-permute-start | bytes 196616 | tf_op jit(solution)/shard_map/ppermute | solution.py:51
  51.2 11.6 %collective-permute-start.24 = (f32[128,512]{1,0:T(8,128)S(1)}, f32[128,512]{1,0:T(8,128)S(1)}, u32[]{:S(2)}, u32[]{:S(2)}) collective-permute-start(f32[128,512]{1,0:T(8,128)S(1)} %get-tuple-element.47.w0), channel_id=1, source_target_pairs={{0,64},{4,20},{8,72},{12,28},{16,80},{20,4},{24,88},{28,12},{32,96... | collective-permute-start | bytes 786440 | tf_op jit(solution)/shard_map/ppermute | solution.py:51
  51.3 11.5 %collective-permute-start.23 = (f32[128,512]{1,0:T(8,128)S(1)}, f32[128,512]{1,0:T(8,128)S(1)}, u32[]{:S(2)}, u32[]{:S(2)}) collective-permute-start(f32[128,512]{1,0:T(8,128)S(1)} %get-tuple-element.47.w0), channel_id=1, source_target_pairs={{0,32},{4,12},{8,40},{12,4},{16,48},{20,28},{24,56},{28,20},{32,0}... | collective-permute-start | bytes 786440 | tf_op jit(solution)/shard_map/ppermute | solution.py:51
  52.6 10.2 %collective-permute-start.22 = (f32[128,512]{1,0:T(8,128)S(1)}, f32[128,512]{1,0:T(8,128)S(1)}, u32[]{:S(2)}, u32[]{:S(2)}) collective-permute-start(f32[128,512]{1,0:T(8,128)S(1)} %get-tuple-element.47.w0), channel_id=1, source_target_pairs={{0,96},{4,28},{8,104},{12,20},{16,112},{20,12},{24,120},{28,4},{32... | collective-permute-start | bytes 786440 | tf_op jit(solution)/shard_map/ppermute | solution.py:51
  63.2 12.5 %collective-permute-start.27 = (f32[128,512]{1,0:T(8,128)S(1)}, f32[128,512]{1,0:T(8,128)S(1)}, u32[]{:S(2)}, u32[]{:S(2)}) collective-permute-start(f32[128,512]{1,0:T(8,128)S(1)} %piece.1.refs_0_), channel_id=1, source_target_pairs={{0,16},{4,68},{8,24},{12,76},{16,0},{20,84},{24,8},{28,92},{32,48}... | collective-permute-start | bytes 786440 | tf_op jit(solution)/shard_map/ppermute | solution.py:51
  65.2 10.5 %collective-permute-start.26 = (f32[128,512]{1,0:T(8,128)S(1)}, f32[128,512]{1,0:T(8,128)S(1)}, u32[]{:S(2)}, u32[]{:S(2)}) collective-permute-start(f32[128,512]{1,0:T(8,128)S(1)} %piece.1.refs_0_), channel_id=1, source_target_pairs={{0,8},{4,36},{8,0},{12,44},{16,24},{20,52},{24,16},{28,60},{32,40}... | collective-permute-start | bytes 786440 | tf_op jit(solution)/shard_map/ppermute | solution.py:51
  67.4 8.3 %collective-permute-start.25 = (f32[128,512]{1,0:T(8,128)S(1)}, f32[128,512]{1,0:T(8,128)S(1)}, u32[]{:S(2)}, u32[]{:S(2)}) collective-permute-start(f32[128,512]{1,0:T(8,128)S(1)} %piece.1.refs_0_), channel_id=1, source_target_pairs={{0,24},{4,100},{8,16},{12,108},{16,8},{20,116},{24,0},{28,124},{32... | collective-permute-start | bytes 786440 | tf_op jit(solution)/shard_map/ppermute | solution.py:51
  (8 other events, 31.0 us)

commit v4 on v3

--- a/solution.py
+++ b/solution.py
@@ -343,7 +343,7 @@
         out_ref[:, WIDTH:] = gram
 
 
-def first_kernel(e0, e1, e2, e3, after_ref, w_ref, g_ref):
+def first_kernel(e0, e1, e2, e3, w_ref, g_ref):
     total = e0[...] + e1[...] + e2[...] + e3[...]
     w_ref[...] = total[:, :WIDTH]
     g_ref[...] = total[:, WIDTH:]
@@ -438,10 +438,10 @@
     w_own = product_call(blocks, lhs=lhs)
     e = small_call(cores_kernel, [(PANEL, WIDTH + PANEL)] * 4, "sum_cores", w_own, w_got, keep, kept)
     e = [e[0]] + [along(0, step, e[i + 1]) for i, step in enumerate(STEPS)]
-    w, g = small_call(first_kernel, [(PANEL, WIDTH), (PANEL, PANEL)], "sum_first", *e, after=(top,))
+    w, g = small_call(first_kernel, [(PANEL, WIDTH), (PANEL, PANEL)], "sum_first", *e)
     g = [g] + [along(1, step, g) for step in STEPS]
     w = [w] + [along(1, step, w) for step in STEPS]
-    (g,) = small_call(gram_kernel, [(PANEL, PANEL)], "sum_gram", *g, after=tops[1:], cost=cost_of(3))
+    (g,) = small_call(gram_kernel, [(PANEL, PANEL)], "sum_gram", *g, cost=cost_of(3))
     g_other = swap(g)
     (linv,) = small_call(factor_kernel, [(PANEL, PANEL)], "factor", g, g_other, cost=cost_of(0.5))
     (z,) = small_call(piece_kernel, [(PANEL, WIDTH)], "piece", linv, *w, *tops)

time: 84.9 us -> 83.1 us (0.979)
  waiting for transfers between devices: 12.1 us -> 5.32 us
  starting transfers between devices: 43 us -> 48.2 us
    ppermute x18, waiting for transfers between devices: 10.5 us -> 3.96 us  [along(): return lax.ppermute(x, 'row', axis_pairs(which, step, keep))]
    ppermute x18, starting transfers between devices: 24.8 us -> 28.6 us  [along(): return lax.ppermute(x, 'row', axis_pairs(which, step, keep))]
    ppermute x7, starting transfers between devices: 7.06 us -> 8.47 us  [swap(): return lax.ppermute(x, 'row', [(r, r ^ 1) for r in range(32)])]
  transfers between devices with their start and end apart: 32 -> 32, of which waited for: 8 -> 5; matrix products, arithmetic and copies ran while one was open for 0% -> 0% of each run, Pallas kernels for 27% -> 25%
where the time goes in v4:
time: 83.1 us; the launch traced here: 82 us
  starting transfers between devices  48.2 us (58%)
  Pallas kernels  27.9 us (34%)
  waiting for transfers between devices  5.32 us (6%)
    ppermute x18, starting transfers between devices, along(): return lax.ppermute(x, 'row', axis_pairs(which, step, keep))  28.6 us
    pallas_call x11, Pallas kernels, small_call(): pl.pallas_call(kernel, in_specs=[pl.BlockSpec(memory_space=pltpu.HBM)] *...  20.3 us
    ppermute x7, starting transfers between devices, swap(): return lax.ppermute(x, 'row', [(r, r ^ 1) for r in range(32)])  8.47 us
    pallas_call x2, Pallas kernels, update_call(): pl.pallas_call(functools.partial(update_kernel, count, begin), in_specs=[...  6.55 us
    ppermute x18, waiting for transfers between devices, along(): return lax.ppermute(x, 'row', axis_pairs(which, step, keep))  3.96 us
    ppermute x1, starting transfers between devices, on_device(): a01 = lax.ppermute(pa, 'col', [(0, 1)])  3.96 us
    ppermute x1, starting transfers between devices, on_device(): b03 = lax.ppermute(pb, 'col', [(0, 3)])  1.94 us
  transfers between devices with their start and end apart: 32, of which 5 were waited for; matrix products, arithmetic and copies ran while one was open for 0% of the time, Pallas kernels for 25%

profile of v4, /device:TPU:1, one launch (start us, length us, event | category | flops | bytes accessed | tf_op | source)
XLA Modules:
  0.0 82.0 jit_solution(16620192968615152233)
XLA Ops:
  1.0 4.0 %collective-permute-start = (f32[384,128]{1,0:T(8,128)S(1)}, f32[384,128]{1,0:T(8,128)S(1)}, u32[]{:S(2)}, u32[]{:S(2)}) collective-permute-start(f32[384,128]{1,0:T(8,128)S(1)} %get-tuple-element.29.refs_0_), channel_id=1, source_target_pairs={{0,1},{4,5},{8,9},{12,13},{16,17},{20,21},{24,25},{28,29},{32,33},... | collective-permute-start | bytes 589832 | tf_op jit(solution)/shard_map/ppermute | solution.py:422
  5.0 1.9 %collective-permute-start.4 = (f32[384,128]{1,0:T(8,128)S(1)}, f32[384,128]{1,0:T(8,128)S(1)}, u32[]{:S(2)}, u32[]{:S(2)}) collective-permute-start(f32[384,128]{1,0:T(8,128)S(1)} %get-tuple-element.30.refs_1_), channel_id=1, source_target_pairs={{0,3},{4,7},{8,11},{12,15},{16,19},{20,23},{24,27},{28,31},{32,35}... | collective-permute-start | bytes 589832 | tf_op jit(solution)/shard_map/ppermute | solution.py:423
  11.2 4.7 %load.1 = (f32[8,768,512]{2,1,0:T(8,128)S(1)}, f32[4,128,512]{2,1,0:T(8,128)S(1)}, f32[4,128,512]{2,1,0:T(8,128)S(1)}) custom-call(f32[768,4096]{1,0:T(8,128)} %a_ref.3), custom_call_target="tpu_custom_call" | custom-call | flops 5750000128 | tf_op jit(solution)/shard_map/load/pallas_call | solution.py:82
  16.0 1.8 %product_first.1 = (f32[4,128,512]{2,1,0:T(8,128)S(1)}, bf16[256,768]{1,0:T(8,128)(2,1)S(1)}, f32[768,128]{1,0:T(8,128)S(1)}, f32[128,128]{1,0:T(8,128)S(1)}, f32[128,128]{1,0:T(8,128)S(1)}) custom-call(f32[8,768,512]{2,1,0:T(8,128)S(1)} %get-tuple-element.28.a_ref, f32[384,128]{1,0:T(8,128)S(1)} %get-tuple-element.29.refs_0_, ...), custom_call_target="tpu_custom_call" | custom-call | flops 2300000000 | tf_op jit(solution)/shard_map/product_first/pallas_call | solution.py:82
  17.8 2.9 %collective-permute-start.6 = (f32[4,128,512]{2,1,0:T(8,128)S(1)}, f32[4,128,512]{2,1,0:T(8,128)S(1)}, u32[]{:S(2)}, u32[]{:S(2)}) collective-permute-start(f32[4,128,512]{2,1,0:T(8,128)S(1)} %get-tuple-element.32), channel_id=1, source_target_pairs={{0,4},{4,0},{8,12},{12,8},{16,20},{20,16},{24,28},{28,24},{32,36},... | collective-permute-start | bytes 3145736 | tf_op jit(solution)/shard_map/ppermute | solution.py:55
  23.3 1.4 %product_second.1.own_ref = f32[4,128,512]{2,1,0:T(8,128)S(1)} custom-call(f32[8,768,512]{2,1,0:T(8,128)S(1)} %get-tuple-element.28.a_ref, bf16[256,768]{1,0:T(8,128)(2,1)S(1)} %get-tuple-element.31.lhs_ref), custom_call_target="tpu_custom_call" | custom-call | flops 1724999936 | tf_op jit(solution)/shard_map/product_second/pallas_call | solution.py:82
  25.5 1.4 %collective-permute-start.8 = (f32[128,640]{1,0:T(8,128)S(1)}, f32[128,640]{1,0:T(8,128)S(1)}, u32[]{:S(2)}, u32[]{:S(2)}) collective-permute-start(f32[128,640]{1,0:T(8,128)S(1)} %get-tuple-element.36), channel_id=1, source_target_pairs={{0,24},{4,100},{8,16},{12,108},{16,8},{20,116},{24,0},{28,124},{32... | collective-permute-start | bytes 983048 | tf_op jit(solution)/shard_map/ppermute | solution.py:51
  26.9 2.5 %collective-permute-start.10 = (f32[128,640]{1,0:T(8,128)S(1)}, f32[128,640]{1,0:T(8,128)S(1)}, u32[]{:S(2)}, u32[]{:S(2)}) collective-permute-start(f32[128,640]{1,0:T(8,128)S(1)} %get-tuple-element.38), channel_id=1, source_target_pairs={{0,16},{4,68},{8,24},{12,76},{16,0},{20,84},{24,8},{28,92},{32,48}... | collective-permute-start | bytes 983048 | tf_op jit(solution)/shard_map/ppermute | solution.py:51
  29.5 3.3 %collective-permute-start.19 = (f32[128,512]{1,0:T(8,128)S(1)}, f32[128,512]{1,0:T(8,128)S(1)}, u32[]{:S(2)}, u32[]{:S(2)}) collective-permute-start(f32[128,512]{1,0:T(8,128)S(1)} %get-tuple-element.45), channel_id=1, source_target_pairs={{0,24},{4,100},{1,25},{5,101},{2,26},{6,102},{3,27},{7,103}} | collective-permute-start | bytes 786440 | tf_op jit(solution)/shard_map/ppermute | solution.py:51
  32.8 1.3 %collective-permute-start.20 = (f32[128,512]{1,0:T(8,128)S(1)}, f32[128,512]{1,0:T(8,128)S(1)}, u32[]{:S(2)}, u32[]{:S(2)}) collective-permute-start(f32[128,512]{1,0:T(8,128)S(1)} %get-tuple-element.46), channel_id=1, source_target_pairs={{0,8},{4,36},{1,9},{5,37},{2,10},{6,38},{3,11},{7,39}} | collective-permute-start | bytes 786440 | tf_op jit(solution)/shard_map/ppermute | solution.py:51
  34.1 1.3 %collective-permute-start.21 = (f32[128,512]{1,0:T(8,128)S(1)}, f32[128,512]{1,0:T(8,128)S(1)}, u32[]{:S(2)}, u32[]{:S(2)}) collective-permute-start(f32[128,512]{1,0:T(8,128)S(1)} %get-tuple-element.47), channel_id=1, source_target_pairs={{0,16},{4,68},{1,17},{5,69},{2,18},{6,70},{3,19},{7,71}} | collective-permute-start | bytes 786440 | tf_op jit(solution)/shard_map/ppermute | solution.py:51
  35.4 2.2 %collective-permute-done.10.e3 = f32[128,640]{1,0:T(8,128)S(1)} collective-permute-done((f32[128,640]{1,0:T(8,128)S(1)}, f32[128,640]{1,0:T(8,128)S(1)}, u32[]{:S(2)}, u32[]{:S(2)}) %collective-permute-start.10) | collective-permute-done | bytes 327712 | tf_op jit(solution)/shard_map/ppermute | solution.py:51
  37.7 1.5 %collective-permute-start.13 = (f32[128,128]{1,0:T(8,128)S(1)}, f32[128,128]{1,0:T(8,128)S(1)}, u32[]{:S(2)}, u32[]{:S(2)}) collective-permute-start(f32[128,128]{1,0:T(8,128)S(1)} %get-tuple-element.39.g0), channel_id=1, source_target_pairs={{0,64},{4,20},{8,72},{12,28},{16,80},{20,4},{24,88},{28,12},{32,96... | collective-permute-start | bytes 196616 | tf_op jit(solution)/shard_map/ppermute | solution.py:51
  41.1 3.3 %collective-permute-start.24 = (f32[128,512]{1,0:T(8,128)S(1)}, f32[128,512]{1,0:T(8,128)S(1)}, u32[]{:S(2)}, u32[]{:S(2)}) collective-permute-start(f32[128,512]{1,0:T(8,128)S(1)} %pick.1.mine_ref), channel_id=1, source_target_pairs={{0,64},{4,20},{8,72},{16,80},{24,88},{36,52},{68,84},{100,116},{1,... | collective-permute-start | bytes 786440 | tf_op jit(solution)/shard_map/ppermute | solution.py:51
  44.5 2.9 %collective-permute-start.14 = (f32[128,128]{1,0:T(8,128)S(1)}, f32[128,128]{1,0:T(8,128)S(1)}, u32[]{:S(2)}, u32[]{:S(2)}) collective-permute-start(f32[128,128]{1,0:T(8,128)S(1)} %sum_gram.1.g_ref), channel_id=1, source_target_pairs={{0,4},{4,0},{8,12},{12,8},{16,20},{20,16},{24,28},{28,24},{32,36},... | collective-permute-start | bytes 196616 | tf_op jit(solution)/shard_map/ppermute | solution.py:55
  47.4 2.0 %collective-permute-start.23 = (f32[128,512]{1,0:T(8,128)S(1)}, f32[128,512]{1,0:T(8,128)S(1)}, u32[]{:S(2)}, u32[]{:S(2)}) collective-permute-start(f32[128,512]{1,0:T(8,128)S(1)} %pick.1.mine_ref), channel_id=1, source_target_pairs={{0,32},{4,12},{8,40},{16,48},{24,56},{36,44},{68,76},{100,108},{1,... | collective-permute-start | bytes 786440 | tf_op jit(solution)/shard_map/ppermute | solution.py:51
  49.4 3.3 %collective-permute-start.22 = (f32[128,512]{1,0:T(8,128)S(1)}, f32[128,512]{1,0:T(8,128)S(1)}, u32[]{:S(2)}, u32[]{:S(2)}) collective-permute-start(f32[128,512]{1,0:T(8,128)S(1)} %pick.1.mine_ref), channel_id=1, source_target_pairs={{0,96},{4,28},{8,104},{16,112},{24,120},{36,60},{68,92},{100,124},... | collective-permute-start | bytes 786440 | tf_op jit(solution)/shard_map/ppermute | solution.py:51
  53.0 3.1 %collective-permute-start.15 = (f32[128,512]{1,0:T(8,128)S(1)}, f32[128,512]{1,0:T(8,128)S(1)}, u32[]{:S(2)}, u32[]{:S(2)}) collective-permute-start(f32[128,512]{1,0:T(8,128)S(1)} %get-tuple-element.41.w0), channel_id=1, source_target_pairs={{0,96},{4,28},{8,104},{12,20},{16,112},{20,12},{24,120},{28,4},{32... | collective-permute-start | bytes 786440 | tf_op jit(solution)/shard_map/ppermute | solution.py:51
  56.1 4.5 %factor.1.linv_ref = f32[128,128]{1,0:T(8,128)S(1)} custom-call(f32[128,128]{1,0:T(8,128)S(1)} %sum_gram.1.g_ref, f32[128,128]{1,0:T(8,128)S(1)} %collective-permute-done.14.other_ref), custom_call_target="tpu_custom_call" | custom-call | flops 575000000 | tf_op jit(solution)/shard_map/factor/pallas_call | solution.py:82
  60.7 1.7 %collective-permute-done.15.w1 = f32[128,512]{1,0:T(8,128)S(1)} collective-permute-done((f32[128,512]{1,0:T(8,128)S(1)}, f32[128,512]{1,0:T(8,128)S(1)}, u32[]{:S(2)}, u32[]{:S(2)}) %collective-permute-start.15) | collective-permute-done | bytes 262176 | tf_op jit(solution)/shard_map/ppermute | solution.py:51
  63.8 2.5 %collective-permute-start.25 = (f32[128,512]{1,0:T(8,128)S(1)}, f32[128,512]{1,0:T(8,128)S(1)}, u32[]{:S(2)}, u32[]{:S(2)}) collective-permute-start(f32[128,512]{1,0:T(8,128)S(1)} %piece.1.refs_0_), channel_id=1, source_target_pairs={{0,24},{4,100},{8,16},{12,108},{16,8},{20,116},{24,0},{28,124},{32... | collective-permute-start | bytes 786440 | tf_op jit(solution)/shard_map/ppermute | solution.py:51
  66.3 7.0 %basis.1.refs_3_.v_ref = bf16[768,384]{1,0:T(8,128)(2,1)S(1)} custom-call(f32[128,128]{1,0:T(8,128)S(1)} %factor.1.linv_ref, f32[128,128]{1,0:T(8,128)S(1)} %sum_gram.1.g_ref, f32[128,128]{1,0:T(8,128)S(1)} %collective-permute-done.14.other_ref, f32[768,128]{1,0:T(8,128)S(1)} %get-tuple-element.40.panel_ref), custom_call_target="tpu_custom_call" | custom-call | flops 8049999872 | tf_op jit(solution)/shard_map/basis/pallas_call | solution.py:82
  75.2 2.3 %update.2.refs_6_ = f32[768,4096]{1,0:T(8,128)} custom-call(f32[8,768,512]{2,1,0:T(8,128)S(1)} %get-tuple-element.28.a_ref, bf16[768,384]{1,0:T(8,128)(2,1)S(1)} %basis.1.refs_3_.v_ref, f32[128,512]{1,0:T(8,128)S(1)} %piece.1.refs_0_, f32[128,512]{1,0:T(8,128)S(1)} %collective-permute-done.31.refs_1_), custom_call_target="tpu_custom_call" | custom-call | tf_op jit(solution)/shard_map/update/pallas_call | solution.py:390
  77.5 4.3 %update.3 = f32[768,4096]{1,0:T(8,128)} custom-call(f32[8,768,512]{2,1,0:T(8,128)S(1)} %get-tuple-element.28.a_ref, bf16[768,384]{1,0:T(8,128)(2,1)S(1)} %basis.1.refs_3_.v_ref, f32[128,512]{1,0:T(8,128)S(1)} %get-tuple-element.48.refs_0_, f32[128,512]{1,0:T(8,128)S(1)} %get-tuple-element.49.refs_1_, ...), custom_call_target="tpu_custom_call", output_to_operand_aliasing={{}: (8, {})} | custom-call | tf_op jit(solution)/shard_map/update/pallas_call | solution.py:390
  (55 shorter events, 14.1 us)
Async XLA Ops:
  1.0 8.5 %collective-permute-start = (f32[384,128]{1,0:T(8,128)S(1)}, f32[384,128]{1,0:T(8,128)S(1)}, u32[]{:S(2)}, u32[]{:S(2)}) collective-permute-start(f32[384,128]{1,0:T(8,128)S(1)} %get-tuple-element.29.refs_0_), channel_id=1, source_target_pairs={{0,1},{4,5},{8,9},{12,13},{16,17},{20,21},{24,25},{28,29},{32,33},... | collective-permute-start | bytes 589832 | tf_op jit(solution)/shard_map/ppermute | solution.py:422
  5.0 5.5 %collective-permute-start.4 = (f32[384,128]{1,0:T(8,128)S(1)}, f32[384,128]{1,0:T(8,128)S(1)}, u32[]{:S(2)}, u32[]{:S(2)}) collective-permute-start(f32[384,128]{1,0:T(8,128)S(1)} %get-tuple-element.30.refs_1_), channel_id=1, source_target_pairs={{0,3},{4,7},{8,11},{12,15},{16,19},{20,23},{24,27},{28,31},{32,35}... | collective-permute-start | bytes 589832 | tf_op jit(solution)/shard_map/ppermute | solution.py:423
  7.0 9.0 %collective-permute-start.1 = (f32[384,128]{1,0:T(8,128)S(1)}, f32[384,128]{1,0:T(8,128)S(1)}, u32[]{:S(2)}, u32[]{:S(2)}) collective-permute-start(f32[384,128]{1,0:T(8,128)S(1)} %get-tuple-element.29.refs_0_), channel_id=1, source_target_pairs={{0,3},{4,7},{8,11},{12,15},{16,19},{20,23},{24,27},{28,31},{32,35}... | collective-permute-start | bytes 589832 | tf_op jit(solution)/shard_map/ppermute | solution.py:425
  8.3 7.7 %collective-permute-start.3 = (f32[384,128]{1,0:T(8,128)S(1)}, f32[384,128]{1,0:T(8,128)S(1)}, u32[]{:S(2)}, u32[]{:S(2)}) collective-permute-start(f32[384,128]{1,0:T(8,128)S(1)} %get-tuple-element.30.refs_1_), channel_id=1, source_target_pairs={{0,1},{4,5},{8,9},{12,13},{16,17},{20,21},{24,25},{28,29},{32,33},... | collective-permute-start | bytes 589832 | tf_op jit(solution)/shard_map/ppermute | solution.py:424
  9.6 6.4 %collective-permute-start.2 = (f32[384,128]{1,0:T(8,128)S(1)}, f32[384,128]{1,0:T(8,128)S(1)}, u32[]{:S(2)}, u32[]{:S(2)}) collective-permute-start(f32[384,128]{1,0:T(8,128)S(1)} %collective-permute-done.refs_2_), channel_id=1, source_target_pairs={{1,2},{5,6},{9,10},{13,14},{17,18},{21,22},{25,26},{29,30},{33,34}... | collective-permute-start | bytes 589832 | tf_op jit(solution)/shard_map/ppermute | solution.py:426
  17.8 7.5 %collective-permute-start.6 = (f32[4,128,512]{2,1,0:T(8,128)S(1)}, f32[4,128,512]{2,1,0:T(8,128)S(1)}, u32[]{:S(2)}, u32[]{:S(2)}) collective-permute-start(f32[4,128,512]{2,1,0:T(8,128)S(1)} %get-tuple-element.32), channel_id=1, source_target_pairs={{0,4},{4,0},{8,12},{12,8},{16,20},{20,16},{24,28},{28,24},{32,36},... | collective-permute-start | bytes 3145736 | tf_op jit(solution)/shard_map/ppermute | solution.py:55
  20.7 8.7 %collective-permute-start.18 = (f32[4,128,512]{2,1,0:T(8,128)S(1)}, f32[4,128,512]{2,1,0:T(8,128)S(1)}, u32[]{:S(2)}, u32[]{:S(2)}) collective-permute-start(f32[4,128,512]{2,1,0:T(8,128)S(1)} %get-tuple-element.43), channel_id=1, source_target_pairs={{0,4},{1,5},{2,6},{3,7}} | collective-permute-start | bytes 3145736 | tf_op jit(solution)/shard_map/ppermute | solution.py:430
  25.5 8.6 %collective-permute-start.8 = (f32[128,640]{1,0:T(8,128)S(1)}, f32[128,640]{1,0:T(8,128)S(1)}, u32[]{:S(2)}, u32[]{:S(2)}) collective-permute-start(f32[128,640]{1,0:T(8,128)S(1)} %get-tuple-element.36), channel_id=1, source_target_pairs={{0,24},{4,100},{8,16},{12,108},{16,8},{20,116},{24,0},{28,124},{32... | collective-permute-start | bytes 983048 | tf_op jit(solution)/shard_map/ppermute | solution.py:51
  26.9 8.5 %collective-permute-start.9 = (f32[128,640]{1,0:T(8,128)S(1)}, f32[128,640]{1,0:T(8,128)S(1)}, u32[]{:S(2)}, u32[]{:S(2)}) collective-permute-start(f32[128,640]{1,0:T(8,128)S(1)} %get-tuple-element.37), channel_id=1, source_target_pairs={{0,8},{4,36},{8,0},{12,44},{16,24},{20,52},{24,16},{28,60},{32,40}... | collective-permute-start | bytes 983048 | tf_op jit(solution)/shard_map/ppermute | solution.py:51
  26.9 10.8 %collective-permute-start.10 = (f32[128,640]{1,0:T(8,128)S(1)}, f32[128,640]{1,0:T(8,128)S(1)}, u32[]{:S(2)}, u32[]{:S(2)}) collective-permute-start(f32[128,640]{1,0:T(8,128)S(1)} %get-tuple-element.38), channel_id=1, source_target_pairs={{0,16},{4,68},{8,24},{12,76},{16,0},{20,84},{24,8},{28,92},{32,48}... | collective-permute-start | bytes 983048 | tf_op jit(solution)/shard_map/ppermute | solution.py:51
  29.5 10.4 %collective-permute-start.19 = (f32[128,512]{1,0:T(8,128)S(1)}, f32[128,512]{1,0:T(8,128)S(1)}, u32[]{:S(2)}, u32[]{:S(2)}) collective-permute-start(f32[128,512]{1,0:T(8,128)S(1)} %get-tuple-element.45), channel_id=1, source_target_pairs={{0,24},{4,100},{1,25},{5,101},{2,26},{6,102},{3,27},{7,103}} | collective-permute-start | bytes 786440 | tf_op jit(solution)/shard_map/ppermute | solution.py:51
  32.8 8.3 %collective-permute-start.20 = (f32[128,512]{1,0:T(8,128)S(1)}, f32[128,512]{1,0:T(8,128)S(1)}, u32[]{:S(2)}, u32[]{:S(2)}) collective-permute-start(f32[128,512]{1,0:T(8,128)S(1)} %get-tuple-element.46), channel_id=1, source_target_pairs={{0,8},{4,36},{1,9},{5,37},{2,10},{6,38},{3,11},{7,39}} | collective-permute-start | bytes 786440 | tf_op jit(solution)/shard_map/ppermute | solution.py:51
  34.1 7.0 %collective-permute-start.21 = (f32[128,512]{1,0:T(8,128)S(1)}, f32[128,512]{1,0:T(8,128)S(1)}, u32[]{:S(2)}, u32[]{:S(2)}) collective-permute-start(f32[128,512]{1,0:T(8,128)S(1)} %get-tuple-element.47), channel_id=1, source_target_pairs={{0,16},{4,68},{1,17},{5,69},{2,18},{6,70},{3,19},{7,71}} | collective-permute-start | bytes 786440 | tf_op jit(solution)/shard_map/ppermute | solution.py:51
  37.7 6.7 %collective-permute-start.13 = (f32[128,128]{1,0:T(8,128)S(1)}, f32[128,128]{1,0:T(8,128)S(1)}, u32[]{:S(2)}, u32[]{:S(2)}) collective-permute-start(f32[128,128]{1,0:T(8,128)S(1)} %get-tuple-element.39.g0), channel_id=1, source_target_pairs={{0,64},{4,20},{8,72},{12,28},{16,80},{20,4},{24,88},{28,12},{32,96... | collective-permute-start | bytes 196616 | tf_op jit(solution)/shard_map/ppermute | solution.py:51
  41.1 11.7 %collective-permute-start.24 = (f32[128,512]{1,0:T(8,128)S(1)}, f32[128,512]{1,0:T(8,128)S(1)}, u32[]{:S(2)}, u32[]{:S(2)}) collective-permute-start(f32[128,512]{1,0:T(8,128)S(1)} %pick.1.mine_ref), channel_id=1, source_target_pairs={{0,64},{4,20},{8,72},{16,80},{24,88},{36,52},{68,84},{100,116},{1,... | collective-permute-start | bytes 786440 | tf_op jit(solution)/shard_map/ppermute | solution.py:51
  44.5 8.5 %collective-permute-start.14 = (f32[128,128]{1,0:T(8,128)S(1)}, f32[128,128]{1,0:T(8,128)S(1)}, u32[]{:S(2)}, u32[]{:S(2)}) collective-permute-start(f32[128,128]{1,0:T(8,128)S(1)} %sum_gram.1.g_ref), channel_id=1, source_target_pairs={{0,4},{4,0},{8,12},{12,8},{16,20},{20,16},{24,28},{28,24},{32,36},... | collective-permute-start | bytes 196616 | tf_op jit(solution)/shard_map/ppermute | solution.py:55
  47.4 13.2 %collective-permute-start.23 = (f32[128,512]{1,0:T(8,128)S(1)}, f32[128,512]{1,0:T(8,128)S(1)}, u32[]{:S(2)}, u32[]{:S(2)}) collective-permute-start(f32[128,512]{1,0:T(8,128)S(1)} %pick.1.mine_ref), channel_id=1, source_target_pairs={{0,32},{4,12},{8,40},{16,48},{24,56},{36,44},{68,76},{100,108},{1,... | collective-permute-start | bytes 786440 | tf_op jit(solution)/shard_map/ppermute | solution.py:51
  49.4 11.2 %collective-permute-start.22 = (f32[128,512]{1,0:T(8,128)S(1)}, f32[128,512]{1,0:T(8,128)S(1)}, u32[]{:S(2)}, u32[]{:S(2)}) collective-permute-start(f32[128,512]{1,0:T(8,128)S(1)} %pick.1.mine_ref), channel_id=1, source_target_pairs={{0,96},{4,28},{8,104},{16,112},{24,120},{36,60},{68,92},{100,124},... | collective-permute-start | bytes 786440 | tf_op jit(solution)/shard_map/ppermute | solution.py:51
  52.8 7.9 %collective-permute-start.17 = (f32[128,512]{1,0:T(8,128)S(1)}, f32[128,512]{1,0:T(8,128)S(1)}, u32[]{:S(2)}, u32[]{:S(2)}) collective-permute-start(f32[128,512]{1,0:T(8,128)S(1)} %get-tuple-element.41.w0), channel_id=1, source_target_pairs={{0,64},{4,20},{8,72},{12,28},{16,80},{20,4},{24,88},{28,12},{32,96... | collective-permute-start | bytes 786440 | tf_op jit(solution)/shard_map/ppermute | solution.py:51
  52.9 7.8 %collective-permute-start.16 = (f32[128,512]{1,0:T(8,128)S(1)}, f32[128,512]{1,0:T(8,128)S(1)}, u32[]{:S(2)}, u32[]{:S(2)}) collective-permute-start(f32[128,512]{1,0:T(8,128)S(1)} %get-tuple-element.41.w0), channel_id=1, source_target_pairs={{0,32},{4,12},{8,40},{12,4},{16,48},{20,28},{24,56},{28,20},{32,0}... | collective-permute-start | bytes 786440 | tf_op jit(solution)/shard_map/ppermute | solution.py:51
  53.0 9.4 %collective-permute-start.15 = (f32[128,512]{1,0:T(8,128)S(1)}, f32[128,512]{1,0:T(8,128)S(1)}, u32[]{:S(2)}, u32[]{:S(2)}) collective-permute-start(f32[128,512]{1,0:T(8,128)S(1)} %get-tuple-element.41.w0), channel_id=1, source_target_pairs={{0,96},{4,28},{8,104},{12,20},{16,112},{20,12},{24,120},{28,4},{32... | collective-permute-start | bytes 786440 | tf_op jit(solution)/shard_map/ppermute | solution.py:51
  62.8 11.3 %collective-permute-start.27 = (f32[128,512]{1,0:T(8,128)S(1)}, f32[128,512]{1,0:T(8,128)S(1)}, u32[]{:S(2)}, u32[]{:S(2)}) collective-permute-start(f32[128,512]{1,0:T(8,128)S(1)} %piece.1.refs_0_), channel_id=1, source_target_pairs={{0,16},{4,68},{8,24},{12,76},{16,0},{20,84},{24,8},{28,92},{32,48}... | collective-permute-start | bytes 786440 | tf_op jit(solution)/shard_map/ppermute | solution.py:51
  63.1 11.0 %collective-permute-start.26 = (f32[128,512]{1,0:T(8,128)S(1)}, f32[128,512]{1,0:T(8,128)S(1)}, u32[]{:S(2)}, u32[]{:S(2)}) collective-permute-start(f32[128,512]{1,0:T(8,128)S(1)} %piece.1.refs_0_), channel_id=1, source_target_pairs={{0,8},{4,36},{8,0},{12,44},{16,24},{20,52},{24,16},{28,60},{32,40}... | collective-permute-start | bytes 786440 | tf_op jit(solution)/shard_map/ppermute | solution.py:51
  63.8 10.3 %collective-permute-start.25 = (f32[128,512]{1,0:T(8,128)S(1)}, f32[128,512]{1,0:T(8,128)S(1)}, u32[]{:S(2)}, u32[]{:S(2)}) collective-permute-start(f32[128,512]{1,0:T(8,128)S(1)} %piece.1.refs_0_), channel_id=1, source_target_pairs={{0,24},{4,100},{8,16},{12,108},{16,8},{20,116},{24,0},{28,124},{32... | collective-permute-start | bytes 786440 | tf_op jit(solution)/shard_map/ppermute | solution.py:51
  (8 other events, 30.0 us)

commit v5 on v4

--- a/solution.py
+++ b/solution.py
@@ -102,10 +102,10 @@
 
 
 def panel_kernel(a_ref, pa_ref, pb_ref, sem):
-    rows = pa_ref.shape[0]
+    upper = pa_ref.shape[0]
     copies = [
-        pltpu.make_async_copy(a_ref.at[i * rows : (i + 1) * rows, :PANEL], out_ref, sem.at[i])
-        for i, out_ref in enumerate((pa_ref, pb_ref))
+        pltpu.make_async_copy(a_ref.at[:upper, :PANEL], pa_ref, sem.at[0]),
+        pltpu.make_async_copy(a_ref.at[upper:, :PANEL], pb_ref, sem.at[1]),
     ]
     for copy in copies:
         copy.start()
@@ -114,12 +114,14 @@
 
 
 def panel_call(a):
-    half = jax.ShapeDtypeStruct((a.shape[0] // 2, PANEL), F32)
+    rows = a.shape[0]
+    upper = rows * 7 // 12
+    parts = [jax.ShapeDtypeStruct((count, PANEL), F32) for count in (upper, rows - upper)]
     return pl.pallas_call(
         panel_kernel,
         in_specs=[pl.BlockSpec(memory_space=pltpu.HBM)],
         out_specs=[pl.BlockSpec(memory_space=pltpu.VMEM)] * 2,
-        out_shape=[half, half],
+        out_shape=parts,
         scratch_shapes=[pltpu.SemaphoreType.DMA((2,))],
         compiler_params=params(LARGE),
         name="panel",

time: 83.1 us -> 82.7 us (level)
  no operation moved by 1% of the time
where the time goes in v5:
time: 82.7 us; the launch traced here: 81.7 us
  starting transfers between devices  47.9 us (58%)
  Pallas kernels  27.9 us (34%)
  waiting for transfers between devices  5.31 us (6%)
    ppermute x18, starting transfers between devices, along(): return lax.ppermute(x, 'row', axis_pairs(which, step, keep))  28.6 us
    pallas_call x11, Pallas kernels, small_call(): pl.pallas_call(kernel, in_specs=[pl.BlockSpec(memory_space=pltpu.HBM)] *...  20.3 us
    ppermute x7, starting transfers between devices, swap(): return lax.ppermute(x, 'row', [(r, r ^ 1) for r in range(32)])  8.15 us
    pallas_call x2, Pallas kernels, update_call(): pl.pallas_call(functools.partial(update_kernel, count, begin), in_specs=[...  6.55 us
    ppermute x18, waiting for transfers between devices, along(): return lax.ppermute(x, 'row', axis_pairs(which, step, keep))  3.96 us
    ppermute x1, starting transfers between devices, on_device(): a01 = lax.ppermute(pa, 'col', [(0, 1)])  3.96 us
    ppermute x1, starting transfers between devices, on_device(): b03 = lax.ppermute(pb, 'col', [(0, 3)])  1.94 us
  transfers between devices with their start and end apart: 32, of which 5 were waited for; matrix products, arithmetic and copies ran while one was open for 0% of the time, Pallas kernels for 25%

profile of v5, /device:TPU:1, one launch (start us, length us, event | category | flops | bytes accessed | tf_op | source)
XLA Modules:
  0.0 81.7 jit_solution(6337863338354625275)
XLA Ops:
  1.1 4.0 %collective-permute-start = (f32[448,128]{1,0:T(8,128)S(1)}, f32[448,128]{1,0:T(8,128)S(1)}, u32[]{:S(2)}, u32[]{:S(2)}) collective-permute-start(f32[448,128]{1,0:T(8,128)S(1)} %get-tuple-element.29.refs_0_), channel_id=1, source_target_pairs={{0,1},{4,5},{8,9},{12,13},{16,17},{20,21},{24,25},{28,29},{32,33},... | collective-permute-start | bytes 688136 | tf_op jit(solution)/shard_map/ppermute | solution.py:424
  5.0 1.9 %collective-permute-start.4 = (f32[320,128]{1,0:T(8,128)S(1)}, f32[320,128]{1,0:T(8,128)S(1)}, u32[]{:S(2)}, u32[]{:S(2)}) collective-permute-start(f32[320,128]{1,0:T(8,128)S(1)} %get-tuple-element.30.refs_1_), channel_id=1, source_target_pairs={{0,3},{4,7},{8,11},{12,15},{16,19},{20,23},{24,27},{28,31},{32,35}... | collective-permute-start | bytes 491528 | tf_op jit(solution)/shard_map/ppermute | solution.py:425
  11.2 4.7 %load.1 = (f32[8,768,512]{2,1,0:T(8,128)S(1)}, f32[4,128,512]{2,1,0:T(8,128)S(1)}, f32[4,128,512]{2,1,0:T(8,128)S(1)}) custom-call(f32[768,4096]{1,0:T(8,128)} %a_ref.3), custom_call_target="tpu_custom_call" | custom-call | flops 5750000128 | tf_op jit(solution)/shard_map/load/pallas_call | solution.py:82
  16.0 1.8 %product_first.1 = (f32[4,128,512]{2,1,0:T(8,128)S(1)}, bf16[256,768]{1,0:T(8,128)(2,1)S(1)}, f32[768,128]{1,0:T(8,128)S(1)}, f32[128,128]{1,0:T(8,128)S(1)}, f32[128,128]{1,0:T(8,128)S(1)}) custom-call(f32[8,768,512]{2,1,0:T(8,128)S(1)} %get-tuple-element.28.a_ref, f32[448,128]{1,0:T(8,128)S(1)} %get-tuple-element.29.refs_0_, ...), custom_call_target="tpu_custom_call" | custom-call | flops 2300000000 | tf_op jit(solution)/shard_map/product_first/pallas_call | solution.py:82
  17.8 2.6 %collective-permute-start.6 = (f32[4,128,512]{2,1,0:T(8,128)S(1)}, f32[4,128,512]{2,1,0:T(8,128)S(1)}, u32[]{:S(2)}, u32[]{:S(2)}) collective-permute-start(f32[4,128,512]{2,1,0:T(8,128)S(1)} %get-tuple-element.32), channel_id=1, source_target_pairs={{0,4},{4,0},{8,12},{12,8},{16,20},{20,16},{24,28},{28,24},{32,36},... | collective-permute-start | bytes 3145736 | tf_op jit(solution)/shard_map/ppermute | solution.py:55
  23.0 1.4 %product_second.1.own_ref = f32[4,128,512]{2,1,0:T(8,128)S(1)} custom-call(f32[8,768,512]{2,1,0:T(8,128)S(1)} %get-tuple-element.28.a_ref, bf16[256,768]{1,0:T(8,128)(2,1)S(1)} %get-tuple-element.31.lhs_ref), custom_call_target="tpu_custom_call" | custom-call | flops 1724999936 | tf_op jit(solution)/shard_map/product_second/pallas_call | solution.py:82
  25.2 1.4 %collective-permute-start.8 = (f32[128,640]{1,0:T(8,128)S(1)}, f32[128,640]{1,0:T(8,128)S(1)}, u32[]{:S(2)}, u32[]{:S(2)}) collective-permute-start(f32[128,640]{1,0:T(8,128)S(1)} %get-tuple-element.36), channel_id=1, source_target_pairs={{0,24},{4,100},{8,16},{12,108},{16,8},{20,116},{24,0},{28,124},{32... | collective-permute-start | bytes 983048 | tf_op jit(solution)/shard_map/ppermute | solution.py:51
  26.6 2.5 %collective-permute-start.10 = (f32[128,640]{1,0:T(8,128)S(1)}, f32[128,640]{1,0:T(8,128)S(1)}, u32[]{:S(2)}, u32[]{:S(2)}) collective-permute-start(f32[128,640]{1,0:T(8,128)S(1)} %get-tuple-element.38), channel_id=1, source_target_pairs={{0,16},{4,68},{8,24},{12,76},{16,0},{20,84},{24,8},{28,92},{32,48}... | collective-permute-start | bytes 983048 | tf_op jit(solution)/shard_map/ppermute | solution.py:51
  29.2 3.3 %collective-permute-start.19 = (f32[128,512]{1,0:T(8,128)S(1)}, f32[128,512]{1,0:T(8,128)S(1)}, u32[]{:S(2)}, u32[]{:S(2)}) collective-permute-start(f32[128,512]{1,0:T(8,128)S(1)} %get-tuple-element.45), channel_id=1, source_target_pairs={{0,24},{4,100},{1,25},{5,101},{2,26},{6,102},{3,27},{7,103}} | collective-permute-start | bytes 786440 | tf_op jit(solution)/shard_map/ppermute | solution.py:51
  32.5 1.3 %collective-permute-start.20 = (f32[128,512]{1,0:T(8,128)S(1)}, f32[128,512]{1,0:T(8,128)S(1)}, u32[]{:S(2)}, u32[]{:S(2)}) collective-permute-start(f32[128,512]{1,0:T(8,128)S(1)} %get-tuple-element.46), channel_id=1, source_target_pairs={{0,8},{4,36},{1,9},{5,37},{2,10},{6,38},{3,11},{7,39}} | collective-permute-start | bytes 786440 | tf_op jit(solution)/shard_map/ppermute | solution.py:51
  33.8 1.3 %collective-permute-start.21 = (f32[128,512]{1,0:T(8,128)S(1)}, f32[128,512]{1,0:T(8,128)S(1)}, u32[]{:S(2)}, u32[]{:S(2)}) collective-permute-start(f32[128,512]{1,0:T(8,128)S(1)} %get-tuple-element.47), channel_id=1, source_target_pairs={{0,16},{4,68},{1,17},{5,69},{2,18},{6,70},{3,19},{7,71}} | collective-permute-start | bytes 786440 | tf_op jit(solution)/shard_map/ppermute | solution.py:51
  35.1 2.2 %collective-permute-done.10.e3 = f32[128,640]{1,0:T(8,128)S(1)} collective-permute-done((f32[128,640]{1,0:T(8,128)S(1)}, f32[128,640]{1,0:T(8,128)S(1)}, u32[]{:S(2)}, u32[]{:S(2)}) %collective-permute-start.10) | collective-permute-done | bytes 327712 | tf_op jit(solution)/shard_map/ppermute | solution.py:51
  37.4 1.5 %collective-permute-start.13 = (f32[128,128]{1,0:T(8,128)S(1)}, f32[128,128]{1,0:T(8,128)S(1)}, u32[]{:S(2)}, u32[]{:S(2)}) collective-permute-start(f32[128,128]{1,0:T(8,128)S(1)} %get-tuple-element.39.g0), channel_id=1, source_target_pairs={{0,64},{4,20},{8,72},{12,28},{16,80},{20,4},{24,88},{28,12},{32,96... | collective-permute-start | bytes 196616 | tf_op jit(solution)/shard_map/ppermute | solution.py:51
  40.8 3.3 %collective-permute-start.24 = (f32[128,512]{1,0:T(8,128)S(1)}, f32[128,512]{1,0:T(8,128)S(1)}, u32[]{:S(2)}, u32[]{:S(2)}) collective-permute-start(f32[128,512]{1,0:T(8,128)S(1)} %pick.1.mine_ref), channel_id=1, source_target_pairs={{0,64},{4,20},{8,72},{16,80},{24,88},{36,52},{68,84},{100,116},{1,... | collective-permute-start | bytes 786440 | tf_op jit(solution)/shard_map/ppermute | solution.py:51
  44.2 2.9 %collective-permute-start.14 = (f32[128,128]{1,0:T(8,128)S(1)}, f32[128,128]{1,0:T(8,128)S(1)}, u32[]{:S(2)}, u32[]{:S(2)}) collective-permute-start(f32[128,128]{1,0:T(8,128)S(1)} %sum_gram.1.g_ref), channel_id=1, source_target_pairs={{0,4},{4,0},{8,12},{12,8},{16,20},{20,16},{24,28},{28,24},{32,36},... | collective-permute-start | bytes 196616 | tf_op jit(solution)/shard_map/ppermute | solution.py:55
  47.1 2.0 %collective-permute-start.23 = (f32[128,512]{1,0:T(8,128)S(1)}, f32[128,512]{1,0:T(8,128)S(1)}, u32[]{:S(2)}, u32[]{:S(2)}) collective-permute-start(f32[128,512]{1,0:T(8,128)S(1)} %pick.1.mine_ref), channel_id=1, source_target_pairs={{0,32},{4,12},{8,40},{16,48},{24,56},{36,44},{68,76},{100,108},{1,... | collective-permute-start | bytes 786440 | tf_op jit(solution)/shard_map/ppermute | solution.py:51
  49.1 3.3 %collective-permute-start.22 = (f32[128,512]{1,0:T(8,128)S(1)}, f32[128,512]{1,0:T(8,128)S(1)}, u32[]{:S(2)}, u32[]{:S(2)}) collective-permute-start(f32[128,512]{1,0:T(8,128)S(1)} %pick.1.mine_ref), channel_id=1, source_target_pairs={{0,96},{4,28},{8,104},{16,112},{24,120},{36,60},{68,92},{100,124},... | collective-permute-start | bytes 786440 | tf_op jit(solution)/shard_map/ppermute | solution.py:51
  52.7 3.1 %collective-permute-start.15 = (f32[128,512]{1,0:T(8,128)S(1)}, f32[128,512]{1,0:T(8,128)S(1)}, u32[]{:S(2)}, u32[]{:S(2)}) collective-permute-start(f32[128,512]{1,0:T(8,128)S(1)} %get-tuple-element.41.w0), channel_id=1, source_target_pairs={{0,96},{4,28},{8,104},{12,20},{16,112},{20,12},{24,120},{28,4},{32... | collective-permute-start | bytes 786440 | tf_op jit(solution)/shard_map/ppermute | solution.py:51
  55.8 4.5 %factor.1.linv_ref = f32[128,128]{1,0:T(8,128)S(1)} custom-call(f32[128,128]{1,0:T(8,128)S(1)} %sum_gram.1.g_ref, f32[128,128]{1,0:T(8,128)S(1)} %collective-permute-done.14.other_ref), custom_call_target="tpu_custom_call" | custom-call | flops 575000000 | tf_op jit(solution)/shard_map/factor/pallas_call | solution.py:82
  60.4 1.7 %collective-permute-done.15.w1 = f32[128,512]{1,0:T(8,128)S(1)} collective-permute-done((f32[128,512]{1,0:T(8,128)S(1)}, f32[128,512]{1,0:T(8,128)S(1)}, u32[]{:S(2)}, u32[]{:S(2)}) %collective-permute-start.15) | collective-permute-done | bytes 262176 | tf_op jit(solution)/shard_map/ppermute | solution.py:51
  63.5 2.5 %collective-permute-start.25 = (f32[128,512]{1,0:T(8,128)S(1)}, f32[128,512]{1,0:T(8,128)S(1)}, u32[]{:S(2)}, u32[]{:S(2)}) collective-permute-start(f32[128,512]{1,0:T(8,128)S(1)} %piece.1.refs_0_), channel_id=1, source_target_pairs={{0,24},{4,100},{8,16},{12,108},{16,8},{20,116},{24,0},{28,124},{32... | collective-permute-start | bytes 786440 | tf_op jit(solution)/shard_map/ppermute | solution.py:51
  66.0 7.0 %basis.1.refs_3_.v_ref = bf16[768,384]{1,0:T(8,128)(2,1)S(1)} custom-call(f32[128,128]{1,0:T(8,128)S(1)} %factor.1.linv_ref, f32[128,128]{1,0:T(8,128)S(1)} %sum_gram.1.g_ref, f32[128,128]{1,0:T(8,128)S(1)} %collective-permute-done.14.other_ref, f32[768,128]{1,0:T(8,128)S(1)} %get-tuple-element.40.panel_ref), custom_call_target="tpu_custom_call" | custom-call | flops 8049999872 | tf_op jit(solution)/shard_map/basis/pallas_call | solution.py:82
  74.9 2.3 %update.2.refs_6_ = f32[768,4096]{1,0:T(8,128)} custom-call(f32[8,768,512]{2,1,0:T(8,128)S(1)} %get-tuple-element.28.a_ref, bf16[768,384]{1,0:T(8,128)(2,1)S(1)} %basis.1.refs_3_.v_ref, f32[128,512]{1,0:T(8,128)S(1)} %piece.1.refs_0_, f32[128,512]{1,0:T(8,128)S(1)} %collective-permute-done.31.refs_1_), custom_call_target="tpu_custom_call" | custom-call | tf_op jit(solution)/shard_map/update/pallas_call | solution.py:392
  77.2 4.3 %update.3 = f32[768,4096]{1,0:T(8,128)} custom-call(f32[8,768,512]{2,1,0:T(8,128)S(1)} %get-tuple-element.28.a_ref, bf16[768,384]{1,0:T(8,128)(2,1)S(1)} %basis.1.refs_3_.v_ref, f32[128,512]{1,0:T(8,128)S(1)} %get-tuple-element.48.refs_0_, f32[128,512]{1,0:T(8,128)S(1)} %get-tuple-element.49.refs_1_, ...), custom_call_target="tpu_custom_call", output_to_operand_aliasing={{}: (8, {})} | custom-call | tf_op jit(solution)/shard_map/update/pallas_call | solution.py:392
  (55 shorter events, 14.0 us)
Async XLA Ops:
  1.1 9.4 %collective-permute-start = (f32[448,128]{1,0:T(8,128)S(1)}, f32[448,128]{1,0:T(8,128)S(1)}, u32[]{:S(2)}, u32[]{:S(2)}) collective-permute-start(f32[448,128]{1,0:T(8,128)S(1)} %get-tuple-element.29.refs_0_), channel_id=1, source_target_pairs={{0,1},{4,5},{8,9},{12,13},{16,17},{20,21},{24,25},{28,29},{32,33},... | collective-permute-start | bytes 688136 | tf_op jit(solution)/shard_map/ppermute | solution.py:424
  7.0 9.0 %collective-permute-start.3 = (f32[320,128]{1,0:T(8,128)S(1)}, f32[320,128]{1,0:T(8,128)S(1)}, u32[]{:S(2)}, u32[]{:S(2)}) collective-permute-start(f32[320,128]{1,0:T(8,128)S(1)} %get-tuple-element.30.refs_1_), channel_id=1, source_target_pairs={{0,1},{4,5},{8,9},{12,13},{16,17},{20,21},{24,25},{28,29},{32,33},... | collective-permute-start | bytes 491528 | tf_op jit(solution)/shard_map/ppermute | solution.py:426
  8.3 7.7 %collective-permute-start.1 = (f32[448,128]{1,0:T(8,128)S(1)}, f32[448,128]{1,0:T(8,128)S(1)}, u32[]{:S(2)}, u32[]{:S(2)}) collective-permute-start(f32[448,128]{1,0:T(8,128)S(1)} %get-tuple-element.29.refs_0_), channel_id=1, source_target_pairs={{0,3},{4,7},{8,11},{12,15},{16,19},{20,23},{24,27},{28,31},{32,35}... | collective-permute-start | bytes 688136 | tf_op jit(solution)/shard_map/ppermute | solution.py:427
  9.8 6.1 %collective-permute-start.5 = (f32[320,128]{1,0:T(8,128)S(1)}, f32[320,128]{1,0:T(8,128)S(1)}, u32[]{:S(2)}, u32[]{:S(2)}) collective-permute-start(f32[320,128]{1,0:T(8,128)S(1)} %collective-permute-done.4.refs_6_), channel_id=1, source_target_pairs={{3,2},{7,6},{11,10},{15,14},{19,18},{23,22},{27,26},{31,30},{35,34... | collective-permute-start | bytes 491528 | tf_op jit(solution)/shard_map/ppermute | solution.py:429
  10.5 5.5 %collective-permute-start.2 = (f32[448,128]{1,0:T(8,128)S(1)}, f32[448,128]{1,0:T(8,128)S(1)}, u32[]{:S(2)}, u32[]{:S(2)}) collective-permute-start(f32[448,128]{1,0:T(8,128)S(1)} %collective-permute-done.refs_2_), channel_id=1, source_target_pairs={{1,2},{5,6},{9,10},{13,14},{17,18},{21,22},{25,26},{29,30},{33,34}... | collective-permute-start | bytes 688136 | tf_op jit(solution)/shard_map/ppermute | solution.py:428
  17.8 7.2 %collective-permute-start.6 = (f32[4,128,512]{2,1,0:T(8,128)S(1)}, f32[4,128,512]{2,1,0:T(8,128)S(1)}, u32[]{:S(2)}, u32[]{:S(2)}) collective-permute-start(f32[4,128,512]{2,1,0:T(8,128)S(1)} %get-tuple-element.32), channel_id=1, source_target_pairs={{0,4},{4,0},{8,12},{12,8},{16,20},{20,16},{24,28},{28,24},{32,36},... | collective-permute-start | bytes 3145736 | tf_op jit(solution)/shard_map/ppermute | solution.py:55
  20.4 8.7 %collective-permute-start.18 = (f32[4,128,512]{2,1,0:T(8,128)S(1)}, f32[4,128,512]{2,1,0:T(8,128)S(1)}, u32[]{:S(2)}, u32[]{:S(2)}) collective-permute-start(f32[4,128,512]{2,1,0:T(8,128)S(1)} %get-tuple-element.43), channel_id=1, source_target_pairs={{0,4},{1,5},{2,6},{3,7}} | collective-permute-start | bytes 3145736 | tf_op jit(solution)/shard_map/ppermute | solution.py:432
  25.2 8.6 %collective-permute-start.8 = (f32[128,640]{1,0:T(8,128)S(1)}, f32[128,640]{1,0:T(8,128)S(1)}, u32[]{:S(2)}, u32[]{:S(2)}) collective-permute-start(f32[128,640]{1,0:T(8,128)S(1)} %get-tuple-element.36), channel_id=1, source_target_pairs={{0,24},{4,100},{8,16},{12,108},{16,8},{20,116},{24,0},{28,124},{32... | collective-permute-start | bytes 983048 | tf_op jit(solution)/shard_map/ppermute | solution.py:51
  26.6 8.5 %collective-permute-start.9 = (f32[128,640]{1,0:T(8,128)S(1)}, f32[128,640]{1,0:T(8,128)S(1)}, u32[]{:S(2)}, u32[]{:S(2)}) collective-permute-start(f32[128,640]{1,0:T(8,128)S(1)} %get-tuple-element.37), channel_id=1, source_target_pairs={{0,8},{4,36},{8,0},{12,44},{16,24},{20,52},{24,16},{28,60},{32,40}... | collective-permute-start | bytes 983048 | tf_op jit(solution)/shard_map/ppermute | solution.py:51
  26.6 10.8 %collective-permute-start.10 = (f32[128,640]{1,0:T(8,128)S(1)}, f32[128,640]{1,0:T(8,128)S(1)}, u32[]{:S(2)}, u32[]{:S(2)}) collective-permute-start(f32[128,640]{1,0:T(8,128)S(1)} %get-tuple-element.38), channel_id=1, source_target_pairs={{0,16},{4,68},{8,24},{12,76},{16,0},{20,84},{24,8},{28,92},{32,48}... | collective-permute-start | bytes 983048 | tf_op jit(solution)/shard_map/ppermute | solution.py:51
  29.2 10.4 %collective-permute-start.19 = (f32[128,512]{1,0:T(8,128)S(1)}, f32[128,512]{1,0:T(8,128)S(1)}, u32[]{:S(2)}, u32[]{:S(2)}) collective-permute-start(f32[128,512]{1,0:T(8,128)S(1)} %get-tuple-element.45), channel_id=1, source_target_pairs={{0,24},{4,100},{1,25},{5,101},{2,26},{6,102},{3,27},{7,103}} | collective-permute-start | bytes 786440 | tf_op jit(solution)/shard_map/ppermute | solution.py:51
  32.5 8.3 %collective-permute-start.20 = (f32[128,512]{1,0:T(8,128)S(1)}, f32[128,512]{1,0:T(8,128)S(1)}, u32[]{:S(2)}, u32[]{:S(2)}) collective-permute-start(f32[128,512]{1,0:T(8,128)S(1)} %get-tuple-element.46), channel_id=1, source_target_pairs={{0,8},{4,36},{1,9},{5,37},{2,10},{6,38},{3,11},{7,39}} | collective-permute-start | bytes 786440 | tf_op jit(solution)/shard_map/ppermute | solution.py:51
  33.8 7.0 %collective-permute-start.21 = (f32[128,512]{1,0:T(8,128)S(1)}, f32[128,512]{1,0:T(8,128)S(1)}, u32[]{:S(2)}, u32[]{:S(2)}) collective-permute-start(f32[128,512]{1,0:T(8,128)S(1)} %get-tuple-element.47), channel_id=1, source_target_pairs={{0,16},{4,68},{1,17},{5,69},{2,18},{6,70},{3,19},{7,71}} | collective-permute-start | bytes 786440 | tf_op jit(solution)/shard_map/ppermute | solution.py:51
  37.4 6.7 %collective-permute-start.13 = (f32[128,128]{1,0:T(8,128)S(1)}, f32[128,128]{1,0:T(8,128)S(1)}, u32[]{:S(2)}, u32[]{:S(2)}) collective-permute-start(f32[128,128]{1,0:T(8,128)S(1)} %get-tuple-element.39.g0), channel_id=1, source_target_pairs={{0,64},{4,20},{8,72},{12,28},{16,80},{20,4},{24,88},{28,12},{32,96... | collective-permute-start | bytes 196616 | tf_op jit(solution)/shard_map/ppermute | solution.py:51
  40.8 11.7 %collective-permute-start.24 = (f32[128,512]{1,0:T(8,128)S(1)}, f32[128,512]{1,0:T(8,128)S(1)}, u32[]{:S(2)}, u32[]{:S(2)}) collective-permute-start(f32[128,512]{1,0:T(8,128)S(1)} %pick.1.mine_ref), channel_id=1, source_target_pairs={{0,64},{4,20},{8,72},{16,80},{24,88},{36,52},{68,84},{100,116},{1,... | collective-permute-start | bytes 786440 | tf_op jit(solution)/shard_map/ppermute | solution.py:51
  44.2 8.5 %collective-permute-start.14 = (f32[128,128]{1,0:T(8,128)S(1)}, f32[128,128]{1,0:T(8,128)S(1)}, u32[]{:S(2)}, u32[]{:S(2)}) collective-permute-start(f32[128,128]{1,0:T(8,128)S(1)} %sum_gram.1.g_ref), channel_id=1, source_target_pairs={{0,4},{4,0},{8,12},{12,8},{16,20},{20,16},{24,28},{28,24},{32,36},... | collective-permute-start | bytes 196616 | tf_op jit(solution)/shard_map/ppermute | solution.py:55
  47.1 13.2 %collective-permute-start.23 = (f32[128,512]{1,0:T(8,128)S(1)}, f32[128,512]{1,0:T(8,128)S(1)}, u32[]{:S(2)}, u32[]{:S(2)}) collective-permute-start(f32[128,512]{1,0:T(8,128)S(1)} %pick.1.mine_ref), channel_id=1, source_target_pairs={{0,32},{4,12},{8,40},{16,48},{24,56},{36,44},{68,76},{100,108},{1,... | collective-permute-start | bytes 786440 | tf_op jit(solution)/shard_map/ppermute | solution.py:51
  49.1 11.2 %collective-permute-start.22 = (f32[128,512]{1,0:T(8,128)S(1)}, f32[128,512]{1,0:T(8,128)S(1)}, u32[]{:S(2)}, u32[]{:S(2)}) collective-permute-start(f32[128,512]{1,0:T(8,128)S(1)} %pick.1.mine_ref), channel_id=1, source_target_pairs={{0,96},{4,28},{8,104},{16,112},{24,120},{36,60},{68,92},{100,124},... | collective-permute-start | bytes 786440 | tf_op jit(solution)/shard_map/ppermute | solution.py:51
  52.4 7.9 %collective-permute-start.17 = (f32[128,512]{1,0:T(8,128)S(1)}, f32[128,512]{1,0:T(8,128)S(1)}, u32[]{:S(2)}, u32[]{:S(2)}) collective-permute-start(f32[128,512]{1,0:T(8,128)S(1)} %get-tuple-element.41.w0), channel_id=1, source_target_pairs={{0,64},{4,20},{8,72},{12,28},{16,80},{20,4},{24,88},{28,12},{32,96... | collective-permute-start | bytes 786440 | tf_op jit(solution)/shard_map/ppermute | solution.py:51
  52.6 7.8 %collective-permute-start.16 = (f32[128,512]{1,0:T(8,128)S(1)}, f32[128,512]{1,0:T(8,128)S(1)}, u32[]{:S(2)}, u32[]{:S(2)}) collective-permute-start(f32[128,512]{1,0:T(8,128)S(1)} %get-tuple-element.41.w0), channel_id=1, source_target_pairs={{0,32},{4,12},{8,40},{12,4},{16,48},{20,28},{24,56},{28,20},{32,0}... | collective-permute-start | bytes 786440 | tf_op jit(solution)/shard_map/ppermute | solution.py:51
  52.7 9.4 %collective-permute-start.15 = (f32[128,512]{1,0:T(8,128)S(1)}, f32[128,512]{1,0:T(8,128)S(1)}, u32[]{:S(2)}, u32[]{:S(2)}) collective-permute-start(f32[128,512]{1,0:T(8,128)S(1)} %get-tuple-element.41.w0), channel_id=1, source_target_pairs={{0,96},{4,28},{8,104},{12,20},{16,112},{20,12},{24,120},{28,4},{32... | collective-permute-start | bytes 786440 | tf_op jit(solution)/shard_map/ppermute | solution.py:51
  62.5 11.3 %collective-permute-start.27 = (f32[128,512]{1,0:T(8,128)S(1)}, f32[128,512]{1,0:T(8,128)S(1)}, u32[]{:S(2)}, u32[]{:S(2)}) collective-permute-start(f32[128,512]{1,0:T(8,128)S(1)} %piece.1.refs_0_), channel_id=1, source_target_pairs={{0,16},{4,68},{8,24},{12,76},{16,0},{20,84},{24,8},{28,92},{32,48}... | collective-permute-start | bytes 786440 | tf_op jit(solution)/shard_map/ppermute | solution.py:51
  62.8 11.0 %collective-permute-start.26 = (f32[128,512]{1,0:T(8,128)S(1)}, f32[128,512]{1,0:T(8,128)S(1)}, u32[]{:S(2)}, u32[]{:S(2)}) collective-permute-start(f32[128,512]{1,0:T(8,128)S(1)} %piece.1.refs_0_), channel_id=1, source_target_pairs={{0,8},{4,36},{8,0},{12,44},{16,24},{20,52},{24,16},{28,60},{32,40}... | collective-permute-start | bytes 786440 | tf_op jit(solution)/shard_map/ppermute | solution.py:51
  63.5 10.3 %collective-permute-start.25 = (f32[128,512]{1,0:T(8,128)S(1)}, f32[128,512]{1,0:T(8,128)S(1)}, u32[]{:S(2)}, u32[]{:S(2)}) collective-permute-start(f32[128,512]{1,0:T(8,128)S(1)} %piece.1.refs_0_), channel_id=1, source_target_pairs={{0,24},{4,100},{8,16},{12,108},{16,8},{20,116},{24,0},{28,124},{32... | collective-permute-start | bytes 786440 | tf_op jit(solution)/shard_map/ppermute | solution.py:51
  (8 other events, 29.4 us)
